TPU v7x, 1024 devices: a whole 4x4x32 slice. The times are simulated.
1024 devices in a mesh: gx: 32 (over z), gy: 8 (over y, core), gz: 4 (over x).
Axes of the slice: x: 4, y: 4, z: 32, core: 2. Of those that a mesh axis runs over, the one named last changes fastest.
Arguments:
- compliance: float32 [32, 8, 4, 768, 768], P('gx', 'gy', 'gz'), may hold values from -1 to 3, as said below
- rigid_modes: float32 [32, 8, 4, 6, 3, 2, 128], P('gx', 'gy', 'gz'), may hold values from -0.21875 to 0.21875
- coarse_inverse: float32 [6144, 6144], P(('gx', 'gy', 'gz')), may hold values from -1 to 1, as said below
- coarse_rhs: float32 [32, 8, 4, 6, 64], P('gx', 'gy', 'gz'), may hold values from -48 to 48
- dual_rhs: float32 [32, 8, 4, 3, 2, 64, 128], P('gx', 'gy', 'gz'), may hold values from -100 to 100, as said below
Outputs:
- multipliers: float32 [32, 8, 4, 3, 2, 64, 128], P('gx', 'gy', 'gz')
- final_residual: float32 [32, 8, 4, 3, 2, 64, 128], P('gx', 'gy', 'gz')
Inputs may be any that keep to these rules, and one draw needn't show every extreme that they name: Each subdomain's compliance block is symmetric positive definite. `coarse_inverse`: symmetric. `dual_rhs`: on every subdomain, the minus side of a direction holds the negated plus side of the previous subdomain in that direction, and zeros where there is none.
All inputs are finite; a program needn't handle non-finite values.
Results may differ from a plain program's by a relative error of at most 0.0023.
The roundings to bfloat16 on the way count: a program that leaves them out, or rounds other values in their place, can miss the bound.
Values may be sent and summed in bfloat16 or wider, within the bound.
No kernel may reach another device: no remote copies, remote signals or barrier semaphores. Data moves between devices by JAX's collectives and lax.ppermute only.
A program may use at most 32 MiB of HBM per device.

v0:
```python
import jax
import jax.numpy as jnp
from jax import lax
from jax.sharding import PartitionSpec as P

HIGHEST = lax.Precision.HIGHEST


def extended_2(x, sides, width):
    for axis, dim in sides:
        size, length = (lax.axis_size(axis), x.shape[dim])
        up = [(i, (i + 1) % size) for i in range(size - 1)]
        down = [(j, i) for i, j in up]
        last = lax.slice_in_dim(x, length - width, length, axis=dim)
        leading = lax.slice_in_dim(x, 0, width, axis=dim)
        before = lax.ppermute(last, axis, up)
        after = lax.ppermute(leading, axis, down)
        x = jnp.concatenate([before, x, after], axis=dim)
    return x


def side_pair(extended, inside):
    new_minus = jnp.where(inside, extended[1] - extended[0], jnp.zeros_like(extended[1]))
    new_plus = extended[2] - extended[3]
    return jnp.stack([new_minus, new_plus])


def assemble(values):
    along_x = extended_2(values[0], (("gx", 0),), 1)
    along_y = extended_2(values[1], (("gy", 0),), 1)
    along_z = extended_2(values[2], (("gz", 0),), 1)
    return jnp.stack(
        [
            side_pair(along_x, lax.axis_index("gx") > 0),
            side_pair(along_y, lax.axis_index("gy") > 0),
            side_pair(along_z, lax.axis_index("gz") > 0),
        ]
    )


def inner_block(first_field, second_field):
    return jnp.einsum("ind,imd->nm", first_field[:, 1], second_field[:, 1], precision=HIGHEST)


def gram_solve(matrix, target):
    factor = jnp.linalg.cholesky(matrix)
    middle = lax.linalg.triangular_solve(factor, target, left_side=True, lower=True)
    return lax.linalg.triangular_solve(factor, middle, left_side=True, lower=True, transpose_a=True)


def combine(values, coeffs):
    return jnp.einsum("ijnd,nm->ijmd", values, coeffs, precision=HIGHEST)


def global_sum(partials):
    return lax.psum(partials, ("gx", "gy", "gz"))


def body(compliance, rigid_modes, coarse_inverse, coarse_rhs, dual_rhs):
    face_dofs = dual_rhs.shape[-1]
    matrix = compliance[0, 0, 0].reshape(3, 2, face_dofs, 3, 2, face_dofs)
    mode_traces = rigid_modes[0, 0, 0]
    right_local = dual_rhs[0, 0, 0]

    def comply(values):
        return jnp.einsum("ijdklm,klnm->ijnd", matrix, values, precision=HIGHEST)

    def add_rows(arrived):
        return jnp.dot(coarse_inverse, arrived.astype(jnp.float32), precision=HIGHEST)

    def coarse(right_side):
        outgoing = right_side.astype(jnp.bfloat16)
        weights = add_rows(lax.all_gather(outgoing, ("gx", "gy", "gz"), axis=0, tiled=True))
        correction = jnp.einsum("mijd,mn->ijnd", mode_traces, weights, precision=HIGHEST)
        return assemble(correction)

    multipliers = coarse(coarse_rhs[0, 0, 0])
    residual = right_local - assemble(comply(multipliers))
    right_side = jnp.einsum("mijd,ijnd->mn", mode_traces, residual, precision=HIGHEST)
    projected = residual - coarse(right_side)
    applied = assemble(comply(projected))
    curvature, alignment = global_sum(
        (inner_block(projected, applied), inner_block(projected, projected))
    )
    step_size = gram_solve(curvature, alignment)
    multipliers = multipliers + combine(projected, step_size)
    final_residual = right_local - assemble(comply(multipliers))
    return (multipliers[None, None, None], final_residual[None, None, None])


def solution(mesh):
    placed = (
        P("gx", "gy", "gz", None, None),
        P("gx", "gy", "gz", None, None, None, None),
        P(("gx", "gy", "gz"), None),
        P("gx", "gy", "gz", None, None),
        P("gx", "gy", "gz", None, None, None, None),
    )
    return jax.shard_map(
        body,
        mesh=mesh,
        in_specs=placed,
        out_specs=(
            P("gx", "gy", "gz", None, None, None, None),
            P("gx", "gy", "gz", None, None, None, None),
        ),
        check_vma=False,
    )
```

profile of v0, /device:TPU:1, one launch (start us, length us, event | category | flops | bytes accessed | tf_op | source)
XLA Modules:
  0.0 893.0 jit_solution(7550947676065616147)
XLA Ops:
  1.4 308.4 %all-gather = bf16[1,1,1,6144,64]{4,2,1,0,3:T(2,128)(2,1)S(1)} all-gather(bf16[1,1,1,6,64]{4,2,1,0,3:T(2,128)(2,1)S(1)} %bitcast_convert_fusion), channel_id=2, replica_groups=mesh['gx'=32,'gy'=8,'gz'=4] {'gx','gy','gz'}, dimensions={3}, use_global_device_ids=true | all-gather | bytes 787200 | tf_op jit(solution)/shard_map/all_gather | solution.py:73
  309.8 4.9 copy.25
  318.7 2.6 collective-permute-start.4
  322.7 16.2 %collective-permute-start.2 = (f32[1,64,128]{2,1,0:T(8,128)S(1)}, f32[1,64,128]{2,1,0:T(8,128)S(1)}, u32[]{:S(2)}, u32[]{:S(2)}) collective-permute-start(f32[1,64,128]{2,1,0:T(8,128)S(1)} %get-tuple-element.61), channel_id=1, source_target_pairs={{0,4},{4,8},{8,12},{12,16},{16,20},{20,24},{24,28},{1,5},{5,9},{9,... | collective-permute-start | bytes 98312 | tf_op jit(solution)/shard_map/ppermute | solution.py:16
  338.8 1.9 collective-permute-start.3
  342.1 2.9 reshape_squeeze.3
  345.5 2.4 fusion.6
  347.9 3.6 collective-permute-start.6
  351.5 4.3 collective-permute-start.10
  357.1 4.5 collective-permute-start.8
  361.5 1.9 collective-permute-start.9
  364.8 2.0 collective-permute-done.9
  368.5 277.2 %all-gather.1 = bf16[1024,6,64]{2,1,0:T(8,128)(2,1)} all-gather(bf16[1,6,64]{2,1,0:T(8,128)(2,1)S(1)} %fusion.17), channel_id=1, replica_groups=mesh['gx'=32,'gy'=8,'gz'=4] {'gx','gy','gz'}, dimensions={0}, use_global_device_ids=true | all-gather | bytes 787200 | tf_op jit(solution)/shard_map/all_gather | solution.py:73
  645.6 3.9 reshape.127
  649.5 2.1 convolution_bitcast_fusion.6
  653.5 2.6 collective-permute-start.16
  657.4 17.0 %collective-permute-start.14 = (f32[1,64,128]{2,1,0:T(8,128)S(1)}, f32[1,64,128]{2,1,0:T(8,128)S(1)}, u32[]{:S(2)}, u32[]{:S(2)}) collective-permute-start(f32[1,64,128]{2,1,0:T(8,128)S(1)} %get-tuple-element.37), channel_id=1, source_target_pairs={{0,4},{4,8},{8,12},{12,16},{16,20},{20,24},{24,28},{1,5},{5,9},{9,... | collective-permute-start | bytes 98312 | tf_op jit(solution)/shard_map/ppermute | solution.py:16
  674.4 2.2 collective-permute-start.15
  679.7 2.0 collective-permute-done.13
  681.8 2.4 fusion.9
  684.1 2.3 collective-permute-start.18
  686.5 4.3 collective-permute-start.22
  692.1 4.2 collective-permute-start.20
  696.3 1.9 collective-permute-start.21
  703.2 159.4 %all-reduce = (f32[64,64]{1,0:T(8,128)S(1)}, f32[64,64]{0,1:T(8,128)S(1)}) all-reduce(f32[64,64]{1,0:T(8,128)S(1)} %convolution_bitcast_fusion.4, f32[64,64]{0,1:T(8,128)S(1)} %convolution_bitcast_fusion.5), channel_id=1, replica_groups=mesh['gx'=32,'gy'=8,'gz'=4] {'gx','gy','gz'}, use_global_device_ids=true, to_apply=%region_3.4 | all-reduce | flops 8192 | bytes 65536 | tf_op jit(solution)/shard_map/psum | solution.py:56
  862.7 5.8 cholesky.16
  869.9 4.9 custom-call.8
  875.6 2.4 fusion.12
  879.3 2.2 collective-permute-start.28
  882.8 2.5 collective-permute-start.26
  885.3 1.9 collective-permute-start.27
  888.6 1.9 collective-permute-done.27
  (89 shorter events, 33.0 us)
Async XLA Ops:
  0.6 314.1 %copy-start = (f32[6,6144]{1,0:T(8,128)S(1)}, f32[6,6144]{1,0:T(8,128)}, u32[]{:S(2)}) copy-start(f32[6,6144]{1,0:T(8,128)} %param.7) | copy-start | bytes 442372
  317.0 23.8 %collective-permute-start = (f32[1,64,128]{2,1,0:T(8,128)S(1)}, f32[1,64,128]{2,1,0:T(8,128)S(1)}, u32[]{:S(2)}, u32[]{:S(2)}) collective-permute-start(f32[1,64,128]{2,1,0:T(8,128)S(1)} %get-tuple-element.58), channel_id=1, source_target_pairs={{0,32},{32,64},{64,96},{96,128},{128,160},{160,192},{192,224},{224... | collective-permute-start | bytes 98312 | tf_op jit(solution)/shard_map/ppermute | solution.py:16
  318.7 26.2 %collective-permute-start.4 = (f32[1,64,128]{2,1,0:T(8,128)S(1)}, f32[1,64,128]{2,1,0:T(8,128)S(1)}, u32[]{:S(2)}, u32[]{:S(2)}) collective-permute-start(f32[1,64,128]{2,1,0:T(8,128)S(1)} %get-tuple-element.59), channel_id=1, source_target_pairs={{0,1},{1,2},{2,3},{4,5},{5,6},{6,7},{8,9},{9,10},{10,11},{12,13},{... | collective-permute-start | bytes 98312 | tf_op jit(solution)/shard_map/ppermute | solution.py:16
  321.4 23.6 %collective-permute-start.5 = (f32[1,64,128]{2,1,0:T(8,128)S(1)}, f32[1,64,128]{2,1,0:T(8,128)S(1)}, u32[]{:S(2)}, u32[]{:S(2)}) collective-permute-start(f32[1,64,128]{2,1,0:T(8,128)S(1)} %get-tuple-element.60), channel_id=1, source_target_pairs={{1,0},{2,1},{3,2},{5,4},{6,5},{7,6},{9,8},{10,9},{11,10},{13,12},{... | collective-permute-start | bytes 98312 | tf_op jit(solution)/shard_map/ppermute | solution.py:17
  322.7 22.3 %collective-permute-start.2 = (f32[1,64,128]{2,1,0:T(8,128)S(1)}, f32[1,64,128]{2,1,0:T(8,128)S(1)}, u32[]{:S(2)}, u32[]{:S(2)}) collective-permute-start(f32[1,64,128]{2,1,0:T(8,128)S(1)} %get-tuple-element.61), channel_id=1, source_target_pairs={{0,4},{4,8},{8,12},{12,16},{16,20},{20,24},{24,28},{1,5},{5,9},{9,... | collective-permute-start | bytes 98312 | tf_op jit(solution)/shard_map/ppermute | solution.py:16
  338.8 6.2 collective-permute-start.3
  340.8 4.7 collective-permute-start.1
  345.5 22.8 %copy-start.1 = (f32[1,1,1,3,2,64,128]{6,5,4,3,2,1,0:T(8,128)S(1)}, f32[1,1,1,3,2,64,128]{6,5,4,3,2,1,0:T(8,128)}, u32[]{:S(2)}) copy-start(f32[1,1,1,3,2,64,128]{6,5,4,3,2,1,0:T(8,128)} %param.9) | copy-start | bytes 589828
  347.9 15.6 %collective-permute-start.6 = (f32[1,64,128]{2,1,0:T(8,128)S(1)}, f32[1,64,128]{2,1,0:T(8,128)S(1)}, u32[]{:S(2)}, u32[]{:S(2)}) collective-permute-start(f32[1,64,128]{2,1,0:T(8,128)S(1)} %get-tuple-element.46), channel_id=1, source_target_pairs={{0,32},{32,64},{64,96},{96,128},{128,160},{160,192},{192,224},{224... | collective-permute-start | bytes 98312 | tf_op jit(solution)/shard_map/ppermute | solution.py:16
  351.5 13.3 %collective-permute-start.10 = (f32[1,64,128]{2,1,0:T(8,128)S(1)}, f32[1,64,128]{2,1,0:T(8,128)S(1)}, u32[]{:S(2)}, u32[]{:S(2)}) collective-permute-start(f32[1,64,128]{2,1,0:T(8,128)S(1)} %get-tuple-element.47), channel_id=1, source_target_pairs={{0,1},{1,2},{2,3},{4,5},{5,6},{6,7},{8,9},{9,10},{10,11},{12,13},{... | collective-permute-start | bytes 98312 | tf_op jit(solution)/shard_map/ppermute | solution.py:16
  355.8 9.0 %collective-permute-start.11 = (f32[1,64,128]{2,1,0:T(8,128)S(1)}, f32[1,64,128]{2,1,0:T(8,128)S(1)}, u32[]{:S(2)}, u32[]{:S(2)}) collective-permute-start(f32[1,64,128]{2,1,0:T(8,128)S(1)} %get-tuple-element.48), channel_id=1, source_target_pairs={{1,0},{2,1},{3,2},{5,4},{6,5},{7,6},{9,8},{10,9},{11,10},{13,12},{... | collective-permute-start | bytes 98312 | tf_op jit(solution)/shard_map/ppermute | solution.py:17
  357.1 7.8 collective-permute-start.8
  361.5 5.2 collective-permute-start.9
  363.5 4.7 collective-permute-start.7
  652.1 24.6 %collective-permute-start.12 = (f32[1,64,128]{2,1,0:T(8,128)S(1)}, f32[1,64,128]{2,1,0:T(8,128)S(1)}, u32[]{:S(2)}, u32[]{:S(2)}) collective-permute-start(f32[1,64,128]{2,1,0:T(8,128)S(1)} %get-tuple-element.34), channel_id=1, source_target_pairs={{0,32},{32,64},{64,96},{96,128},{128,160},{160,192},{192,224},{224... | collective-permute-start | bytes 98312 | tf_op jit(solution)/shard_map/ppermute | solution.py:16
  653.5 24.5 %collective-permute-start.16 = (f32[1,64,128]{2,1,0:T(8,128)S(1)}, f32[1,64,128]{2,1,0:T(8,128)S(1)}, u32[]{:S(2)}, u32[]{:S(2)}) collective-permute-start(f32[1,64,128]{2,1,0:T(8,128)S(1)} %get-tuple-element.35), channel_id=1, source_target_pairs={{0,1},{1,2},{2,3},{4,5},{5,6},{6,7},{8,9},{9,10},{10,11},{12,13},{... | collective-permute-start | bytes 98312 | tf_op jit(solution)/shard_map/ppermute | solution.py:16
  656.1 21.9 %collective-permute-start.17 = (f32[1,64,128]{2,1,0:T(8,128)S(1)}, f32[1,64,128]{2,1,0:T(8,128)S(1)}, u32[]{:S(2)}, u32[]{:S(2)}) collective-permute-start(f32[1,64,128]{2,1,0:T(8,128)S(1)} %get-tuple-element.36), channel_id=1, source_target_pairs={{1,0},{2,1},{3,2},{5,4},{6,5},{7,6},{9,8},{10,9},{11,10},{13,12},{... | collective-permute-start | bytes 98312 | tf_op jit(solution)/shard_map/ppermute | solution.py:17
  657.4 20.6 %collective-permute-start.14 = (f32[1,64,128]{2,1,0:T(8,128)S(1)}, f32[1,64,128]{2,1,0:T(8,128)S(1)}, u32[]{:S(2)}, u32[]{:S(2)}) collective-permute-start(f32[1,64,128]{2,1,0:T(8,128)S(1)} %get-tuple-element.37), channel_id=1, source_target_pairs={{0,4},{4,8},{8,12},{12,16},{16,20},{20,24},{24,28},{1,5},{5,9},{9,... | collective-permute-start | bytes 98312 | tf_op jit(solution)/shard_map/ppermute | solution.py:16
  674.4 5.2 collective-permute-start.15
  676.7 5.0 collective-permute-start.13
  684.1 14.1 %collective-permute-start.18 = (f32[1,64,128]{2,1,0:T(8,128)S(1)}, f32[1,64,128]{2,1,0:T(8,128)S(1)}, u32[]{:S(2)}, u32[]{:S(2)}) collective-permute-start(f32[1,64,128]{2,1,0:T(8,128)S(1)} %get-tuple-element.22), channel_id=1, source_target_pairs={{0,32},{32,64},{64,96},{96,128},{128,160},{160,192},{192,224},{224... | collective-permute-start | bytes 98312 | tf_op jit(solution)/shard_map/ppermute | solution.py:16
  686.5 13.3 %collective-permute-start.22 = (f32[1,64,128]{2,1,0:T(8,128)S(1)}, f32[1,64,128]{2,1,0:T(8,128)S(1)}, u32[]{:S(2)}, u32[]{:S(2)}) collective-permute-start(f32[1,64,128]{2,1,0:T(8,128)S(1)} %get-tuple-element.23), channel_id=1, source_target_pairs={{0,1},{1,2},{2,3},{4,5},{5,6},{6,7},{8,9},{9,10},{10,11},{12,13},{... | collective-permute-start | bytes 98312 | tf_op jit(solution)/shard_map/ppermute | solution.py:16
  690.8 9.1 %collective-permute-start.23 = (f32[1,64,128]{2,1,0:T(8,128)S(1)}, f32[1,64,128]{2,1,0:T(8,128)S(1)}, u32[]{:S(2)}, u32[]{:S(2)}) collective-permute-start(f32[1,64,128]{2,1,0:T(8,128)S(1)} %get-tuple-element.24), channel_id=1, source_target_pairs={{1,0},{2,1},{3,2},{5,4},{6,5},{7,6},{9,8},{10,9},{11,10},{13,12},{... | collective-permute-start | bytes 98312 | tf_op jit(solution)/shard_map/ppermute | solution.py:17
  692.1 7.8 collective-permute-start.20
  696.3 5.2 collective-permute-start.21
  698.2 4.7 collective-permute-start.19
  878.0 9.2 %collective-permute-start.24 = (f32[1,64,128]{2,1,0:T(8,128)S(1)}, f32[1,64,128]{2,1,0:T(8,128)S(1)}, u32[]{:S(2)}, u32[]{:S(2)}) collective-permute-start(f32[1,64,128]{2,1,0:T(8,128)S(1)} %get-tuple-element.10), channel_id=1, source_target_pairs={{0,32},{32,64},{64,96},{96,128},{128,160},{160,192},{192,224},{224... | collective-permute-start | bytes 98312 | tf_op jit(solution)/shard_map/ppermute | solution.py:16
  879.3 9.3 %collective-permute-start.28 = (f32[1,64,128]{2,1,0:T(8,128)S(1)}, f32[1,64,128]{2,1,0:T(8,128)S(1)}, u32[]{:S(2)}, u32[]{:S(2)}) collective-permute-start(f32[1,64,128]{2,1,0:T(8,128)S(1)} %get-tuple-element.11), channel_id=1, source_target_pairs={{0,1},{1,2},{2,3},{4,5},{5,6},{6,7},{8,9},{9,10},{10,11},{12,13},{... | collective-permute-start | bytes 98312 | tf_op jit(solution)/shard_map/ppermute | solution.py:16
  881.5 7.1 collective-permute-start.29
  882.8 5.8 collective-permute-start.26
  885.3 5.2 collective-permute-start.27
  887.3 5.0 collective-permute-start.25
  (2 other events, 24.2 us)
where the time goes:
time: 896 us; the launch traced here: 893 us
  blocking collectives  745 us (83%)
  starting transfers between devices  93.5 us (10%)
  waiting for transfers between devices  14.2 us (2%)
  other arithmetic  13.8 us (2%)
  matrix products  13.3 us (1%)
  local copies, waits for them, and re-layouts  11.9 us (1%)
    all_gather x2, blocking collectives, coarse(): lax.all_gather(outgoing, ('gx', 'gy', 'gz'), axis=0, tiled=True)  586 us
    psum x1, blocking collectives, global_sum(): return lax.psum(partials, ('gx', 'gy', 'gz'))  159 us
    ppermute x15, starting transfers between devices, extended_2(): before = lax.ppermute(last, axis, up)  70.7 us
    ppermute x15, starting transfers between devices, extended_2(): after = lax.ppermute(leading, axis, down)  22.9 us
  transfers between devices with their start and end apart: 30, of which 9 were waited for; matrix products, arithmetic and copies ran while one was open for 0% of the time, Pallas kernels for 0%

commit v1 on v0

v1 whole, which is shorter than its diff:
```python
import jax
import jax.numpy as jnp
from jax import lax
from jax.sharding import PartitionSpec as P

HIGHEST = lax.Precision.HIGHEST
AXES = ("gx", "gy", "gz")
PLANE = ("gy", "gz")
bf16 = jnp.bfloat16


def to_all(block, axis):
    return lax.all_to_all(
        jnp.broadcast_to(block[None], (lax.axis_size(axis),) + block.shape), axis, 0, 0, tiled=True
    )


def neighbours(to_lower, to_upper):
    arrived = []
    for d, axis in enumerate(AXES):
        size = lax.axis_size(axis)
        up = [(i, i + 1) for i in range(size - 1)]
        down = [(j, i) for i, j in up]
        arrived.append(lax.ppermute(to_upper[d], axis, up))
        arrived.append(lax.ppermute(to_lower[d], axis, down))
    return arrived


def gram_solve(matrix, target):
    factor = jnp.linalg.cholesky(matrix)
    middle = lax.linalg.triangular_solve(factor, target, left_side=True, lower=True)
    return lax.linalg.triangular_solve(factor, middle, left_side=True, lower=True, transpose_a=True)


def body(compliance, rigid_modes, coarse_inverse, coarse_rhs, dual_rhs):
    face, loads = dual_rhs.shape[-1], dual_rhs.shape[-2]
    modes = rigid_modes.shape[3]
    long, plane = lax.axis_size("gx"), lax.axis_size(PLANE)
    parts = long * plane
    order = 6 * face
    matrix = compliance[0, 0, 0]
    traces = rigid_modes[0, 0, 0].reshape(modes, 6, face)
    gaps = dual_rhs[0, 0, 0].reshape(6, loads, face)
    inside = jnp.stack(
        [flag for axis in AXES for flag in (lax.axis_index(axis) > 0, jnp.bool_(True))]
    )[:, None, None]

    def gather(right_side):
        flat = right_side.astype(bf16).reshape(1, modes * loads)
        column = to_all(flat, "gx").reshape(long, modes * loads)
        return to_all(column, PLANE).reshape(parts, modes * loads)

    start = gather(coarse_rhs[0, 0, 0])

    rows = coarse_inverse.reshape(modes, long, plane, modes).transpose(0, 3, 2, 1)
    rows = rows.reshape(modes, modes * parts)
    packed = [
        jnp.concatenate([rows, traces[:, f]], axis=1) for f in range(6)
    ]
    arrived = neighbours(packed[0::2], packed[1::2])
    all_rows = jnp.concatenate([rows] + [a[:, : modes * parts] for a in arrived], axis=0)
    all_rows = all_rows.reshape(7 * modes, modes // 2, 2, parts).transpose(1, 2, 0, 3)
    all_rows = all_rows.reshape(modes // 2, 14 * modes, parts)
    high = lax.reduce_precision(all_rows, 8, 7)
    rest = all_rows - high
    middle = lax.reduce_precision(rest, 8, 7)
    pieces = jnp.concatenate([high, middle, rest - middle], axis=1).astype(bf16)
    spread = jnp.stack(
        [
            jnp.concatenate([traces[:, f], -arrived[f][:, modes * parts :]], axis=0)
            for f in range(6)
        ]
    )
    spread = jnp.where(inside, spread, 0.0)

    def coarse(stacked):
        total = 0.0
        for q in range(modes // 2):
            columns = stacked[:, 2 * loads * q : 2 * loads * (q + 1)]
            total = total + jnp.dot(pieces[q], columns, preferred_element_type=jnp.float32)
        total = total.reshape(3, 2, 7, modes, 2 * loads)
        total = total[0] + (total[1] + total[2])
        weights = total[0, :, :, :loads] + total[1, :, :, loads:]
        both = jnp.concatenate(
            [jnp.broadcast_to(weights[:1], (6, modes, loads)), weights[1:]], axis=1
        )
        return jnp.einsum("fkn,fkd->fnd", both, spread, precision=HIGHEST)

    def comply(values):
        wide = jnp.concatenate([values[f] for f in range(6)], axis=1)
        return jnp.dot(wide, matrix, precision=HIGHEST)

    def assemble(wide):
        values = [wide[:, face * f : face * (f + 1)] for f in range(6)]
        across = neighbours(values[0::2], values[1::2])
        return jnp.where(inside, jnp.stack([v - a for v, a in zip(values, across)]), 0.0)

    multipliers = coarse(start)
    residual = gaps - assemble(comply(multipliers))
    right_side = jnp.einsum("mfd,fnd->mn", traces, residual, precision=HIGHEST)
    projected = residual - coarse(gather(right_side))
    image = comply(projected)

    curvature = sum(
        jnp.dot(projected[f], image[:, face * f : face * (f + 1)].T, precision=HIGHEST)
        for f in range(6)
    )
    plus = projected[1::2]
    alignment = jnp.einsum("ind,imd->nm", plus, plus, precision=HIGHEST)
    grams = jnp.concatenate([curvature, alignment], axis=1)
    grams = lax.all_to_all(
        grams.reshape(plane, loads // plane, 2 * loads), PLANE, 0, 0, tiled=True
    ).sum(0)
    grams = to_all(grams, "gx").sum(0)
    grams = to_all(grams, PLANE).reshape(loads, 2 * loads)

    applied = assemble(image)
    step_size = gram_solve(grams[:, :loads], grams[:, loads:])
    multipliers = multipliers + jnp.einsum(
        "fnd,nm->fmd", projected, step_size, precision=HIGHEST
    )
    final_residual = residual - jnp.einsum("fnd,nm->fmd", applied, step_size, precision=HIGHEST)
    shape = (1, 1, 1, 3, 2, loads, face)
    return multipliers.reshape(shape), final_residual.reshape(shape)


def solution(mesh):
    placed = (
        P("gx", "gy", "gz", None, None),
        P("gx", "gy", "gz", None, None, None, None),
        P(AXES, None),
        P("gx", "gy", "gz", None, None),
        P("gx", "gy", "gz", None, None, None, None),
    )
    return jax.shard_map(
        body,
        mesh=mesh,
        in_specs=placed,
        out_specs=(
            P("gx", "gy", "gz", None, None, None, None),
            P("gx", "gy", "gz", None, None, None, None),
        ),
        check_vma=False,
    )
```

time: 896 us -> 300 us (0.33)
  blocking collectives: 745 us -> 68.3 us
  local copies, waits for them, and re-layouts: 11.9 us -> 44.3 us
  waiting for transfers between devices: 14.2 us -> 38.9 us
  other arithmetic: 13.8 us -> 31.3 us
    all_gather x2 -> x0, blocking collectives: 586 us -> none  [coarse(): lax.all_gather(outgoing, ('gx', 'gy', 'gz'), axis=0, tiled=True)]
    psum x1 -> x0, blocking collectives: 159 us -> none  [global_sum(): return lax.psum(partials, ('gx', 'gy', 'gz'))]
    all_to_all x0 -> x2, blocking collectives: none -> 68.3 us  [to_all(): lax.all_to_all(jnp.broadcast_to(block[None], (lax.axis_size(axis),) + blo...]
    all_to_all x0 -> x5, starting transfers between devices: none -> 49.2 us  [the longest x4 44.2 us: to_all(): lax.all_to_all(jnp.broadcast_to(block[None], (lax.axis_size(axis),) + blo...]
    ppermute x30 -> x18, starting transfers between devices: 93.5 us -> 51.2 us  [the longest x9 28.7 us: neighbours(): arrived.append(lax.ppermute(to_upper[d], axis, up))]
    all_to_all x0 -> x5, waiting for transfers between devices: none -> 35.2 us  [the longest x4 35.2 us: to_all(): lax.all_to_all(jnp.broadcast_to(block[None], (lax.axis_size(axis),) + blo...]
    ppermute x30 -> x18, waiting for transfers between devices: 14.2 us -> 3.68 us  [the longest x9 3.66 us: neighbours(): arrived.append(lax.ppermute(to_lower[d], axis, down))]
    concatenate x0 -> x10, local copies, waits for them, and re-layouts: none -> 9.97 us  [the longest x8 9.96 us: body(): jnp.concatenate([rows] + [a[:, :modes * parts] for a in arrived], axis=0)]
  transfers between devices with their start and end apart: 30 -> 23, of which waited for: 9 -> 5; matrix products, arithmetic and copies ran while one was open for 0% -> 16% of each run, Pallas kernels for 0% -> 0%
where the time goes in v1:
time: 300 us; the launch traced here: 298 us
  starting transfers between devices  100 us (33%)
  blocking collectives  68.3 us (23%)
  local copies, waits for them, and re-layouts  44.3 us (15%)
  waiting for transfers between devices  38.9 us (13%)
  other arithmetic  31.3 us (10%)
  matrix products  13.3 us (4%)
    all_to_all x2, blocking collectives, to_all(): lax.all_to_all(jnp.broadcast_to(block[None], (lax.axis_size(axis),) + blo...  68.3 us
    all_to_all x4, starting transfers between devices, to_all(): lax.all_to_all(jnp.broadcast_to(block[None], (lax.axis_size(axis),) + blo...  44.2 us
    all_to_all x4, waiting for transfers between devices, to_all(): lax.all_to_all(jnp.broadcast_to(block[None], (lax.axis_size(axis),) + blo...  35.2 us
    ppermute x9, starting transfers between devices, neighbours(): arrived.append(lax.ppermute(to_upper[d], axis, up))  28.7 us
    ppermute x9, starting transfers between devices, neighbours(): arrived.append(lax.ppermute(to_lower[d], axis, down))  22.5 us
    concatenate x8, local copies, waits for them, and re-layouts, body(): jnp.concatenate([rows] + [a[:, :modes * parts] for a in arrived], axis=0)  9.96 us
    slice x6, local copies, waits for them, and re-layouts, body(): a[:, :modes * parts]  9.7 us
    unnamed x52, local copies, waits for them, and re-layouts  8.85 us
  transfers between devices with their start and end apart: 23, of which 5 were waited for; matrix products, arithmetic and copies ran while one was open for 16% of the time, Pallas kernels for 0%

profile of v1, /device:TPU:1, one launch (start us, length us, event | category | flops | bytes accessed | tf_op | source)
XLA Modules:
  0.0 298.0 jit_solution(396918082127780982)
XLA Ops:
  2.1 5.8 %reshape.93 = f32[6,32,32,6]{3,2,1,0:T(8,128)} reshape(f32[6,6144]{1,0:T(8,128)} %param.7) | data formatting | bytes 294912 | tf_op jit(solution)/shard_map/reshape | solution.py:55
  8.0 3.2 %copy.55 = f32[6,6,32,32]{3,2,1,0:T(8,128)S(1)} copy(f32[6,6,32,32]{1,2,3,0:T(8,128)} %bitcast.204) | data formatting | bytes 294912 | tf_op jit(solution)/shard_map/transpose | solution.py:55
  12.6 5.0 %collective-permute-start = (f32[6,6272]{1,0:T(8,128)}, f32[6,6272]{1,0:T(8,128)}, u32[]{:S(2)}, u32[]{:S(2)}) collective-permute-start(f32[6,6272]{1,0:T(8,128)} %get-tuple-element.22), channel_id=1, source_target_pairs={{0,32},{32,64},{64,96},{96,128},{128,160},{160,192},{192,224},{224... | collective-permute-start | bytes 451592 | tf_op jit(solution)/shard_map/ppermute | solution.py:24
  18.9 4.0 %collective-permute-start.2 = (f32[6,6272]{1,0:T(8,128)}, f32[6,6272]{1,0:T(8,128)}, u32[]{:S(2)}, u32[]{:S(2)}) collective-permute-start(f32[6,6272]{1,0:T(8,128)} %get-tuple-element.19), channel_id=1, source_target_pairs={{0,4},{4,8},{8,12},{12,16},{16,20},{20,24},{24,28},{1,5},{5,9},{9,... | collective-permute-start | bytes 451592 | tf_op jit(solution)/shard_map/ppermute | solution.py:24
  22.9 10.9 %collective-permute-start.3 = (f32[6,6272]{1,0:T(8,128)}, f32[6,6272]{1,0:T(8,128)}, u32[]{:S(2)}, u32[]{:S(2)}) collective-permute-start(f32[6,6272]{1,0:T(8,128)} %get-tuple-element.20), channel_id=1, source_target_pairs={{4,0},{8,4},{12,8},{16,12},{20,16},{24,20},{28,24},{5,1},{9,5},{13... | collective-permute-start | bytes 451592 | tf_op jit(solution)/shard_map/ppermute | solution.py:25
  33.8 2.0 collective-permute-start.4
  38.0 22.7 %all-to-all-start = ((bf16[32,2,192]{2,1,0:T(2,128)(2,1)}), bf16[32,2,192]{2,1,0:T(2,128)(2,1)}, u32[]{:S(2)}, u32[]{:S(2)}) async-start(bf16[32,2,192]{2,1,0:T(2,128)(2,1)} %reshape.107), calls=%async_computation | async-start | bytes 65536 | tf_op jit(solution)/shard_map/all_to_all | solution.py:13
  67.0 1.6 slice.324
  68.6 1.7 concatenate.77
  71.9 1.7 concatenate.79
  75.3 1.7 concatenate.81
  78.6 1.7 concatenate.83
  83.2 1.7 concatenate.85
  100.2 9.1 %all-to-all-start.1 = ((bf16[32,32,384]{2,1,0:T(8,128)(2,1)}), bf16[32,32,384]{2,1,0:T(8,128)(2,1)}, u32[]{:S(2)}, u32[]{:S(2)}) async-start(bf16[32,32,384]{2,1,0:T(8,128)(2,1)} %broadcast_in_dim.85), calls=%async_computation.1 | async-start | bytes 1572864 | tf_op jit(solution)/shard_map/all_to_all | solution.py:13
  111.8 11.3 %all-to-all-done.1 = bf16[32,32,384]{2,1,0:T(8,128)(2,1)} async-done(((bf16[32,32,384]{2,1,0:T(8,128)(2,1)}), bf16[32,32,384]{2,1,0:T(8,128)(2,1)}, u32[]{:S(2)}, u32[]{:S(2)}) %all-to-all-start.1) | async-done | bytes 786464 | tf_op jit(solution)/shard_map/all_to_all | solution.py:13
  129.7 3.3 %collective-permute-start.6 = (f32[64,128]{1,0:T(8,128)S(1)}, f32[64,128]{1,0:T(8,128)S(1)}, u32[]{:S(2)}, u32[]{:S(2)}) collective-permute-start(f32[64,128]{1,0:T(8,128)S(1)} %get-tuple-element.15), channel_id=1, source_target_pairs={{0,32},{32,64},{64,96},{96,128},{128,160},{160,192},{192,224},{224... | collective-permute-start | bytes 98312 | tf_op jit(solution)/shard_map/ppermute | solution.py:24
  134.4 3.6 %collective-permute-start.8 = (f32[64,128]{1,0:T(8,128)S(1)}, f32[64,128]{1,0:T(8,128)S(1)}, u32[]{:S(2)}, u32[]{:S(2)}) collective-permute-start(f32[64,128]{1,0:T(8,128)S(1)} %get-tuple-element.13), channel_id=1, source_target_pairs={{0,4},{4,8},{8,12},{12,16},{16,20},{20,24},{24,28},{1,5},{5,9},{9,... | collective-permute-start | bytes 98312 | tf_op jit(solution)/shard_map/ppermute | solution.py:24
  138.0 1.9 collective-permute-start.9
  143.3 3.0 %collective-permute-done.11 = f32[64,128]{1,0:T(8,128)S(1)} collective-permute-done((f32[64,128]{1,0:T(8,128)S(1)}, f32[64,128]{1,0:T(8,128)S(1)}, u32[]{:S(2)}, u32[]{:S(2)}) %collective-permute-start.11) | collective-permute-done | bytes 32800 | tf_op jit(solution)/shard_map/ppermute | solution.py:25
  147.7 44.9 %all_to_all.35 = bf16[32,2,192]{2,1,0:T(2,128)(2,1)S(1)} all-to-all(bf16[32,2,192]{2,1,0:T(2,128)(2,1)S(1)} %reshape.109), channel_id=1, replica_groups=mesh['gx'=32,'gy'=8,'gz'=4] {'gx'}, dimensions={0} | all-to-all | bytes 49152 | tf_op jit(solution)/shard_map/all_to_all | solution.py:13
  192.8 23.4 %all_to_all.36 = bf16[32,32,384]{2,1,0:T(8,128)(2,1)S(1)} all-to-all(bf16[32,32,384]{2,1,0:T(8,128)(2,1)S(1)} %broadcast_in_dim.95), channel_id=1, replica_groups=mesh['gx'=32,'gy'=8,'gz'=4] {'gy','gz'}, dimensions={0} | all-to-all | bytes 1572864 | tf_op jit(solution)/shard_map/all_to_all | solution.py:13
  219.9 2.2 collective-permute-start.12
  223.7 5.0 %all-to-all-start.4 = ((f32[32,2,128]{2,1,0:T(2,128)}), f32[32,2,128]{2,1,0:T(2,128)S(1)}, u32[]{:S(2)}, u32[]{:S(2)}) async-start(f32[32,2,128]{2,1,0:T(2,128)} %bitcast.50), calls=%async_computation.4 | async-start | bytes 65536 | tf_op jit(solution)/shard_map/all_to_all | solution.py:111
  230.0 3.5 %collective-permute-start.14 = (f32[64,128]{1,0:T(8,128)S(1)}, f32[64,128]{1,0:T(8,128)}, u32[]{:S(2)}, u32[]{:S(2)}) collective-permute-start(f32[64,128]{1,0:T(8,128)S(1)} %get-tuple-element.7), channel_id=1, source_target_pairs={{0,4},{4,8},{8,12},{12,16},{16,20},{20,24},{24,28},{1,5},{5,9},{9,... | collective-permute-start | bytes 98312 | tf_op jit(solution)/shard_map/ppermute | solution.py:24
  233.5 1.9 collective-permute-start.15
  235.5 3.7 %collective-permute-start.16 = (f32[64,128]{1,0:T(8,128)S(1)}, f32[64,128]{1,0:T(8,128)}, u32[]{:S(2)}, u32[]{:S(2)}) collective-permute-start(f32[64,128]{1,0:T(8,128)S(1)} %get-tuple-element.6), channel_id=1, source_target_pairs={{0,1},{1,2},{2,3},{4,5},{5,6},{6,7},{8,9},{9,10},{10,11},{12,13},{... | collective-permute-start | bytes 98312 | tf_op jit(solution)/shard_map/ppermute | solution.py:24
  239.8 5.2 %all-to-all-start.5 = ((f32[32,2,128]{2,1,0:T(2,128)}), f32[32,2,128]{2,1,0:T(2,128)S(1)}, u32[]{:S(2)}, u32[]{:S(2)}) async-start(f32[32,2,128]{2,1,0:T(2,128)} %broadcast_in_dim.98), calls=%async_computation.5 | async-start | bytes 65536 | tf_op jit(solution)/shard_map/all_to_all | solution.py:13
  250.8 17.4 %all-to-all-done.5 = f32[32,2,128]{2,1,0:T(2,128)S(1)} async-done(((f32[32,2,128]{2,1,0:T(2,128)}), f32[32,2,128]{2,1,0:T(2,128)S(1)}, u32[]{:S(2)}, u32[]{:S(2)}) %all-to-all-start.5) | async-done | bytes 32800 | tf_op jit(solution)/shard_map/all_to_all | solution.py:13
  268.9 7.1 %all-to-all-start.6 = ((f32[32,2,128]{2,1,0:T(2,128)}), f32[32,2,128]{2,1,0:T(2,128)S(1)}, u32[]{:S(2)}, u32[]{:S(2)}) async-start(f32[32,2,128]{2,1,0:T(2,128)} %broadcast_in_dim.99), calls=%async_computation.6 | async-start | bytes 65536 | tf_op jit(solution)/shard_map/all_to_all | solution.py:13
  276.8 6.4 %all-to-all-done.6 = f32[32,2,128]{2,1,0:T(2,128)S(1)} async-done(((f32[32,2,128]{2,1,0:T(2,128)}), f32[32,2,128]{2,1,0:T(2,128)S(1)}, u32[]{:S(2)}, u32[]{:S(2)}) %all-to-all-start.6) | async-done | bytes 32800 | tf_op jit(solution)/shard_map/all_to_all | solution.py:13
  283.4 5.8 %cholesky.16 = f32[64,64]{1,0:T(8,128)S(1)} custom-call(f32[64,64]{1,0:T(8,128)S(1)} %fusion.37), custom_call_target="Cholesky" | custom-call | tf_op jit(solution)/shard_map/jit(cholesky)/cholesky | solution.py:30
  290.6 4.9 %custom-call.8 = f32[1,64,64]{1,2,0:T(8,128)S(1)} custom-call(f32[1,64,64]{2,1,0:T(8,128)S(1)} %fusion.32), custom_call_target="InvertDiagBlocksLowerTriangular" | custom-call | tf_op jit(solution)/shard_map/triangular_solve | solution.py:32
  (176 shorter events, 68.8 us)
Async XLA Ops:
  0.6 127.5 %copy-start = (f32[1,1,1,768,768]{4,3,2,1,0:T(8,128)S(1)}, f32[1,1,1,768,768]{4,3,2,1,0:T(8,128)}, u32[]{:S(2)}) copy-start(f32[1,1,1,768,768]{4,3,2,1,0:T(8,128)} %param.5) | copy-start | bytes 7077892
  2.1 9.3 %copy-start.9 = (f32[6,128]{1,0:T(8,128)}, f32[6,128]{1,0:T(8,128)S(1)}, u32[]{:S(2)}) copy-start(f32[6,128]{1,0:T(8,128)S(1)} %get-tuple-element.28) | copy-start | bytes 9220
  2.1 9.3 %copy-start.10 = (f32[6,128]{1,0:T(8,128)}, f32[6,128]{1,0:T(8,128)S(1)}, u32[]{:S(2)}) copy-start(f32[6,128]{1,0:T(8,128)S(1)} %get-tuple-element.27) | copy-start | bytes 9220
  11.1 24.7 %copy-start.13 = (f32[1,1,1,6,64]{4,2,3,1,0:T(1,128)S(1)}, f32[1,1,1,6,64]{4,2,3,1,0:T(1,128)}, u32[]{:S(2)}) copy-start(f32[1,1,1,6,64]{4,2,3,1,0:T(1,128)} %param.8) | copy-start | bytes 4612
  12.6 49.2 %collective-permute-start = (f32[6,6272]{1,0:T(8,128)}, f32[6,6272]{1,0:T(8,128)}, u32[]{:S(2)}, u32[]{:S(2)}) collective-permute-start(f32[6,6272]{1,0:T(8,128)} %get-tuple-element.22), channel_id=1, source_target_pairs={{0,32},{32,64},{64,96},{96,128},{128,160},{160,192},{192,224},{224... | collective-permute-start | bytes 451592 | tf_op jit(solution)/shard_map/ppermute | solution.py:24
  17.6 49.4 %collective-permute-start.1 = (f32[6,6272]{1,0:T(8,128)}, f32[6,6272]{1,0:T(8,128)}, u32[]{:S(2)}, u32[]{:S(2)}) collective-permute-start(f32[6,6272]{1,0:T(8,128)} %get-tuple-element.18), channel_id=1, source_target_pairs={{32,0},{64,32},{96,64},{128,96},{160,128},{192,160},{224,192},{256... | collective-permute-start | bytes 451592 | tf_op jit(solution)/shard_map/ppermute | solution.py:25
  18.9 51.5 %collective-permute-start.2 = (f32[6,6272]{1,0:T(8,128)}, f32[6,6272]{1,0:T(8,128)}, u32[]{:S(2)}, u32[]{:S(2)}) collective-permute-start(f32[6,6272]{1,0:T(8,128)} %get-tuple-element.19), channel_id=1, source_target_pairs={{0,4},{4,8},{8,12},{12,16},{16,20},{20,24},{24,28},{1,5},{5,9},{9,... | collective-permute-start | bytes 451592 | tf_op jit(solution)/shard_map/ppermute | solution.py:24
  22.9 50.7 %collective-permute-start.3 = (f32[6,6272]{1,0:T(8,128)}, f32[6,6272]{1,0:T(8,128)}, u32[]{:S(2)}, u32[]{:S(2)}) collective-permute-start(f32[6,6272]{1,0:T(8,128)} %get-tuple-element.20), channel_id=1, source_target_pairs={{4,0},{8,4},{12,8},{16,12},{20,16},{24,20},{28,24},{5,1},{9,5},{13... | collective-permute-start | bytes 451592 | tf_op jit(solution)/shard_map/ppermute | solution.py:25
  33.8 43.2 %collective-permute-start.4 = (f32[6,6272]{1,0:T(8,128)}, f32[6,6272]{1,0:T(8,128)}, u32[]{:S(2)}, u32[]{:S(2)}) collective-permute-start(f32[6,6272]{1,0:T(8,128)} %get-tuple-element.21), channel_id=1, source_target_pairs={{0,1},{1,2},{2,3},{4,5},{5,6},{6,7},{8,9},{9,10},{10,11},{12,13},{... | collective-permute-start | bytes 451592 | tf_op jit(solution)/shard_map/ppermute | solution.py:24
  38.0 60.4 %all-to-all-start = ((bf16[32,2,192]{2,1,0:T(2,128)(2,1)}), bf16[32,2,192]{2,1,0:T(2,128)(2,1)}, u32[]{:S(2)}, u32[]{:S(2)}) async-start(bf16[32,2,192]{2,1,0:T(2,128)(2,1)} %reshape.107), calls=%async_computation | async-start | bytes 65536 | tf_op jit(solution)/shard_map/all_to_all | solution.py:13
  61.7 19.9 %collective-permute-start.5 = (f32[6,6272]{1,0:T(8,128)}, f32[6,6272]{1,0:T(8,128)}, u32[]{:S(2)}, u32[]{:S(2)}) collective-permute-start(f32[6,6272]{1,0:T(8,128)} %get-tuple-element.17), channel_id=1, source_target_pairs={{1,0},{2,1},{3,2},{5,4},{6,5},{7,6},{9,8},{10,9},{11,10},{13,12},{... | collective-permute-start | bytes 451592 | tf_op jit(solution)/shard_map/ppermute | solution.py:25
  92.5 17.6 %copy-start.1 = (f32[3,84,1024]{2,1,0:T(8,128)S(1)}, f32[3,84,1024]{2,1,0:T(8,128)}, u32[]{:S(2)}) copy-start(f32[3,84,1024]{2,1,0:T(8,128)} %reshape.95) | copy-start | bytes 3096580
  98.3 11.7 %copy-start.5 = (f32[6,12,128]{2,1,0:T(8,128)S(1)}, f32[6,12,128]{2,1,0:T(8,128)}, u32[]{:S(2)}) copy-start(f32[6,12,128]{2,1,0:T(8,128)} %constant_dynamic-update-slice_fusion.8) | copy-start | bytes 110596
  100.2 22.9 %all-to-all-start.1 = ((bf16[32,32,384]{2,1,0:T(8,128)(2,1)}), bf16[32,32,384]{2,1,0:T(8,128)(2,1)}, u32[]{:S(2)}, u32[]{:S(2)}) async-start(bf16[32,32,384]{2,1,0:T(8,128)(2,1)} %broadcast_in_dim.85), calls=%async_computation.1 | async-start | bytes 1572864 | tf_op jit(solution)/shard_map/all_to_all | solution.py:13
  128.1 18.2 %copy-start.8 = (f32[1,1,1,3,2,64,128]{6,5,4,3,2,1,0:T(8,128)S(1)}, f32[1,1,1,3,2,64,128]{6,5,4,3,2,1,0:T(8,128)}, u32[]{:S(2)}) copy-start(f32[1,1,1,3,2,64,128]{6,5,4,3,2,1,0:T(8,128)} %param.9) | copy-start | bytes 589828
  128.1 18.2 %copy-start.7 = (f32[1,1,1,6,3,2,128]{6,3,5,4,2,1,0:T(8,128)S(1)}, f32[1,1,1,6,3,2,128]{6,3,5,4,2,1,0:T(8,128)}, u32[]{:S(2)}) copy-start(f32[1,1,1,6,3,2,128]{6,3,5,4,2,1,0:T(8,128)} %copy-done.6) | copy-start | bytes 55300
  129.7 11.5 %collective-permute-start.6 = (f32[64,128]{1,0:T(8,128)S(1)}, f32[64,128]{1,0:T(8,128)S(1)}, u32[]{:S(2)}, u32[]{:S(2)}) collective-permute-start(f32[64,128]{1,0:T(8,128)S(1)} %get-tuple-element.15), channel_id=1, source_target_pairs={{0,32},{32,64},{64,96},{96,128},{128,160},{160,192},{192,224},{224... | collective-permute-start | bytes 98312 | tf_op jit(solution)/shard_map/ppermute | solution.py:24
  133.1 9.5 %collective-permute-start.7 = (f32[64,128]{1,0:T(8,128)S(1)}, f32[64,128]{1,0:T(8,128)S(1)}, u32[]{:S(2)}, u32[]{:S(2)}) collective-permute-start(f32[64,128]{1,0:T(8,128)S(1)} %get-tuple-element.16), channel_id=1, source_target_pairs={{32,0},{64,32},{96,64},{128,96},{160,128},{192,160},{224,192},{256... | collective-permute-start | bytes 98312 | tf_op jit(solution)/shard_map/ppermute | solution.py:25
  134.4 8.2 %collective-permute-start.8 = (f32[64,128]{1,0:T(8,128)S(1)}, f32[64,128]{1,0:T(8,128)S(1)}, u32[]{:S(2)}, u32[]{:S(2)}) collective-permute-start(f32[64,128]{1,0:T(8,128)S(1)} %get-tuple-element.13), channel_id=1, source_target_pairs={{0,4},{4,8},{8,12},{12,16},{16,20},{20,24},{24,28},{1,5},{5,9},{9,... | collective-permute-start | bytes 98312 | tf_op jit(solution)/shard_map/ppermute | solution.py:24
  138.0 5.2 %collective-permute-start.9 = (f32[64,128]{1,0:T(8,128)S(1)}, f32[64,128]{1,0:T(8,128)S(1)}, u32[]{:S(2)}, u32[]{:S(2)}) collective-permute-start(f32[64,128]{1,0:T(8,128)S(1)} %get-tuple-element.14), channel_id=1, source_target_pairs={{4,0},{8,4},{12,8},{16,12},{20,16},{24,20},{28,24},{5,1},{9,5},{13... | collective-permute-start | bytes 98312 | tf_op jit(solution)/shard_map/ppermute | solution.py:25
  139.9 3.3 %collective-permute-start.10 = (f32[64,128]{1,0:T(8,128)S(1)}, f32[64,128]{1,0:T(8,128)S(1)}, u32[]{:S(2)}, u32[]{:S(2)}) collective-permute-start(f32[64,128]{1,0:T(8,128)S(1)} %get-tuple-element.12), channel_id=1, source_target_pairs={{0,1},{1,2},{2,3},{4,5},{5,6},{6,7},{8,9},{9,10},{10,11},{12,13},{... | collective-permute-start | bytes 98312 | tf_op jit(solution)/shard_map/ppermute | solution.py:24
  141.2 5.0 %collective-permute-start.11 = (f32[64,128]{1,0:T(8,128)S(1)}, f32[64,128]{1,0:T(8,128)S(1)}, u32[]{:S(2)}, u32[]{:S(2)}) collective-permute-start(f32[64,128]{1,0:T(8,128)S(1)} %get-tuple-element.11), channel_id=1, source_target_pairs={{1,0},{2,1},{3,2},{5,4},{6,5},{7,6},{9,8},{10,9},{11,10},{13,12},{... | collective-permute-start | bytes 98312 | tf_op jit(solution)/shard_map/ppermute | solution.py:25
  192.7 23.5 %copy-start.2 = (bf16[3,252,1024]{2,1,0:T(8,128)(2,1)S(1)}, bf16[3,252,1024]{2,1,0:T(8,128)(2,1)}, u32[]{:S(2)}) copy-start(bf16[3,252,1024]{2,1,0:T(8,128)(2,1)} %pad_maximum_fusion) | copy-start | bytes 4644868
  219.9 25.2 %collective-permute-start.12 = (f32[64,128]{1,0:T(8,128)S(1)}, f32[64,128]{1,0:T(8,128)S(1)}, u32[]{:S(2)}, u32[]{:S(2)}) collective-permute-start(f32[64,128]{1,0:T(8,128)S(1)} %get-tuple-element.9), channel_id=1, source_target_pairs={{0,32},{32,64},{64,96},{96,128},{128,160},{160,192},{192,224},{224... | collective-permute-start | bytes 98312 | tf_op jit(solution)/shard_map/ppermute | solution.py:24
  223.7 15.5 %all-to-all-start.4 = ((f32[32,2,128]{2,1,0:T(2,128)}), f32[32,2,128]{2,1,0:T(2,128)S(1)}, u32[]{:S(2)}, u32[]{:S(2)}) async-start(f32[32,2,128]{2,1,0:T(2,128)} %bitcast.50), calls=%async_computation.4 | async-start | bytes 65536 | tf_op jit(solution)/shard_map/all_to_all | solution.py:111
  228.7 19.1 %collective-permute-start.13 = (f32[64,128]{1,0:T(8,128)S(1)}, f32[64,128]{1,0:T(8,128)}, u32[]{:S(2)}, u32[]{:S(2)}) collective-permute-start(f32[64,128]{1,0:T(8,128)S(1)} %get-tuple-element.10), channel_id=1, source_target_pairs={{32,0},{64,32},{96,64},{128,96},{160,128},{192,160},{224,192},{256... | collective-permute-start | bytes 98312 | tf_op jit(solution)/shard_map/ppermute | solution.py:25
  230.0 18.5 %collective-permute-start.14 = (f32[64,128]{1,0:T(8,128)S(1)}, f32[64,128]{1,0:T(8,128)}, u32[]{:S(2)}, u32[]{:S(2)}) collective-permute-start(f32[64,128]{1,0:T(8,128)S(1)} %get-tuple-element.7), channel_id=1, source_target_pairs={{0,4},{4,8},{8,12},{12,16},{16,20},{20,24},{24,28},{1,5},{5,9},{9,... | collective-permute-start | bytes 98312 | tf_op jit(solution)/shard_map/ppermute | solution.py:24
  233.5 15.8 %collective-permute-start.15 = (f32[64,128]{1,0:T(8,128)S(1)}, f32[64,128]{1,0:T(8,128)}, u32[]{:S(2)}, u32[]{:S(2)}) collective-permute-start(f32[64,128]{1,0:T(8,128)S(1)} %get-tuple-element.8), channel_id=1, source_target_pairs={{4,0},{8,4},{12,8},{16,12},{20,16},{24,20},{28,24},{5,1},{9,5},{13... | collective-permute-start | bytes 98312 | tf_op jit(solution)/shard_map/ppermute | solution.py:25
  235.5 14.6 %collective-permute-start.16 = (f32[64,128]{1,0:T(8,128)S(1)}, f32[64,128]{1,0:T(8,128)}, u32[]{:S(2)}, u32[]{:S(2)}) collective-permute-start(f32[64,128]{1,0:T(8,128)S(1)} %get-tuple-element.6), channel_id=1, source_target_pairs={{0,1},{1,2},{2,3},{4,5},{5,6},{6,7},{8,9},{9,10},{10,11},{12,13},{... | collective-permute-start | bytes 98312 | tf_op jit(solution)/shard_map/ppermute | solution.py:24
  239.8 28.4 %all-to-all-start.5 = ((f32[32,2,128]{2,1,0:T(2,128)}), f32[32,2,128]{2,1,0:T(2,128)S(1)}, u32[]{:S(2)}, u32[]{:S(2)}) async-start(f32[32,2,128]{2,1,0:T(2,128)} %broadcast_in_dim.98), calls=%async_computation.5 | async-start | bytes 65536 | tf_op jit(solution)/shard_map/all_to_all | solution.py:13
  245.7 30.4 %collective-permute-start.17 = (f32[64,128]{1,0:T(8,128)S(1)}, f32[64,128]{1,0:T(8,128)}, u32[]{:S(2)}, u32[]{:S(2)}) collective-permute-start(f32[64,128]{1,0:T(8,128)S(1)} %get-tuple-element.5), channel_id=1, source_target_pairs={{1,0},{2,1},{3,2},{5,4},{6,5},{7,6},{9,8},{10,9},{11,10},{13,12},{... | collective-permute-start | bytes 98312 | tf_op jit(solution)/shard_map/ppermute | solution.py:25
  268.9 14.3 %all-to-all-start.6 = ((f32[32,2,128]{2,1,0:T(2,128)}), f32[32,2,128]{2,1,0:T(2,128)S(1)}, u32[]{:S(2)}, u32[]{:S(2)}) async-start(f32[32,2,128]{2,1,0:T(2,128)} %broadcast_in_dim.99), calls=%async_computation.6 | async-start | bytes 65536 | tf_op jit(solution)/shard_map/all_to_all | solution.py:13
  (5 other events, 9.0 us)

commit v2 on v1

--- a/solution.py
+++ b/solution.py
@@ -1,7 +1,11 @@
+import functools
+
 import jax
 import jax.numpy as jnp
 from jax import lax
+from jax.experimental import pallas as pl
 from jax.sharding import PartitionSpec as P
+
 
 HIGHEST = lax.Precision.HIGHEST
 AXES = ("gx", "gy", "gz")
@@ -26,10 +30,44 @@
     return arrived
 
 
-def gram_solve(matrix, target):
-    factor = jnp.linalg.cholesky(matrix)
-    middle = lax.linalg.triangular_solve(factor, target, left_side=True, lower=True)
-    return lax.linalg.triangular_solve(factor, middle, left_side=True, lower=True, transpose_a=True)
+def build_kernel(modes, parts, *refs):
+    own, arrived, (pieces, spread) = refs[0], refs[1:7], refs[7:]
+    every = (own,) + arrived
+    width = modes * parts
+    height = 14 * 8
+    for q in range(modes // 2):
+        for t in range(7):
+            blocks = []
+            for g in (2 * t, 2 * t + 1):
+                half, source = divmod(g, 7)
+                begin = (2 * q + half) * parts
+                blocks.append(every[source][:, begin : begin + parts])
+            value = jnp.concatenate(blocks, axis=0)
+            for piece in range(3):
+                rounded = value.astype(bf16)
+                pieces[q, piece * height + 16 * t : piece * height + 16 * (t + 1), :] = rounded
+                value = value - rounded.astype(jnp.float32)
+    for f in range(6):
+        spread[f, 0:8, :] = own[:, width + 128 * f : width + 128 * (f + 1)]
+        spread[f, 8:16, :] = -arrived[f][:, width : width + 128]
+
+
+def solve_kernel(grams, solution):
+    size = grams.shape[0]
+    table = grams[...]
+    row_index = lax.broadcasted_iota(jnp.int32, table.shape, 0)
+    for k in range(size):
+        pivot = table[k : k + 1, :] / table[k : k + 1, k : k + 1]
+        column = table[:, k : k + 1]
+        table = jnp.where(row_index == k, pivot, table - column * pivot)
+    solution[...] = table[:, size:]
+
+
+def gram_solve(grams):
+    size = grams.shape[0]
+    return pl.pallas_call(
+        solve_kernel, out_shape=jax.ShapeDtypeStruct((size, size), jnp.float32), name="gram_solve"
+    )(grams)
 
 
 def body(compliance, rigid_modes, coarse_inverse, coarse_rhs, dual_rhs):
@@ -50,27 +88,24 @@
         column = to_all(flat, "gx").reshape(long, modes * loads)
         return to_all(column, PLANE).reshape(parts, modes * loads)
 
-    start = gather(coarse_rhs[0, 0, 0])
+    flat = coarse_rhs[0, 0, 0].astype(bf16).reshape(1, modes * loads)
+    column = to_all(flat, "gx").reshape(long, modes * loads)
+    start = to_all(column, PLANE).reshape(parts, modes * loads)
 
     rows = coarse_inverse.reshape(modes, long, plane, modes).transpose(0, 3, 2, 1)
-    rows = rows.reshape(modes, modes * parts)
-    packed = [
-        jnp.concatenate([rows, traces[:, f]], axis=1) for f in range(6)
-    ]
+    rows = jnp.pad(rows.reshape(modes, modes * parts), ((0, 8 - modes), (0, 0)))
+    padded = jnp.pad(traces, ((0, 8 - modes), (0, 0), (0, 0)))
+    packed = [jnp.concatenate([rows, padded[:, f]], axis=1) for f in range(6)]
+    own = jnp.concatenate([rows, padded.reshape(8, order)], axis=1)
     arrived = neighbours(packed[0::2], packed[1::2])
-    all_rows = jnp.concatenate([rows] + [a[:, : modes * parts] for a in arrived], axis=0)
-    all_rows = all_rows.reshape(7 * modes, modes // 2, 2, parts).transpose(1, 2, 0, 3)
-    all_rows = all_rows.reshape(modes // 2, 14 * modes, parts)
-    high = lax.reduce_precision(all_rows, 8, 7)
-    rest = all_rows - high
-    middle = lax.reduce_precision(rest, 8, 7)
-    pieces = jnp.concatenate([high, middle, rest - middle], axis=1).astype(bf16)
-    spread = jnp.stack(
-        [
-            jnp.concatenate([traces[:, f], -arrived[f][:, modes * parts :]], axis=0)
-            for f in range(6)
-        ]
-    )
+    pieces, spread = pl.pallas_call(
+        functools.partial(build_kernel, modes, parts),
+        out_shape=(
+            jax.ShapeDtypeStruct((modes // 2, 3 * 14 * 8, parts), bf16),
+            jax.ShapeDtypeStruct((6, 16, face), jnp.float32),
+        ),
+        name="build_rows",
+    )(own, *arrived)
     spread = jnp.where(inside, spread, 0.0)
 
     def coarse(stacked):
@@ -78,11 +113,11 @@
         for q in range(modes // 2):
             columns = stacked[:, 2 * loads * q : 2 * loads * (q + 1)]
             total = total + jnp.dot(pieces[q], columns, preferred_element_type=jnp.float32)
-        total = total.reshape(3, 2, 7, modes, 2 * loads)
+        total = total.reshape(3, 2, 7, 8, 2 * loads)
         total = total[0] + (total[1] + total[2])
         weights = total[0, :, :, :loads] + total[1, :, :, loads:]
         both = jnp.concatenate(
-            [jnp.broadcast_to(weights[:1], (6, modes, loads)), weights[1:]], axis=1
+            [jnp.broadcast_to(weights[:1], (6, 8, loads)), weights[1:]], axis=1
         )
         return jnp.einsum("fkn,fkd->fnd", both, spread, precision=HIGHEST)
 
@@ -115,7 +150,7 @@
     grams = to_all(grams, PLANE).reshape(loads, 2 * loads)
 
     applied = assemble(image)
-    step_size = gram_solve(grams[:, :loads], grams[:, loads:])
+    step_size = gram_solve(grams)
     multipliers = multipliers + jnp.einsum(
         "fnd,nm->fmd", projected, step_size, precision=HIGHEST
     )
@@ -132,6 +167,7 @@
         P("gx", "gy", "gz", None, None),
         P("gx", "gy", "gz", None, None, None, None),
     )
+
     return jax.shard_map(
         body,
         mesh=mesh,

time: 300 us -> 260 us (0.87)
  local copies, waits for them, and re-layouts: 44.3 us -> 15.8 us
  other arithmetic: 31.3 us -> 9.1 us
  waiting for transfers between devices: 38.9 us -> 51.3 us
  blocking collectives: 68.3 us -> 56.9 us
  Pallas kernels: 0 us -> 9.9 us
    ppermute x9, waiting for transfers between devices: 3.66 us -> 16.1 us  [neighbours(): arrived.append(lax.ppermute(to_lower[d], axis, down))]
    another operation x7 -> x0, other arithmetic: 12.4 us -> none  [the longest x3 6.52 us: gram_solve(): factor = jnp.linalg.cholesky(matrix)]
    all_to_all x2, blocking collectives: 68.3 us -> 56.9 us  [to_all(): lax.all_to_all(jnp.broadcast_to(block[None], (lax.axis_size(axis),) + blo...]
    concatenate x8 -> x0, local copies, waits for them, and re-layouts: 9.96 us -> none  [body(): jnp.concatenate([rows] + [a[:, :modes * parts] for a in arrived], axis=0)]
    pallas_call x0 -> x2, Pallas kernels: none -> 9.9 us  [the longest x1 6.86 us: gram_solve(): pl.pallas_call(solve_kernel, out_shape=jax.ShapeDtypeStruct((size, size),...]
    slice x6 -> x0, local copies, waits for them, and re-layouts: 9.7 us -> none  [body(): a[:, :modes * parts]]
    ppermute x9, starting transfers between devices: 22.5 us -> 13.5 us  [neighbours(): arrived.append(lax.ppermute(to_lower[d], axis, down))]
    unnamed x52 -> x29, local copies, waits for them, and re-layouts: 8.85 us -> 2.59 us
  transfers between devices with their start and end apart: 23 -> 23, of which waited for: 5 -> 5; matrix products, arithmetic and copies ran while one was open for 16% -> 4% of each run, Pallas kernels for 0% -> 1%
where the time goes in v2:
time: 260 us; the launch traced here: 258 us
  starting transfers between devices  99.3 us (38%)
  blocking collectives  56.9 us (22%)
  waiting for transfers between devices  51.3 us (20%)
  local copies, waits for them, and re-layouts  15.8 us (6%)
  matrix products  14.8 us (6%)
  Pallas kernels  9.9 us (4%)
  other arithmetic  9.1 us (4%)
    all_to_all x2, blocking collectives, to_all(): lax.all_to_all(jnp.broadcast_to(block[None], (lax.axis_size(axis),) + blo...  56.9 us
    all_to_all x4, starting transfers between devices, to_all(): lax.all_to_all(jnp.broadcast_to(block[None], (lax.axis_size(axis),) + blo...  48 us
    all_to_all x4, waiting for transfers between devices, to_all(): lax.all_to_all(jnp.broadcast_to(block[None], (lax.axis_size(axis),) + blo...  35.2 us
    ppermute x9, starting transfers between devices, neighbours(): arrived.append(lax.ppermute(to_upper[d], axis, up))  32.8 us
    ppermute x9, waiting for transfers between devices, neighbours(): arrived.append(lax.ppermute(to_lower[d], axis, down))  16.1 us
    ppermute x9, starting transfers between devices, neighbours(): arrived.append(lax.ppermute(to_lower[d], axis, down))  13.5 us
    pallas_call x1, Pallas kernels, gram_solve(): pl.pallas_call(solve_kernel, out_shape=jax.ShapeDtypeStruct((size, size),...  6.86 us
    reshape x1, local copies, waits for them, and re-layouts, body(): coarse_inverse.reshape(modes, long, plane, modes).transpose(0, 3, 2, 1)  5.83 us
  transfers between devices with their start and end apart: 23, of which 5 were waited for; matrix products, arithmetic and copies ran while one was open for 4% of the time, Pallas kernels for 1%

profile of v2, /device:TPU:1, one launch (start us, length us, event | category | flops | bytes accessed | tf_op | source)
XLA Modules:
  0.0 258.3 jit_solution(649913992625900666)
XLA Ops:
  1.5 5.8 %reshape.73 = f32[6,32,32,6]{3,2,1,0:T(8,128)} reshape(f32[6,6144]{1,0:T(8,128)} %param.7) | data formatting | bytes 294912 | tf_op jit(solution)/shard_map/reshape | solution.py:95
  7.4 3.2 %copy.23 = f32[6,6,32,32]{3,2,1,0:T(8,128)S(1)} copy(f32[6,6,32,32]{1,2,3,0:T(8,128)} %bitcast.172) | data formatting | bytes 294912 | tf_op jit(solution)/shard_map/transpose | solution.py:95
  12.0 5.0 %collective-permute-start = (f32[8,6272]{1,0:T(8,128)}, f32[8,6272]{1,0:T(8,128)}, u32[]{:S(2)}, u32[]{:S(2)}) collective-permute-start(f32[8,6272]{1,0:T(8,128)} %get-tuple-element.23), channel_id=1, source_target_pairs={{0,32},{32,64},{64,96},{96,128},{128,160},{160,192},{192,224},{224... | collective-permute-start | bytes 602120 | tf_op jit(solution)/shard_map/ppermute | solution.py:28
  19.2 26.9 %all-to-all-start = ((bf16[32,2,192]{2,1,0:T(2,128)(2,1)}), bf16[32,2,192]{2,1,0:T(2,128)(2,1)S(1)}, u32[]{:S(2)}, u32[]{:S(2)}) async-start(bf16[32,2,192]{2,1,0:T(2,128)(2,1)} %reshape.87), calls=%async_computation | async-start | bytes 65536 | tf_op jit(solution)/shard_map/all_to_all | solution.py:17
  47.4 4.3 %collective-permute-start.2 = (f32[8,6272]{1,0:T(8,128)}, f32[8,6272]{1,0:T(8,128)}, u32[]{:S(2)}, u32[]{:S(2)}) collective-permute-start(f32[8,6272]{1,0:T(8,128)} %get-tuple-element.20), channel_id=1, source_target_pairs={{0,4},{4,8},{8,12},{12,16},{16,20},{20,24},{24,28},{1,5},{5,9},{9,... | collective-permute-start | bytes 602120 | tf_op jit(solution)/shard_map/ppermute | solution.py:28
  51.7 1.9 collective-permute-start.3
  53.6 3.8 %collective-permute-start.4 = (f32[8,6272]{1,0:T(8,128)}, f32[8,6272]{1,0:T(8,128)}, u32[]{:S(2)}, u32[]{:S(2)}) collective-permute-start(f32[8,6272]{1,0:T(8,128)} %get-tuple-element.22), channel_id=1, source_target_pairs={{0,1},{1,2},{2,3},{4,5},{5,6},{6,7},{8,9},{9,10},{10,11},{12,13},{... | collective-permute-start | bytes 602120 | tf_op jit(solution)/shard_map/ppermute | solution.py:28
  57.4 10.7 %all-to-all-done = bf16[32,2,192]{2,1,0:T(2,128)(2,1)S(1)} async-done(((bf16[32,2,192]{2,1,0:T(2,128)(2,1)}), bf16[32,2,192]{2,1,0:T(2,128)(2,1)S(1)}, u32[]{:S(2)}, u32[]{:S(2)}) %all-to-all-start) | async-done | bytes 24608 | tf_op jit(solution)/shard_map/all_to_all | solution.py:17
  69.2 9.4 %all-to-all-start.1 = ((bf16[32,32,384]{2,1,0:T(8,128)(2,1)}), bf16[32,32,384]{2,1,0:T(8,128)(2,1)S(1)}, u32[]{:S(2)}, u32[]{:S(2)}) async-start(bf16[32,32,384]{2,1,0:T(8,128)(2,1)} %broadcast_in_dim.83), calls=%async_computation.1 | async-start | bytes 1572864 | tf_op jit(solution)/shard_map/all_to_all | solution.py:17
  80.8 12.8 %collective-permute-done.5.refs_6_ = f32[8,6272]{1,0:T(8,128)} collective-permute-done((f32[8,6272]{1,0:T(8,128)}, f32[8,6272]{1,0:T(8,128)}, u32[]{:S(2)}, u32[]{:S(2)}) %collective-permute-start.5) | collective-permute-done | bytes 200736 | tf_op jit(solution)/shard_map/ppermute | solution.py:29
  93.6 3.0 %build_rows.1 = (bf16[3,336,1024]{2,1,0:T(8,128)(2,1)}, f32[6,16,128]{2,1,0:T(8,128)}) custom-call(f32[8,6912]{1,0:T(8,128)} %pad_maximum_fusion.refs_0_, f32[8,6272]{1,0:T(8,128)} %collective-permute-done.refs_1_, f32[8,6272]{1,0:T(8,128)} %collective-permute-done.1.refs_2_, f32[8,6272]{1,0:T(8,128)} %collective-permute-done.2.refs_3_, ...), custom_call_target="tpu_custom_call" | custom-call | tf_op jit(solution)/shard_map/build_rows/pallas_call | solution.py:101
  101.8 1.5 fusion.2
  103.4 2.2 collective-permute-start.6
  106.9 4.2 %collective-permute-start.8 = (f32[64,128]{1,0:T(8,128)S(1)}, f32[64,128]{1,0:T(8,128)S(1)}, u32[]{:S(2)}, u32[]{:S(2)}) collective-permute-start(f32[64,128]{1,0:T(8,128)S(1)} %get-tuple-element.14), channel_id=1, source_target_pairs={{0,4},{4,8},{8,12},{12,16},{16,20},{20,24},{24,28},{1,5},{5,9},{9,... | collective-permute-start | bytes 98312 | tf_op jit(solution)/shard_map/ppermute | solution.py:28
  111.1 1.9 collective-permute-start.9
  113.0 3.1 %collective-permute-start.10 = (f32[64,128]{1,0:T(8,128)S(1)}, f32[64,128]{1,0:T(8,128)S(1)}, u32[]{:S(2)}, u32[]{:S(2)}) collective-permute-start(f32[64,128]{1,0:T(8,128)S(1)} %get-tuple-element.13), channel_id=1, source_target_pairs={{0,1},{1,2},{2,3},{4,5},{5,6},{6,7},{8,9},{9,10},{10,11},{12,13},{... | collective-permute-start | bytes 98312 | tf_op jit(solution)/shard_map/ppermute | solution.py:28
  117.6 3.2 %collective-permute-done.11 = f32[64,128]{1,0:T(8,128)S(1)} collective-permute-done((f32[64,128]{1,0:T(8,128)S(1)}, f32[64,128]{1,0:T(8,128)S(1)}, u32[]{:S(2)}, u32[]{:S(2)}) %collective-permute-start.11) | collective-permute-done | bytes 32800 | tf_op jit(solution)/shard_map/ppermute | solution.py:29
  122.2 36.1 %all_to_all.35 = bf16[32,2,192]{2,1,0:T(2,128)(2,1)S(1)} all-to-all(bf16[32,2,192]{2,1,0:T(2,128)(2,1)S(1)} %reshape.89), channel_id=1, replica_groups=mesh['gx'=32,'gy'=8,'gz'=4] {'gx'}, dimensions={0} | all-to-all | bytes 49152 | tf_op jit(solution)/shard_map/all_to_all | solution.py:17
  158.5 20.8 %all_to_all.36 = bf16[32,32,384]{2,1,0:T(8,128)(2,1)S(1)} all-to-all(bf16[32,32,384]{2,1,0:T(8,128)(2,1)S(1)} %broadcast_in_dim.93), channel_id=1, replica_groups=mesh['gx'=32,'gy'=8,'gz'=4] {'gy','gz'}, dimensions={0} | all-to-all | bytes 1572864 | tf_op jit(solution)/shard_map/all_to_all | solution.py:17
  181.1 1.5 fusion
  183.8 2.8 %collective-permute-start.12 = (f32[64,128]{1,0:T(8,128)S(1)}, f32[64,128]{1,0:T(8,128)}, u32[]{:S(2)}, u32[]{:S(2)}) collective-permute-start(f32[64,128]{1,0:T(8,128)S(1)} %get-tuple-element.10), channel_id=1, source_target_pairs={{0,32},{32,64},{64,96},{96,128},{128,160},{160,192},{192,224},{224... | collective-permute-start | bytes 98312 | tf_op jit(solution)/shard_map/ppermute | solution.py:28
  188.2 5.0 %all-to-all-start.4 = ((f32[32,2,128]{2,1,0:T(2,128)}), f32[32,2,128]{2,1,0:T(2,128)S(1)}, u32[]{:S(2)}, u32[]{:S(2)}) async-start(f32[32,2,128]{2,1,0:T(2,128)} %bitcast.46), calls=%async_computation.4 | async-start | bytes 65536 | tf_op jit(solution)/shard_map/all_to_all | solution.py:146
  194.5 3.5 %collective-permute-start.14 = (f32[64,128]{1,0:T(8,128)S(1)}, f32[64,128]{1,0:T(8,128)}, u32[]{:S(2)}, u32[]{:S(2)}) collective-permute-start(f32[64,128]{1,0:T(8,128)S(1)} %get-tuple-element.8), channel_id=1, source_target_pairs={{0,4},{4,8},{8,12},{12,16},{16,20},{20,24},{24,28},{1,5},{5,9},{9,... | collective-permute-start | bytes 98312 | tf_op jit(solution)/shard_map/ppermute | solution.py:28
  198.1 1.9 collective-permute-start.15
  200.0 3.7 %collective-permute-start.16 = (f32[64,128]{1,0:T(8,128)S(1)}, f32[64,128]{1,0:T(8,128)}, u32[]{:S(2)}, u32[]{:S(2)}) collective-permute-start(f32[64,128]{1,0:T(8,128)S(1)} %get-tuple-element.7), channel_id=1, source_target_pairs={{0,1},{1,2},{2,3},{4,5},{5,6},{6,7},{8,9},{9,10},{10,11},{12,13},{... | collective-permute-start | bytes 98312 | tf_op jit(solution)/shard_map/ppermute | solution.py:28
  204.4 4.6 %all-to-all-start.5 = ((f32[32,2,128]{2,1,0:T(2,128)}), f32[32,2,128]{2,1,0:T(2,128)S(1)}, u32[]{:S(2)}, u32[]{:S(2)}) async-start(f32[32,2,128]{2,1,0:T(2,128)} %broadcast_in_dim.96), calls=%async_computation.5 | async-start | bytes 65536 | tf_op jit(solution)/shard_map/all_to_all | solution.py:17
  214.1 18.1 %all-to-all-done.5 = f32[32,2,128]{2,1,0:T(2,128)S(1)} async-done(((f32[32,2,128]{2,1,0:T(2,128)}), f32[32,2,128]{2,1,0:T(2,128)S(1)}, u32[]{:S(2)}, u32[]{:S(2)}) %all-to-all-start.5) | async-done | bytes 32800 | tf_op jit(solution)/shard_map/all_to_all | solution.py:17
  232.8 7.1 %all-to-all-start.6 = ((f32[32,2,128]{2,1,0:T(2,128)}), f32[32,2,128]{2,1,0:T(2,128)S(1)}, u32[]{:S(2)}, u32[]{:S(2)}) async-start(f32[32,2,128]{2,1,0:T(2,128)} %broadcast_in_dim.97), calls=%async_computation.6 | async-start | bytes 65536 | tf_op jit(solution)/shard_map/all_to_all | solution.py:17
  240.7 6.4 %all-to-all-done.6 = f32[32,2,128]{2,1,0:T(2,128)S(1)} async-done(((f32[32,2,128]{2,1,0:T(2,128)}), f32[32,2,128]{2,1,0:T(2,128)S(1)}, u32[]{:S(2)}, u32[]{:S(2)}) %all-to-all-start.6) | async-done | bytes 32800 | tf_op jit(solution)/shard_map/all_to_all | solution.py:17
  247.8 6.9 %gram_solve.1 = f32[64,64]{1,0:T(8,128)} custom-call(f32[64,128]{1,0:T(8,128)} %bitcast.186), custom_call_target="tpu_custom_call" | custom-call | tf_op jit(solution)/shard_map/gram_solve/pallas_call | solution.py:68
  254.7 1.8 fusion.5
  256.5 1.8 fusion.4
  (118 shorter events, 31.7 us)
Async XLA Ops:
  0.6 101.2 %copy-start = (f32[1,1,1,768,768]{4,3,2,1,0:T(8,128)S(1)}, f32[1,1,1,768,768]{4,3,2,1,0:T(8,128)}, u32[]{:S(2)}) copy-start(f32[1,1,1,768,768]{4,3,2,1,0:T(8,128)} %param.5) | copy-start | bytes 7077892
  10.5 6.5 %copy-start.4 = (f32[1,1,1,6,64]{4,2,3,1,0:T(1,128)S(1)}, f32[1,1,1,6,64]{4,2,3,1,0:T(1,128)}, u32[]{:S(2)}) copy-start(f32[1,1,1,6,64]{4,2,3,1,0:T(1,128)} %param.8) | copy-start | bytes 4612
  12.0 66.7 %collective-permute-start = (f32[8,6272]{1,0:T(8,128)}, f32[8,6272]{1,0:T(8,128)}, u32[]{:S(2)}, u32[]{:S(2)}) collective-permute-start(f32[8,6272]{1,0:T(8,128)} %get-tuple-element.23), channel_id=1, source_target_pairs={{0,32},{32,64},{64,96},{96,128},{128,160},{160,192},{192,224},{224... | collective-permute-start | bytes 602120 | tf_op jit(solution)/shard_map/ppermute | solution.py:28
  19.2 48.9 %all-to-all-start = ((bf16[32,2,192]{2,1,0:T(2,128)(2,1)}), bf16[32,2,192]{2,1,0:T(2,128)(2,1)S(1)}, u32[]{:S(2)}, u32[]{:S(2)}) async-start(bf16[32,2,192]{2,1,0:T(2,128)(2,1)} %reshape.87), calls=%async_computation | async-start | bytes 65536 | tf_op jit(solution)/shard_map/all_to_all | solution.py:17
  46.1 34.7 %collective-permute-start.1 = (f32[8,6272]{1,0:T(8,128)}, f32[8,6272]{1,0:T(8,128)}, u32[]{:S(2)}, u32[]{:S(2)}) collective-permute-start(f32[8,6272]{1,0:T(8,128)} %get-tuple-element.19), channel_id=1, source_target_pairs={{32,0},{64,32},{96,64},{128,96},{160,128},{192,160},{224,192},{256... | collective-permute-start | bytes 602120 | tf_op jit(solution)/shard_map/ppermute | solution.py:29
  47.4 33.4 %collective-permute-start.2 = (f32[8,6272]{1,0:T(8,128)}, f32[8,6272]{1,0:T(8,128)}, u32[]{:S(2)}, u32[]{:S(2)}) collective-permute-start(f32[8,6272]{1,0:T(8,128)} %get-tuple-element.20), channel_id=1, source_target_pairs={{0,4},{4,8},{8,12},{12,16},{16,20},{20,24},{24,28},{1,5},{5,9},{9,... | collective-permute-start | bytes 602120 | tf_op jit(solution)/shard_map/ppermute | solution.py:28
  51.7 29.1 %collective-permute-start.3 = (f32[8,6272]{1,0:T(8,128)}, f32[8,6272]{1,0:T(8,128)}, u32[]{:S(2)}, u32[]{:S(2)}) collective-permute-start(f32[8,6272]{1,0:T(8,128)} %get-tuple-element.21), channel_id=1, source_target_pairs={{4,0},{8,4},{12,8},{16,12},{20,16},{24,20},{28,24},{5,1},{9,5},{13... | collective-permute-start | bytes 602120 | tf_op jit(solution)/shard_map/ppermute | solution.py:29
  53.6 27.1 %collective-permute-start.4 = (f32[8,6272]{1,0:T(8,128)}, f32[8,6272]{1,0:T(8,128)}, u32[]{:S(2)}, u32[]{:S(2)}) collective-permute-start(f32[8,6272]{1,0:T(8,128)} %get-tuple-element.22), channel_id=1, source_target_pairs={{0,1},{1,2},{2,3},{4,5},{5,6},{6,7},{8,9},{9,10},{10,11},{12,13},{... | collective-permute-start | bytes 602120 | tf_op jit(solution)/shard_map/ppermute | solution.py:28
  69.2 27.4 %all-to-all-start.1 = ((bf16[32,32,384]{2,1,0:T(8,128)(2,1)}), bf16[32,32,384]{2,1,0:T(8,128)(2,1)S(1)}, u32[]{:S(2)}, u32[]{:S(2)}) async-start(bf16[32,32,384]{2,1,0:T(8,128)(2,1)} %broadcast_in_dim.83), calls=%async_computation.1 | async-start | bytes 1572864 | tf_op jit(solution)/shard_map/all_to_all | solution.py:17
  78.6 14.9 %collective-permute-start.5 = (f32[8,6272]{1,0:T(8,128)}, f32[8,6272]{1,0:T(8,128)}, u32[]{:S(2)}, u32[]{:S(2)}) collective-permute-start(f32[8,6272]{1,0:T(8,128)} %get-tuple-element.18), channel_id=1, source_target_pairs={{1,0},{2,1},{3,2},{5,4},{6,5},{7,6},{9,8},{10,9},{11,10},{13,12},{... | collective-permute-start | bytes 602120 | tf_op jit(solution)/shard_map/ppermute | solution.py:29
  96.6 4.5 %copy-start.1 = (f32[6,16,128]{2,1,0:T(8,128)S(1)}, f32[6,16,128]{2,1,0:T(8,128)}, u32[]{:S(2)}) copy-start(f32[6,16,128]{2,1,0:T(8,128)} %get-tuple-element.5) | copy-start | bytes 147460
  101.7 19.1 %copy-start.2 = (f32[1,1,1,3,2,64,128]{6,5,4,3,2,1,0:T(8,128)S(1)}, f32[1,1,1,3,2,64,128]{6,5,4,3,2,1,0:T(8,128)}, u32[]{:S(2)}) copy-start(f32[1,1,1,3,2,64,128]{6,5,4,3,2,1,0:T(8,128)} %param.9) | copy-start | bytes 589828
  103.4 12.8 %collective-permute-start.6 = (f32[64,128]{1,0:T(8,128)S(1)}, f32[64,128]{1,0:T(8,128)S(1)}, u32[]{:S(2)}, u32[]{:S(2)}) collective-permute-start(f32[64,128]{1,0:T(8,128)S(1)} %get-tuple-element.16), channel_id=1, source_target_pairs={{0,32},{32,64},{64,96},{96,128},{128,160},{160,192},{192,224},{224... | collective-permute-start | bytes 98312 | tf_op jit(solution)/shard_map/ppermute | solution.py:28
  105.6 11.9 %collective-permute-start.7 = (f32[64,128]{1,0:T(8,128)S(1)}, f32[64,128]{1,0:T(8,128)S(1)}, u32[]{:S(2)}, u32[]{:S(2)}) collective-permute-start(f32[64,128]{1,0:T(8,128)S(1)} %get-tuple-element.17), channel_id=1, source_target_pairs={{32,0},{64,32},{96,64},{128,96},{160,128},{192,160},{224,192},{256... | collective-permute-start | bytes 98312 | tf_op jit(solution)/shard_map/ppermute | solution.py:29
  106.9 10.6 %collective-permute-start.8 = (f32[64,128]{1,0:T(8,128)S(1)}, f32[64,128]{1,0:T(8,128)S(1)}, u32[]{:S(2)}, u32[]{:S(2)}) collective-permute-start(f32[64,128]{1,0:T(8,128)S(1)} %get-tuple-element.14), channel_id=1, source_target_pairs={{0,4},{4,8},{8,12},{12,16},{16,20},{20,24},{24,28},{1,5},{5,9},{9,... | collective-permute-start | bytes 98312 | tf_op jit(solution)/shard_map/ppermute | solution.py:28
  111.1 6.4 %collective-permute-start.9 = (f32[64,128]{1,0:T(8,128)S(1)}, f32[64,128]{1,0:T(8,128)S(1)}, u32[]{:S(2)}, u32[]{:S(2)}) collective-permute-start(f32[64,128]{1,0:T(8,128)S(1)} %get-tuple-element.15), channel_id=1, source_target_pairs={{4,0},{8,4},{12,8},{16,12},{20,16},{24,20},{28,24},{5,1},{9,5},{13... | collective-permute-start | bytes 98312 | tf_op jit(solution)/shard_map/ppermute | solution.py:29
  113.0 4.5 %collective-permute-start.10 = (f32[64,128]{1,0:T(8,128)S(1)}, f32[64,128]{1,0:T(8,128)S(1)}, u32[]{:S(2)}, u32[]{:S(2)}) collective-permute-start(f32[64,128]{1,0:T(8,128)S(1)} %get-tuple-element.13), channel_id=1, source_target_pairs={{0,1},{1,2},{2,3},{4,5},{5,6},{6,7},{8,9},{9,10},{10,11},{12,13},{... | collective-permute-start | bytes 98312 | tf_op jit(solution)/shard_map/ppermute | solution.py:28
  116.2 4.7 %collective-permute-start.11 = (f32[64,128]{1,0:T(8,128)S(1)}, f32[64,128]{1,0:T(8,128)S(1)}, u32[]{:S(2)}, u32[]{:S(2)}) collective-permute-start(f32[64,128]{1,0:T(8,128)S(1)} %get-tuple-element.12), channel_id=1, source_target_pairs={{1,0},{2,1},{3,2},{5,4},{6,5},{7,6},{9,8},{10,9},{11,10},{13,12},{... | collective-permute-start | bytes 98312 | tf_op jit(solution)/shard_map/ppermute | solution.py:29
  158.4 20.9 %copy-start.5 = (bf16[3,336,1024]{2,1,0:T(8,128)(2,1)S(1)}, bf16[3,336,1024]{2,1,0:T(8,128)(2,1)}, u32[]{:S(2)}) copy-start(bf16[3,336,1024]{2,1,0:T(8,128)(2,1)} %get-tuple-element.4) | copy-start | bytes 6193156
  183.8 25.2 %collective-permute-start.12 = (f32[64,128]{1,0:T(8,128)S(1)}, f32[64,128]{1,0:T(8,128)}, u32[]{:S(2)}, u32[]{:S(2)}) collective-permute-start(f32[64,128]{1,0:T(8,128)S(1)} %get-tuple-element.10), channel_id=1, source_target_pairs={{0,32},{32,64},{64,96},{96,128},{128,160},{160,192},{192,224},{224... | collective-permute-start | bytes 98312 | tf_op jit(solution)/shard_map/ppermute | solution.py:28
  188.2 15.5 %all-to-all-start.4 = ((f32[32,2,128]{2,1,0:T(2,128)}), f32[32,2,128]{2,1,0:T(2,128)S(1)}, u32[]{:S(2)}, u32[]{:S(2)}) async-start(f32[32,2,128]{2,1,0:T(2,128)} %bitcast.46), calls=%async_computation.4 | async-start | bytes 65536 | tf_op jit(solution)/shard_map/all_to_all | solution.py:146
  193.2 17.8 %collective-permute-start.13 = (f32[64,128]{1,0:T(8,128)}, f32[64,128]{1,0:T(8,128)}, u32[]{:S(2)}, u32[]{:S(2)}) collective-permute-start(f32[64,128]{1,0:T(8,128)} %get-tuple-element.11), channel_id=1, source_target_pairs={{32,0},{64,32},{96,64},{128,96},{160,128},{192,160},{224,192},{256... | collective-permute-start | bytes 98312 | tf_op jit(solution)/shard_map/ppermute | solution.py:29
  194.5 17.3 %collective-permute-start.14 = (f32[64,128]{1,0:T(8,128)S(1)}, f32[64,128]{1,0:T(8,128)}, u32[]{:S(2)}, u32[]{:S(2)}) collective-permute-start(f32[64,128]{1,0:T(8,128)S(1)} %get-tuple-element.8), channel_id=1, source_target_pairs={{0,4},{4,8},{8,12},{12,16},{16,20},{20,24},{24,28},{1,5},{5,9},{9,... | collective-permute-start | bytes 98312 | tf_op jit(solution)/shard_map/ppermute | solution.py:28
  198.1 14.5 %collective-permute-start.15 = (f32[64,128]{1,0:T(8,128)S(1)}, f32[64,128]{1,0:T(8,128)}, u32[]{:S(2)}, u32[]{:S(2)}) collective-permute-start(f32[64,128]{1,0:T(8,128)S(1)} %get-tuple-element.9), channel_id=1, source_target_pairs={{4,0},{8,4},{12,8},{16,12},{20,16},{24,20},{28,24},{5,1},{9,5},{13... | collective-permute-start | bytes 98312 | tf_op jit(solution)/shard_map/ppermute | solution.py:29
  200.0 13.4 %collective-permute-start.16 = (f32[64,128]{1,0:T(8,128)S(1)}, f32[64,128]{1,0:T(8,128)}, u32[]{:S(2)}, u32[]{:S(2)}) collective-permute-start(f32[64,128]{1,0:T(8,128)S(1)} %get-tuple-element.7), channel_id=1, source_target_pairs={{0,1},{1,2},{2,3},{4,5},{5,6},{6,7},{8,9},{9,10},{10,11},{12,13},{... | collective-permute-start | bytes 98312 | tf_op jit(solution)/shard_map/ppermute | solution.py:28
  204.4 27.8 %all-to-all-start.5 = ((f32[32,2,128]{2,1,0:T(2,128)}), f32[32,2,128]{2,1,0:T(2,128)S(1)}, u32[]{:S(2)}, u32[]{:S(2)}) async-start(f32[32,2,128]{2,1,0:T(2,128)} %broadcast_in_dim.96), calls=%async_computation.5 | async-start | bytes 65536 | tf_op jit(solution)/shard_map/all_to_all | solution.py:17
  209.0 31.0 %collective-permute-start.17 = (f32[64,128]{1,0:T(8,128)S(1)}, f32[64,128]{1,0:T(8,128)}, u32[]{:S(2)}, u32[]{:S(2)}) collective-permute-start(f32[64,128]{1,0:T(8,128)S(1)} %get-tuple-element.6), channel_id=1, source_target_pairs={{1,0},{2,1},{3,2},{5,4},{6,5},{7,6},{9,8},{10,9},{11,10},{13,12},{... | collective-permute-start | bytes 98312 | tf_op jit(solution)/shard_map/ppermute | solution.py:29
  232.8 14.3 %all-to-all-start.6 = ((f32[32,2,128]{2,1,0:T(2,128)}), f32[32,2,128]{2,1,0:T(2,128)S(1)}, u32[]{:S(2)}, u32[]{:S(2)}) async-start(f32[32,2,128]{2,1,0:T(2,128)} %broadcast_in_dim.97), calls=%async_computation.6 | async-start | bytes 65536 | tf_op jit(solution)/shard_map/all_to_all | solution.py:17
  247.2 0.6 copy-start.3

commit v3 on v1

v3 whole, which is shorter than its diff:
```python
import functools

import jax
import jax.numpy as jnp
from jax import lax
from jax.experimental import pallas as pl
from jax.experimental.pallas import tpu as pltpu
from jax.sharding import PartitionSpec as P


HIGHEST = lax.Precision.HIGHEST
AXES = ("gx", "gy", "gz")
PLANE = ("gy", "gz")
bf16 = jnp.bfloat16
f32 = jnp.float32


def to_all(block, axis):
    return lax.all_to_all(
        jnp.broadcast_to(block[None], (lax.axis_size(axis),) + block.shape), axis, 0, 0, tiled=True
    )


def swap(outgoing):
    arrived = []
    for d, axis in enumerate(AXES):
        size = lax.axis_size(axis)
        even = [(i, i ^ 1) for i in range(size)]
        odd = [(i, i + 1 if i % 2 else i - 1) for i in range(1, size - 1)]
        arrived.append(lax.ppermute(outgoing[2 * d], axis, even))
        arrived.append(lax.ppermute(outgoing[2 * d + 1], axis, odd))
    return arrived


def pick(is_even, f, pair):
    even, odd = pair
    first, second = (odd, even) if f % 2 == 0 else (even, odd)
    return jnp.where(is_even, first, second)


def prepare(modes, long, plane, flags, rows, traces, *packed):
    turned = packed[-1]
    packed = packed[:-1]
    parts = long * plane
    blank = jnp.zeros((8 - modes, 128), f32)
    for b in range(modes * parts // 128):
        block = jnp.concatenate([rows[:, 128 * b : 128 * (b + 1)], blank], axis=0)
        turned[128 * b : 128 * (b + 1), :] = block.T
    group = 128 // long
    for j in range(modes):
        for b in range(parts // 128):
            strips = [
                turned[pl.ds((group * b + i) * modes + j, long, stride=plane * modes), :]
                for i in range(group)
            ]
            block = jnp.concatenate(strips, axis=0).T
            begin = j * parts + 128 * b
            for out in packed:
                out[:, begin : begin + 128] = block
    for d in range(3):
        is_even = flags[d] == 0
        minus = jnp.concatenate([traces[2 * d], blank], axis=0)
        plus = jnp.concatenate([traces[2 * d + 1], blank], axis=0)
        packed[2 * d][:, modes * parts :] = jnp.where(is_even, plus, minus)
        packed[2 * d + 1][:, modes * parts :] = jnp.where(is_even, minus, plus)


def build(modes, parts, flags, traces, own, *refs):
    arrived, (pieces, spread) = refs[:6], refs[6:]
    width = modes * parts
    height = 14 * 8
    evens = [flags[d] == 0 for d in range(3)]
    blank = jnp.zeros((8 - modes, 128), f32)

    def take(source, begin, size):
        if source == 0:
            return own[:, begin : begin + size]
        f = source - 1
        pair = [r[:, begin : begin + size] for r in arrived[2 * (f // 2) : 2 * (f // 2) + 2]]
        return pick(evens[f // 2], f, pair)

    for q in range(modes // 2):
        for t in range(7):
            blocks = []
            for g in (2 * t, 2 * t + 1):
                half, source = divmod(g, 7)
                blocks.append(take(source, (2 * q + half) * parts, parts))
            value = jnp.concatenate(blocks, axis=0)
            for piece in range(3):
                rounded = value.astype(bf16)
                pieces[q, piece * height + 16 * t : piece * height + 16 * (t + 1), :] = rounded
                value = value - rounded.astype(f32)
    spread[...] = jnp.zeros_like(spread)
    for f in range(6):
        lanes = slice(128 * f, 128 * (f + 1))
        mine = jnp.concatenate([traces[f], blank], axis=0)
        other = -take(f + 1, width, 128)
        if f % 2 == 0:
            inside = flags[3 + f // 2] > 0
            mine = jnp.where(inside, mine, 0.0)
            other = jnp.where(inside, other, 0.0)
        spread[0:8, lanes] = mine
        spread[8 * (f + 1) : 8 * (f + 2), lanes] = other


def coarse(stacked, pieces, spread):
    lanes = stacked.shape[1] // pieces.shape[0]
    total = jnp.zeros((pieces.shape[1], lanes), f32)
    for q in range(pieces.shape[0]):
        total = total + jnp.dot(
            pieces[q], stacked[:, lanes * q : lanes * (q + 1)], preferred_element_type=f32
        )
    height = pieces.shape[1] // 3
    total = total[:height] + (total[height : 2 * height] + total[2 * height :])
    weights = total[: height // 2, : lanes // 2] + total[height // 2 :, lanes // 2 :]
    return jnp.dot(weights.T, spread[...], precision=HIGHEST, preferred_element_type=f32)


def send_faces(flags, wide, outgoing):
    for d in range(3):
        minus = wide[:, 256 * d : 256 * d + 128]
        plus = wide[:, 256 * d + 128 : 256 * d + 256]
        outgoing[2 * d][...] = jnp.where(flags[d] == 0, plus, minus)
        outgoing[2 * d + 1][...] = jnp.where(flags[d] == 0, minus, plus)


def assembled(flags, wide, arrived, f):
    d = f // 2
    pair = (arrived[2 * d][...], arrived[2 * d + 1][...])
    value = wide[:, 128 * f : 128 * (f + 1)] - pick(flags[d] == 0, f, pair)
    return jnp.where(flags[3 + d] > 0, value, 0.0) if f % 2 == 0 else value


def start_kernel(flags, stacked, pieces, spread, matrix, field, image, *outgoing):
    value = coarse(stacked, pieces, spread)
    field[...] = value
    image[...] = jnp.dot(value, matrix[...], precision=HIGHEST, preferred_element_type=f32)
    send_faces(flags, image, outgoing)


def residual_kernel(flags, gaps, traces, image, *refs):
    arrived, (residual, sums) = refs[:6], refs[6:]
    total = 0.0
    for f in range(6):
        value = gaps[f] - assembled(flags, image, arrived, f)
        residual[:, 128 * f : 128 * (f + 1)] = value
        total = total + lax.dot_general(
            traces[f], value, (((1,), (1,)), ((), ())), precision=HIGHEST, preferred_element_type=f32
        )
    sums[...] = total.astype(bf16)


def project_kernel(flags, stacked, pieces, spread, matrix, residual, field, image, grams, *outgoing):
    value = residual[...] - coarse(stacked, pieces, spread)
    field[...] = value
    applied = jnp.dot(value, matrix[...], precision=HIGHEST, preferred_element_type=f32)
    image[...] = applied
    across = (((1,), (1,)), ((), ()))
    loads = value.shape[0]
    grams[:, :loads] = lax.dot_general(
        value, applied, across, precision=HIGHEST, preferred_element_type=f32
    )
    plus = jnp.concatenate([value[:, 256 * d + 128 : 256 * d + 256] for d in range(3)], axis=1)
    grams[:, loads:] = lax.dot_general(
        plus, plus, across, precision=HIGHEST, preferred_element_type=f32
    )
    send_faces(flags, image, outgoing)


def solve(table):
    size = table.shape[0]
    row = lax.broadcasted_iota(jnp.int32, table.shape, 0)
    for k in range(0, size, 2):
        first, second = table[k : k + 1, :], table[k + 1 : k + 2, :]
        left, right = table[:, k : k + 1], table[:, k + 1 : k + 2]
        inverse = 1.0 / left[k : k + 1]
        ratio = left[k + 1 : k + 2] * inverse
        corner = 1.0 / (right[k + 1 : k + 2] - ratio * right[k : k + 1])
        lower = (second - ratio * first) * corner
        upper = (first - right[k : k + 1] * lower) * inverse
        table = jnp.where(
            row == k, upper, jnp.where(row == k + 1, lower, table - left * upper - right * lower)
        )
    return table[:, size:]


def final_kernel(flags, grams, multipliers, residual, field, image, *refs):
    arrived, (new_multipliers, new_residual) = refs[:6], refs[6:]
    step = solve(grams[...]).T
    change = jnp.dot(step, field[...], precision=HIGHEST, preferred_element_type=f32)
    for f in range(6):
        lanes = slice(128 * f, 128 * (f + 1))
        new_multipliers[f] = multipliers[:, lanes] + change[:, lanes]
        applied = assembled(flags, image, arrived, f)
        new_residual[f] = residual[:, lanes] - jnp.dot(
            step, applied, precision=HIGHEST, preferred_element_type=f32
        )


def call(kernel, outs, *args, **options):
    flags = pl.BlockSpec(memory_space=pltpu.SMEM)
    block = pl.BlockSpec(memory_space=pltpu.VMEM)
    return pl.pallas_call(
        kernel,
        out_shape=[jax.ShapeDtypeStruct(shape, kind) for shape, kind in outs],
        in_specs=[flags] + [block] * (len(args) - 1),
        out_specs=[block] * len(outs),
        compiler_params=pltpu.CompilerParams(vmem_limit_bytes=24 << 20),
        **options,
    )(*args)


def body(compliance, rigid_modes, coarse_inverse, coarse_rhs, dual_rhs):
    face, loads = dual_rhs.shape[-1], dual_rhs.shape[-2]
    modes = rigid_modes.shape[3]
    long, plane = lax.axis_size("gx"), lax.axis_size(PLANE)
    parts = long * plane
    matrix = compliance[0, 0, 0]
    traces = rigid_modes[0, 0, 0].transpose(1, 2, 0, 3).reshape(6, modes, face)
    gaps = dual_rhs[0, 0, 0].reshape(6, loads, face)
    where = [lax.axis_index(axis) for axis in AXES]
    flags = jnp.stack([w % 2 for w in where] + [jnp.minimum(w, 1) for w in where]).astype(jnp.int32)
    wide, faces = ((loads, 6 * face), f32), ((6, loads, face), f32)
    packs = ((8, modes * parts + face), f32)

    def along(sums):
        return to_all(sums.astype(bf16).reshape(1, modes * loads), "gx").reshape(long, modes * loads)

    def across(column):
        return to_all(column, PLANE).reshape(parts, modes * loads)

    column = along(coarse_rhs[0, 0, 0])
    packed = call(
        functools.partial(prepare, modes, long, plane),
        [packs] * 6,
        flags,
        coarse_inverse,
        traces,
        scratch_shapes=[pltpu.VMEM((modes * parts, 8), f32)],
        name="prepare_rows",
    )
    arrived = swap(packed)
    stacked = across(column)
    pieces, spread = call(
        functools.partial(build, modes, parts),
        [((modes // 2, 3 * 14 * 8, parts), bf16), ((7 * 8, 6 * face), f32)],
        flags,
        traces,
        packed[0],
        *arrived,
        name="build_rows",
    )

    multipliers, image, *outgoing = call(
        start_kernel,
        [wide, wide] + [((loads, face), f32)] * 6,
        flags,
        stacked,
        pieces,
        spread,
        matrix,
        name="start_fields",
    )
    residual, sums = call(
        residual_kernel,
        [wide, ((modes, loads), bf16)],
        flags,
        gaps,
        traces,
        image,
        *swap(outgoing),
        name="residual",
    )
    projected, image, grams, *outgoing = call(
        project_kernel,
        [wide, wide, ((loads, 2 * loads), f32)] + [((loads, face), f32)] * 6,
        flags,
        across(along(sums)),
        pieces,
        spread,
        matrix,
        residual,
        name="project",
    )
    grams = lax.all_to_all(
        grams.reshape(plane, loads // plane, 2 * loads), PLANE, 0, 0, tiled=True
    ).sum(0)
    grams = to_all(grams, "gx").sum(0)
    grams = to_all(grams, PLANE).reshape(loads, 2 * loads)
    arrived = swap(outgoing)
    outputs = call(
        final_kernel,
        [faces, faces],
        flags,
        grams,
        multipliers,
        residual,
        projected,
        image,
        *arrived,
        name="final_update",
    )
    return tuple(out.reshape(1, 1, 1, 3, 2, loads, face) for out in outputs)


def solution(mesh):
    placed = (
        P("gx", "gy", "gz", None, None),
        P("gx", "gy", "gz", None, None, None, None),
        P(AXES, None),
        P("gx", "gy", "gz", None, None),
        P("gx", "gy", "gz", None, None, None, None),
    )

    return jax.shard_map(
        body,
        mesh=mesh,
        in_specs=placed,
        out_specs=(
            P("gx", "gy", "gz", None, None, None, None),
            P("gx", "gy", "gz", None, None, None, None),
        ),
        check_vma=False,
    )
```

time: 300 us -> 233 us (0.78)
  blocking collectives: 68.3 us -> 116 us
  local copies, waits for them, and re-layouts: 44.3 us -> 6.46 us
  starting transfers between devices: 100 us -> 62.3 us
  other arithmetic: 31.3 us -> 2.32 us
  Pallas kernels: 0 us -> 22.4 us
  waiting for transfers between devices: 38.9 us -> 21.7 us
  matrix products: 13.3 us -> 0 us
    all_to_all x2 -> x3, blocking collectives: 68.3 us -> 104 us  [to_all(): lax.all_to_all(jnp.broadcast_to(block[None], (lax.axis_size(axis),) + blo...]
    all_to_all x4 -> x3, starting transfers between devices: 44.2 us -> 18.8 us  [to_all(): lax.all_to_all(jnp.broadcast_to(block[None], (lax.axis_size(axis),) + blo...]
    pallas_call x0 -> x6, Pallas kernels: none -> 22.4 us  [call(): pl.pallas_call(kernel, out_shape=[jax.ShapeDtypeStruct(shape, kind) for s...]
    all_to_all x4 -> x3, waiting for transfers between devices: 35.2 us -> 17.5 us  [to_all(): lax.all_to_all(jnp.broadcast_to(block[None], (lax.axis_size(axis),) + blo...]
    another operation x9 -> x0, other arithmetic: 13.2 us -> none  [the longest x3 6.52 us: gram_solve(): factor = jnp.linalg.cholesky(matrix)]
    dot_general x20 -> x0, matrix products: 12.8 us -> none  [the longest x6 5.04 us: coarse(): jnp.dot(pieces[q], columns, preferred_element_type=jnp.float32)]
    all_to_all x0 -> x1, blocking collectives: none -> 11.7 us  [body(): lax.all_to_all(grams.reshape(plane, loads // plane, 2 * loads), PLANE, 0,...]
    concatenate x10 -> x0, local copies, waits for them, and re-layouts: 9.97 us -> none  [the longest x8 9.96 us: body(): jnp.concatenate([rows] + [a[:, :modes * parts] for a in arrived], axis=0)]
  transfers between devices with their start and end apart: 23 -> 21, of which waited for: 5 -> 5; matrix products, arithmetic and copies ran while one was open for 16% -> 0% of each run, Pallas kernels for 0% -> 2%
where the time goes in v3:
time: 233 us; the launch traced here: 232 us
  blocking collectives  116 us (50%)
  starting transfers between devices  62.3 us (27%)
  Pallas kernels  22.4 us (10%)
  waiting for transfers between devices  21.7 us (9%)
  local copies, waits for them, and re-layouts  6.46 us (3%)
    all_to_all x3, blocking collectives, to_all(): lax.all_to_all(jnp.broadcast_to(block[None], (lax.axis_size(axis),) + blo...  104 us
    ppermute x9, starting transfers between devices, swap(): arrived.append(lax.ppermute(outgoing[2 * d], axis, even))  28 us
    pallas_call x6, Pallas kernels, call(): pl.pallas_call(kernel, out_shape=[jax.ShapeDtypeStruct(shape, kind) for s...  22.4 us
    all_to_all x3, starting transfers between devices, to_all(): lax.all_to_all(jnp.broadcast_to(block[None], (lax.axis_size(axis),) + blo...  18.8 us
    all_to_all x3, waiting for transfers between devices, to_all(): lax.all_to_all(jnp.broadcast_to(block[None], (lax.axis_size(axis),) + blo...  17.5 us
    ppermute x9, starting transfers between devices, swap(): arrived.append(lax.ppermute(outgoing[2 * d + 1], axis, odd))  15.5 us
    all_to_all x1, blocking collectives, body(): lax.all_to_all(grams.reshape(plane, loads // plane, 2 * loads), PLANE, 0,...  11.7 us
  transfers between devices with their start and end apart: 21, of which 5 were waited for; matrix products, arithmetic and copies ran while one was open for 0% of the time, Pallas kernels for 2%

profile of v3, /device:TPU:1, one launch (start us, length us, event | category | flops | bytes accessed | tf_op | source)
XLA Modules:
  0.0 232.4 jit_solution(16863773721294041795)
XLA Ops:
  2.9 51.0 %all_to_all.35 = bf16[32,2,192]{2,1,0:T(2,128)(2,1)S(1)} all-to-all(bf16[32,2,192]{2,1,0:T(2,128)(2,1)S(1)} %reshape.48), channel_id=1, replica_groups=mesh['gx'=32,'gy'=8,'gz'=4] {'gx'}, dimensions={0} | all-to-all | bytes 49152 | tf_op jit(solution)/shard_map/all_to_all | solution.py:19
  54.1 1.0 broadcast_in_dim.40
  55.0 9.3 %all-to-all-start.1 = ((bf16[32,32,384]{2,1,0:T(8,128)(2,1)}), bf16[32,32,384]{2,1,0:T(8,128)(2,1)S(1)}, u32[]{:S(2)}, u32[]{:S(2)}) async-start(bf16[32,32,384]{2,1,0:T(8,128)(2,1)} %broadcast_in_dim.40), calls=%async_computation.1 | async-start | bytes 1572864 | tf_op jit(solution)/shard_map/all_to_all | solution.py:19
  64.5 3.2 %prepare_rows.1 = (f32[8,6272]{1,0:T(8,128)S(1)}, f32[8,6272]{1,0:T(8,128)S(1)}, f32[8,6272]{1,0:T(8,128)S(1)}, f32[8,6272]{1,0:T(8,128)S(1)}, f32[8,6272]{1,0:T(8,128)S(1)}, /*index=5*/f32[8,6272]{1,0:T(8,128)S(1)}) custom-call(s32[6]{0:T(128)S(1)} %stack.27.flags, f32[6,6144]{1,0:T(8,128)S(1)} %copy-done.4, f32[6,6,128]{2,1,0:T(8,128)S(1)} %bitcast.28), custom_call_target="tpu_custom_call" | custom-call | tf_op jit(solution)/shard_map/prepare_rows/pallas_call | solution.py:203
  67.7 2.2 collective-permute-start
  70.5 2.4 %collective-permute-start.2 = (f32[8,6272]{1,0:T(8,128)S(1)}, f32[8,6272]{1,0:T(8,128)S(1)}, u32[]{:S(2)}, u32[]{:S(2)}) collective-permute-start(f32[8,6272]{1,0:T(8,128)S(1)} %get-tuple-element.33), channel_id=1, source_target_pairs={{0,4},{4,0},{8,12},{12,8},{16,20},{20,16},{24,28},{28,24},{1,5},{5... | collective-permute-start | bytes 602120 | tf_op jit(solution)/shard_map/ppermute | solution.py:30
  73.0 3.3 %collective-permute-start.3 = (f32[8,6272]{1,0:T(8,128)S(1)}, f32[8,6272]{1,0:T(8,128)S(1)}, u32[]{:S(2)}, u32[]{:S(2)}) collective-permute-start(f32[8,6272]{1,0:T(8,128)S(1)} %get-tuple-element.34), channel_id=1, source_target_pairs={{4,8},{8,4},{12,16},{16,12},{20,24},{24,20},{5,9},{9,5},{13,17},{1... | collective-permute-start | bytes 602120 | tf_op jit(solution)/shard_map/ppermute | solution.py:31
  76.3 3.1 %collective-permute-start.4 = (f32[8,6272]{1,0:T(8,128)S(1)}, f32[8,6272]{1,0:T(8,128)S(1)}, u32[]{:S(2)}, u32[]{:S(2)}) collective-permute-start(f32[8,6272]{1,0:T(8,128)S(1)} %get-tuple-element.35), channel_id=1, source_target_pairs={{0,1},{1,0},{2,3},{3,2},{4,5},{5,4},{6,7},{7,6},{8,9},{9,8},{10,11... | collective-permute-start | bytes 602120 | tf_op jit(solution)/shard_map/ppermute | solution.py:30
  80.3 2.5 %collective-permute-done.4.refs_4_ = f32[8,6272]{1,0:T(8,128)S(1)} collective-permute-done((f32[8,6272]{1,0:T(8,128)S(1)}, f32[8,6272]{1,0:T(8,128)S(1)}, u32[]{:S(2)}, u32[]{:S(2)}) %collective-permute-start.4) | collective-permute-done | bytes 200736 | tf_op jit(solution)/shard_map/ppermute | solution.py:30
  82.8 0.9 build_rows.1
  83.7 1.3 copy-done.1
  85.0 1.6 copy-done.2
  86.6 3.6 %start_fields.1 = (f32[64,768]{1,0:T(8,128)S(1)}, f32[64,768]{1,0:T(8,128)S(1)}, f32[64,128]{1,0:T(8,128)S(1)}, f32[64,128]{1,0:T(8,128)S(1)}, f32[64,128]{1,0:T...) custom-call(s32[6]{0:T(128)S(1)} %stack.27.flags, ...), custom_call_target="tpu_custom_call" | custom-call | tf_op jit(solution)/shard_map/start_fields/pallas_call | solution.py:203
  90.1 6.5 %collective-permute-start.10 = (f32[64,128]{1,0:T(8,128)S(1)}, f32[64,128]{1,0:T(8,128)S(1)}, u32[]{:S(2)}, u32[]{:S(2)}) collective-permute-start(f32[64,128]{1,0:T(8,128)S(1)} %get-tuple-element.44), channel_id=1, source_target_pairs={{0,1},{1,0},{2,3},{3,2},{4,5},{5,4},{6,7},{7,6},{8,9},{9,8},{10,11... | collective-permute-start | bytes 98312 | tf_op jit(solution)/shard_map/ppermute | solution.py:30
  97.3 3.8 %collective-permute-start.6 = (f32[64,128]{1,0:T(8,128)S(1)}, f32[64,128]{1,0:T(8,128)S(1)}, u32[]{:S(2)}, u32[]{:S(2)}) collective-permute-start(f32[64,128]{1,0:T(8,128)S(1)} %get-tuple-element.40), channel_id=1, source_target_pairs={{0,32},{32,0},{64,96},{96,64},{128,160},{160,128},{192,224},{224,1... | collective-permute-start | bytes 98312 | tf_op jit(solution)/shard_map/ppermute | solution.py:30
  101.8 1.9 collective-permute-start.8
  103.7 6.1 %collective-permute-start.9 = (f32[64,128]{1,0:T(8,128)S(1)}, f32[64,128]{1,0:T(8,128)S(1)}, u32[]{:S(2)}, u32[]{:S(2)}) collective-permute-start(f32[64,128]{1,0:T(8,128)S(1)} %get-tuple-element.43), channel_id=1, source_target_pairs={{4,8},{8,4},{12,16},{16,12},{20,24},{24,20},{5,9},{9,5},{13,17},{1... | collective-permute-start | bytes 98312 | tf_op jit(solution)/shard_map/ppermute | solution.py:31
  109.8 1.5 collective-permute-done.9.refs_3_
  111.4 1.0 residual.1
  113.3 30.0 %all_to_all.36 = bf16[32,2,192]{2,1,0:T(2,128)(2,1)S(1)} all-to-all(bf16[32,2,192]{2,1,0:T(2,128)(2,1)S(1)} %reshape.50), channel_id=1, replica_groups=mesh['gx'=32,'gy'=8,'gz'=4] {'gx'}, dimensions={0} | all-to-all | bytes 49152 | tf_op jit(solution)/shard_map/all_to_all | solution.py:19
  143.5 23.3 %all_to_all.37 = bf16[32,32,384]{2,1,0:T(8,128)(2,1)S(1)} all-to-all(bf16[32,32,384]{2,1,0:T(8,128)(2,1)S(1)} %broadcast_in_dim.44), channel_id=1, replica_groups=mesh['gx'=32,'gy'=8,'gz'=4] {'gy','gz'}, dimensions={0} | all-to-all | bytes 1572864 | tf_op jit(solution)/shard_map/all_to_all | solution.py:19
  166.8 4.6 %project.1 = (f32[64,768]{1,0:T(8,128)S(1)}, f32[64,768]{1,0:T(8,128)S(1)}, f32[64,128]{1,0:T(8,128)S(1)}, f32[64,128]{1,0:T(8,128)}, f32[64,128]{1,0:T(8,128)},...) custom-call(s32[6]{0:T(128)S(1)} %stack.27.flags, ...), custom_call_target="tpu_custom_call" | custom-call | tf_op jit(solution)/shard_map/project/pallas_call | solution.py:203
  171.4 11.7 %all_to_all.38 = f32[32,2,128]{2,1,0:T(2,128)S(1)} all-to-all(f32[32,2,128]{2,1,0:T(2,128)S(1)} %bitcast.33), channel_id=1, replica_groups=mesh['gx'=32,'gy'=8,'gz'=4] {'gy','gz'}, dimensions={0} | all-to-all | bytes 65536 | tf_op jit(solution)/shard_map/all_to_all | solution.py:285
  183.8 3.8 %all-to-all-start.5 = ((f32[32,2,128]{2,1,0:T(2,128)}), f32[32,2,128]{2,1,0:T(2,128)S(1)}, u32[]{:S(2)}, u32[]{:S(2)}) async-start(f32[32,2,128]{2,1,0:T(2,128)} %broadcast_in_dim.45), calls=%async_computation.5 | async-start | bytes 65536 | tf_op jit(solution)/shard_map/all_to_all | solution.py:19
  187.6 3.0 %collective-permute-start.12 = (f32[64,128]{1,0:T(8,128)}, f32[64,128]{1,0:T(8,128)S(1)}, u32[]{:S(2)}, u32[]{:S(2)}) collective-permute-start(f32[64,128]{1,0:T(8,128)} %get-tuple-element.52), channel_id=1, source_target_pairs={{0,32},{32,0},{64,96},{96,64},{128,160},{160,128},{192,224},{224,1... | collective-permute-start | bytes 98312 | tf_op jit(solution)/shard_map/ppermute | solution.py:30
  191.3 2.9 %collective-permute-start.14 = (f32[64,128]{1,0:T(8,128)}, f32[64,128]{1,0:T(8,128)S(1)}, u32[]{:S(2)}, u32[]{:S(2)}) collective-permute-start(f32[64,128]{1,0:T(8,128)} %get-tuple-element.54), channel_id=1, source_target_pairs={{0,4},{4,0},{8,12},{12,8},{16,20},{20,16},{24,28},{28,24},{1,5},{5... | collective-permute-start | bytes 98312 | tf_op jit(solution)/shard_map/ppermute | solution.py:30
  194.2 2.1 collective-permute-start.15
  196.3 2.2 collective-permute-start.16
  199.2 10.3 %all-to-all-done.5 = f32[32,2,128]{2,1,0:T(2,128)S(1)} async-done(((f32[32,2,128]{2,1,0:T(2,128)}), f32[32,2,128]{2,1,0:T(2,128)S(1)}, u32[]{:S(2)}, u32[]{:S(2)}) %all-to-all-start.5) | async-done | bytes 32800 | tf_op jit(solution)/shard_map/all_to_all | solution.py:19
  210.2 5.7 %all-to-all-start.6 = ((f32[32,2,128]{2,1,0:T(2,128)}), f32[32,2,128]{2,1,0:T(2,128)S(1)}, u32[]{:S(2)}, u32[]{:S(2)}) async-start(f32[32,2,128]{2,1,0:T(2,128)} %broadcast_in_dim.46), calls=%async_computation.6 | async-start | bytes 65536 | tf_op jit(solution)/shard_map/all_to_all | solution.py:19
  215.9 7.3 %all-to-all-done.6 = f32[32,2,128]{2,1,0:T(2,128)S(1)} async-done(((f32[32,2,128]{2,1,0:T(2,128)}), f32[32,2,128]{2,1,0:T(2,128)S(1)}, u32[]{:S(2)}, u32[]{:S(2)}) %all-to-all-start.6) | async-done | bytes 32800 | tf_op jit(solution)/shard_map/all_to_all | solution.py:19
  223.2 9.2 %final_update.1 = (f32[6,64,128]{2,1,0:T(8,128)}, f32[6,64,128]{2,1,0:T(8,128)}) custom-call(s32[6]{0:T(128)S(1)} %stack.27.flags, f32[64,128]{1,0:T(8,128)S(1)} %bitcast.32, f32[64,768]{1,0:T(8,128)S(1)} %get-tuple-element.49.multipliers, f32[64,768]{1,0:T(8,128)S(1)} %get-tuple-element.47.residual, f32[64,768]{1,0:T(8,128)S(1)} %get-tuple-element.50.field, ...), custom_call_target="tpu_custom_call" | custom-call | tf_op jit(solution)/shard_map/final_update/pallas_call | solution.py:203
  (60 shorter events, 9.2 us)
Async XLA Ops:
  0.6 63.7 %copy-start.8 = (f32[1,1,1,6,3,2,128]{6,5,4,3,2,1,0:T(2,128)S(1)}, f32[1,1,1,6,3,2,128]{6,5,4,3,2,1,0:T(2,128)}, u32[]{:S(2)}) copy-start(f32[1,1,1,6,3,2,128]{6,5,4,3,2,1,0:T(2,128)} %param.6) | copy-start | bytes 55300
  0.6 63.8 %copy-start.4 = (f32[6,6144]{1,0:T(8,128)S(1)}, f32[6,6144]{1,0:T(8,128)}, u32[]{:S(2)}) copy-start(f32[6,6144]{1,0:T(8,128)} %rows.1) | copy-start | bytes 442372
  0.7 84.3 %copy-start = (f32[1,1,1,768,768]{4,3,2,1,0:T(8,128)S(1)}, f32[1,1,1,768,768]{4,3,2,1,0:T(8,128)}, u32[]{:S(2)}) copy-start(f32[1,1,1,768,768]{4,3,2,1,0:T(8,128)} %param.5) | copy-start | bytes 7077892
  55.0 30.0 %all-to-all-start.1 = ((bf16[32,32,384]{2,1,0:T(8,128)(2,1)}), bf16[32,32,384]{2,1,0:T(8,128)(2,1)S(1)}, u32[]{:S(2)}, u32[]{:S(2)}) async-start(bf16[32,32,384]{2,1,0:T(8,128)(2,1)} %broadcast_in_dim.40), calls=%async_computation.1 | async-start | bytes 1572864 | tf_op jit(solution)/shard_map/all_to_all | solution.py:19
  67.7 11.7 %collective-permute-start = (f32[8,6272]{1,0:T(8,128)S(1)}, f32[8,6272]{1,0:T(8,128)S(1)}, u32[]{:S(2)}, u32[]{:S(2)}) collective-permute-start(f32[8,6272]{1,0:T(8,128)S(1)} %get-tuple-element.31.own), channel_id=1, source_target_pairs={{0,32},{32,0},{64,96},{96,64},{128,160},{160,128},{192,224},{224,1... | collective-permute-start | bytes 602120 | tf_op jit(solution)/shard_map/ppermute | solution.py:30
  69.9 10.2 %collective-permute-start.1 = (f32[8,6272]{1,0:T(8,128)S(1)}, f32[8,6272]{1,0:T(8,128)S(1)}, u32[]{:S(2)}, u32[]{:S(2)}) collective-permute-start(f32[8,6272]{1,0:T(8,128)S(1)} %get-tuple-element.32), channel_id=1, source_target_pairs={{32,64},{64,32},{96,128},{128,96},{160,192},{192,160},{224,256},{2... | collective-permute-start | bytes 602120 | tf_op jit(solution)/shard_map/ppermute | solution.py:31
  70.5 9.6 %collective-permute-start.2 = (f32[8,6272]{1,0:T(8,128)S(1)}, f32[8,6272]{1,0:T(8,128)S(1)}, u32[]{:S(2)}, u32[]{:S(2)}) collective-permute-start(f32[8,6272]{1,0:T(8,128)S(1)} %get-tuple-element.33), channel_id=1, source_target_pairs={{0,4},{4,0},{8,12},{12,8},{16,20},{20,16},{24,28},{28,24},{1,5},{5... | collective-permute-start | bytes 602120 | tf_op jit(solution)/shard_map/ppermute | solution.py:30
  73.0 7.3 %collective-permute-start.3 = (f32[8,6272]{1,0:T(8,128)S(1)}, f32[8,6272]{1,0:T(8,128)S(1)}, u32[]{:S(2)}, u32[]{:S(2)}) collective-permute-start(f32[8,6272]{1,0:T(8,128)S(1)} %get-tuple-element.34), channel_id=1, source_target_pairs={{4,8},{8,4},{12,16},{16,12},{20,24},{24,20},{5,9},{9,5},{13,17},{1... | collective-permute-start | bytes 602120 | tf_op jit(solution)/shard_map/ppermute | solution.py:31
  76.3 6.5 %collective-permute-start.4 = (f32[8,6272]{1,0:T(8,128)S(1)}, f32[8,6272]{1,0:T(8,128)S(1)}, u32[]{:S(2)}, u32[]{:S(2)}) collective-permute-start(f32[8,6272]{1,0:T(8,128)S(1)} %get-tuple-element.35), channel_id=1, source_target_pairs={{0,1},{1,0},{2,3},{3,2},{4,5},{5,4},{6,7},{7,6},{8,9},{9,8},{10,11... | collective-permute-start | bytes 602120 | tf_op jit(solution)/shard_map/ppermute | solution.py:30
  79.4 3.4 %collective-permute-start.5 = (f32[8,6272]{1,0:T(8,128)S(1)}, f32[8,6272]{1,0:T(8,128)S(1)}, u32[]{:S(2)}, u32[]{:S(2)}) collective-permute-start(f32[8,6272]{1,0:T(8,128)S(1)} %get-tuple-element.36), channel_id=1, source_target_pairs={{1,2},{2,1},{5,6},{6,5},{9,10},{10,9},{13,14},{14,13},{17,18},{18,... | collective-permute-start | bytes 602120 | tf_op jit(solution)/shard_map/ppermute | solution.py:31
  83.7 1.3 copy-start.1
  85.0 1.6 copy-start.2
  86.6 24.8 %copy-start.5 = (f32[1,1,1,3,2,64,128]{6,5,4,3,2,1,0:T(8,128)S(1)}, f32[1,1,1,3,2,64,128]{6,5,4,3,2,1,0:T(8,128)}, u32[]{:S(2)}) copy-start(f32[1,1,1,3,2,64,128]{6,5,4,3,2,1,0:T(8,128)} %param.9) | copy-start | bytes 589828
  90.1 13.6 %collective-permute-start.10 = (f32[64,128]{1,0:T(8,128)S(1)}, f32[64,128]{1,0:T(8,128)S(1)}, u32[]{:S(2)}, u32[]{:S(2)}) collective-permute-start(f32[64,128]{1,0:T(8,128)S(1)} %get-tuple-element.44), channel_id=1, source_target_pairs={{0,1},{1,0},{2,3},{3,2},{4,5},{5,4},{6,7},{7,6},{8,9},{9,8},{10,11... | collective-permute-start | bytes 98312 | tf_op jit(solution)/shard_map/ppermute | solution.py:30
  96.7 13.1 %collective-permute-start.11 = (f32[64,128]{1,0:T(8,128)S(1)}, f32[64,128]{1,0:T(8,128)S(1)}, u32[]{:S(2)}, u32[]{:S(2)}) collective-permute-start(f32[64,128]{1,0:T(8,128)S(1)} %get-tuple-element.45), channel_id=1, source_target_pairs={{1,2},{2,1},{5,6},{6,5},{9,10},{10,9},{13,14},{14,13},{17,18},{18,... | collective-permute-start | bytes 98312 | tf_op jit(solution)/shard_map/ppermute | solution.py:31
  97.3 12.5 %collective-permute-start.6 = (f32[64,128]{1,0:T(8,128)S(1)}, f32[64,128]{1,0:T(8,128)S(1)}, u32[]{:S(2)}, u32[]{:S(2)}) collective-permute-start(f32[64,128]{1,0:T(8,128)S(1)} %get-tuple-element.40), channel_id=1, source_target_pairs={{0,32},{32,0},{64,96},{96,64},{128,160},{160,128},{192,224},{224,1... | collective-permute-start | bytes 98312 | tf_op jit(solution)/shard_map/ppermute | solution.py:30
  101.1 8.7 %collective-permute-start.7 = (f32[64,128]{1,0:T(8,128)S(1)}, f32[64,128]{1,0:T(8,128)S(1)}, u32[]{:S(2)}, u32[]{:S(2)}) collective-permute-start(f32[64,128]{1,0:T(8,128)S(1)} %get-tuple-element.41), channel_id=1, source_target_pairs={{32,64},{64,32},{96,128},{128,96},{160,192},{192,160},{224,256},{2... | collective-permute-start | bytes 98312 | tf_op jit(solution)/shard_map/ppermute | solution.py:31
  101.8 8.1 %collective-permute-start.8 = (f32[64,128]{1,0:T(8,128)S(1)}, f32[64,128]{1,0:T(8,128)S(1)}, u32[]{:S(2)}, u32[]{:S(2)}) collective-permute-start(f32[64,128]{1,0:T(8,128)S(1)} %get-tuple-element.42), channel_id=1, source_target_pairs={{0,4},{4,0},{8,12},{12,8},{16,20},{20,16},{24,28},{28,24},{1,5},{5... | collective-permute-start | bytes 98312 | tf_op jit(solution)/shard_map/ppermute | solution.py:30
  103.7 7.7 %collective-permute-start.9 = (f32[64,128]{1,0:T(8,128)S(1)}, f32[64,128]{1,0:T(8,128)S(1)}, u32[]{:S(2)}, u32[]{:S(2)}) collective-permute-start(f32[64,128]{1,0:T(8,128)S(1)} %get-tuple-element.43), channel_id=1, source_target_pairs={{4,8},{8,4},{12,16},{16,12},{20,24},{24,20},{5,9},{9,5},{13,17},{1... | collective-permute-start | bytes 98312 | tf_op jit(solution)/shard_map/ppermute | solution.py:31
  143.4 23.4 %copy-start.3 = (bf16[3,336,1024]{2,1,0:T(8,128)(2,1)S(1)}, bf16[3,336,1024]{2,1,0:T(8,128)(2,1)}, u32[]{:S(2)}) copy-start(bf16[3,336,1024]{2,1,0:T(8,128)(2,1)} %copy-done.1) | copy-start | bytes 6193156
  171.4 16.2 %copy-start.6 = (f32[64,128]{1,0:T(8,128)}, f32[64,128]{1,0:T(8,128)S(1)}, u32[]{:S(2)}) copy-start(f32[64,128]{1,0:T(8,128)S(1)} %get-tuple-element.57) | copy-start | bytes 98308
  171.4 19.3 %copy-start.7 = (f32[64,128]{1,0:T(8,128)}, f32[64,128]{1,0:T(8,128)S(1)}, u32[]{:S(2)}) copy-start(f32[64,128]{1,0:T(8,128)S(1)} %get-tuple-element.56) | copy-start | bytes 98308
  183.8 25.7 %all-to-all-start.5 = ((f32[32,2,128]{2,1,0:T(2,128)}), f32[32,2,128]{2,1,0:T(2,128)S(1)}, u32[]{:S(2)}, u32[]{:S(2)}) async-start(f32[32,2,128]{2,1,0:T(2,128)} %broadcast_in_dim.45), calls=%async_computation.5 | async-start | bytes 65536 | tf_op jit(solution)/shard_map/all_to_all | solution.py:19
  187.6 10.9 %collective-permute-start.12 = (f32[64,128]{1,0:T(8,128)}, f32[64,128]{1,0:T(8,128)S(1)}, u32[]{:S(2)}, u32[]{:S(2)}) collective-permute-start(f32[64,128]{1,0:T(8,128)} %get-tuple-element.52), channel_id=1, source_target_pairs={{0,32},{32,0},{64,96},{96,64},{128,160},{160,128},{192,224},{224,1... | collective-permute-start | bytes 98312 | tf_op jit(solution)/shard_map/ppermute | solution.py:30
  190.7 25.2 %collective-permute-start.13 = (f32[64,128]{1,0:T(8,128)}, f32[64,128]{1,0:T(8,128)S(1)}, u32[]{:S(2)}, u32[]{:S(2)}) collective-permute-start(f32[64,128]{1,0:T(8,128)} %get-tuple-element.53), channel_id=1, source_target_pairs={{32,64},{64,32},{96,128},{128,96},{160,192},{192,160},{224,256},{2... | collective-permute-start | bytes 98312 | tf_op jit(solution)/shard_map/ppermute | solution.py:31
  191.3 24.6 %collective-permute-start.14 = (f32[64,128]{1,0:T(8,128)}, f32[64,128]{1,0:T(8,128)S(1)}, u32[]{:S(2)}, u32[]{:S(2)}) collective-permute-start(f32[64,128]{1,0:T(8,128)} %get-tuple-element.54), channel_id=1, source_target_pairs={{0,4},{4,0},{8,12},{12,8},{16,20},{20,16},{24,28},{28,24},{1,5},{5... | collective-permute-start | bytes 98312 | tf_op jit(solution)/shard_map/ppermute | solution.py:30
  194.2 21.7 %collective-permute-start.15 = (f32[64,128]{1,0:T(8,128)}, f32[64,128]{1,0:T(8,128)S(1)}, u32[]{:S(2)}, u32[]{:S(2)}) collective-permute-start(f32[64,128]{1,0:T(8,128)} %get-tuple-element.55), channel_id=1, source_target_pairs={{4,8},{8,4},{12,16},{16,12},{20,24},{24,20},{5,9},{9,5},{13,17},{1... | collective-permute-start | bytes 98312 | tf_op jit(solution)/shard_map/ppermute | solution.py:31
  196.3 19.6 %collective-permute-start.16 = (f32[64,128]{1,0:T(8,128)}, f32[64,128]{1,0:T(8,128)S(1)}, u32[]{:S(2)}, u32[]{:S(2)}) collective-permute-start(f32[64,128]{1,0:T(8,128)} %copy-done.7), channel_id=1, source_target_pairs={{0,1},{1,0},{2,3},{3,2},{4,5},{5,4},{6,7},{7,6},{8,9},{9,8},{10,11... | collective-permute-start | bytes 98312 | tf_op jit(solution)/shard_map/ppermute | solution.py:30
  198.6 17.4 %collective-permute-start.17 = (f32[64,128]{1,0:T(8,128)}, f32[64,128]{1,0:T(8,128)S(1)}, u32[]{:S(2)}, u32[]{:S(2)}) collective-permute-start(f32[64,128]{1,0:T(8,128)} %copy-done.6), channel_id=1, source_target_pairs={{1,2},{2,1},{5,6},{6,5},{9,10},{10,9},{13,14},{14,13},{17,18},{18,... | collective-permute-start | bytes 98312 | tf_op jit(solution)/shard_map/ppermute | solution.py:31
  210.2 13.0 %all-to-all-start.6 = ((f32[32,2,128]{2,1,0:T(2,128)}), f32[32,2,128]{2,1,0:T(2,128)S(1)}, u32[]{:S(2)}, u32[]{:S(2)}) async-start(f32[32,2,128]{2,1,0:T(2,128)} %broadcast_in_dim.46), calls=%async_computation.6 | async-start | bytes 65536 | tf_op jit(solution)/shard_map/all_to_all | solution.py:19

commit v4 on v3

--- a/solution.py
+++ b/solution.py
@@ -21,9 +21,9 @@
     )
 
 
-def swap(outgoing):
+def swap(outgoing, axes=AXES):
     arrived = []
-    for d, axis in enumerate(AXES):
+    for d, axis in enumerate(axes):
         size = lax.axis_size(axis)
         even = [(i, i ^ 1) for i in range(size)]
         odd = [(i, i + 1 if i % 2 else i - 1) for i in range(1, size - 1)]
@@ -131,6 +131,24 @@
     return jnp.where(flags[3 + d] > 0, value, 0.0) if f % 2 == 0 else value
 
 
+def as_rows(sums, out):
+    modes, loads = sums.shape
+    rows = [jnp.concatenate([sums[m : m + 1], sums[m + 1 : m + 2]], axis=1) for m in range(0, modes, 2)]
+    rows = jnp.concatenate(rows + [jnp.zeros((1, 2 * loads), f32)], axis=0)
+    out[...] = jnp.broadcast_to(rows[None], out.shape).astype(bf16)
+
+
+def modes_kernel(flags, right_side, out):
+    as_rows(right_side[...], out)
+
+
+def widen_kernel(flags, column, out):
+    value = column[...].astype(f32)
+    wide = jnp.concatenate([value[:, q, :] for q in range(value.shape[1] - 1)], axis=1).astype(bf16)
+    for p in range(out.shape[0]):
+        out[p] = wide
+
+
 def start_kernel(flags, stacked, pieces, spread, matrix, field, image, *outgoing):
     value = coarse(stacked, pieces, spread)
     field[...] = value
@@ -147,7 +165,7 @@
         total = total + lax.dot_general(
             traces[f], value, (((1,), (1,)), ((), ())), precision=HIGHEST, preferred_element_type=f32
         )
-    sums[...] = total.astype(bf16)
+    as_rows(total, sums)
 
 
 def project_kernel(flags, stacked, pieces, spread, matrix, residual, field, image, grams, *outgoing):
@@ -170,17 +188,19 @@
 def solve(table):
     size = table.shape[0]
     row = lax.broadcasted_iota(jnp.int32, table.shape, 0)
-    for k in range(0, size, 2):
-        first, second = table[k : k + 1, :], table[k + 1 : k + 2, :]
-        left, right = table[:, k : k + 1], table[:, k + 1 : k + 2]
-        inverse = 1.0 / left[k : k + 1]
-        ratio = left[k + 1 : k + 2] * inverse
-        corner = 1.0 / (right[k + 1 : k + 2] - ratio * right[k : k + 1])
-        lower = (second - ratio * first) * corner
-        upper = (first - right[k : k + 1] * lower) * inverse
-        table = jnp.where(
-            row == k, upper, jnp.where(row == k + 1, lower, table - left * upper - right * lower)
-        )
+    for begin in range(0, size, 4):
+        columns = [
+            jnp.broadcast_to(table[:, k : k + 1], table.shape) for k in range(begin, begin + 4)
+        ]
+        for i in range(4):
+            k = begin + i
+            column = columns[i]
+            inverse = 1.0 / column[k : k + 1]
+            pivot = table[k : k + 1] * inverse
+            table = jnp.where(row == k, pivot, table - column * pivot)
+            for j in range(i + 1, 4):
+                pivot = columns[j][k : k + 1] * inverse
+                columns[j] = jnp.where(row == k, pivot, columns[j] - column * pivot)
     return table[:, size:]
 
 
@@ -223,13 +243,18 @@
     wide, faces = ((loads, 6 * face), f32), ((6, loads, face), f32)
     packs = ((8, modes * parts + face), f32)
 
-    def along(sums):
-        return to_all(sums.astype(bf16).reshape(1, modes * loads), "gx").reshape(long, modes * loads)
+    row = ((long, modes // 2 + 1, 2 * loads), bf16)
+
+    def along(rows):
+        return lax.all_to_all(rows, "gx", 0, 0, tiled=True)
 
     def across(column):
-        return to_all(column, PLANE).reshape(parts, modes * loads)
-
-    column = along(coarse_rhs[0, 0, 0])
+        column = call(
+            widen_kernel, [((plane, long, modes * loads), bf16)], flags, column, name="widen"
+        )[0]
+        return lax.all_to_all(column, PLANE, 0, 0, tiled=True).reshape(parts, modes * loads)
+
+    column = along(call(modes_kernel, [row], flags, coarse_rhs[0, 0, 0], name="modes")[0])
     packed = call(
         functools.partial(prepare, modes, long, plane),
         [packs] * 6,
@@ -239,7 +264,8 @@
         scratch_shapes=[pltpu.VMEM((modes * parts, 8), f32)],
         name="prepare_rows",
     )
-    arrived = swap(packed)
+    in_plane = swap(packed[2:], PLANE)
+    arrived = swap(packed[:2], AXES[:1]) + in_plane
     stacked = across(column)
     pieces, spread = call(
         functools.partial(build, modes, parts),
@@ -263,7 +289,7 @@
     )
     residual, sums = call(
         residual_kernel,
-        [wide, ((modes, loads), bf16)],
+        [wide, row],
         flags,
         gaps,
         traces,

time: 233 us -> 227 us (0.974)
    all_to_all x3 -> x2, starting transfers between devices: 18.8 us -> 9.21 us  [to_all(): lax.all_to_all(jnp.broadcast_to(block[None], (lax.axis_size(axis),) + blo...]
    all_to_all x0 -> x1, starting transfers between devices: none -> 9.29 us  [across(): lax.all_to_all(column, PLANE, 0, 0, tiled=True)]
    pallas_call x6 -> x9, Pallas kernels: 22.4 us -> 20.2 us  [call(): pl.pallas_call(kernel, out_shape=[jax.ShapeDtypeStruct(shape, kind) for s...]
    all_to_all x3 -> x2, waiting for transfers between devices: 17.5 us -> 17.8 us  [to_all(): lax.all_to_all(jnp.broadcast_to(block[None], (lax.axis_size(axis),) + blo...]
where the time goes in v4:
time: 227 us
  blocking collectives  116 us (51%)
  starting transfers between devices  62.1 us (27%)
  waiting for transfers between devices  22.1 us (10%)
  Pallas kernels  20.2 us (9%)
  local copies, waits for them, and re-layouts  5.11 us (2%)
    all_to_all x2, blocking collectives, along(): return lax.all_to_all(rows, 'gx', 0, 0, tiled=True)  81 us
    ppermute x9, starting transfers between devices, swap(): arrived.append(lax.ppermute(outgoing[2 * d], axis, even))  28.1 us
    all_to_all x1, blocking collectives, across(): lax.all_to_all(column, PLANE, 0, 0, tiled=True)  23.2 us
    pallas_call x9, Pallas kernels, call(): pl.pallas_call(kernel, out_shape=[jax.ShapeDtypeStruct(shape, kind) for s...  20.2 us
    all_to_all x2, waiting for transfers between devices, to_all(): lax.all_to_all(jnp.broadcast_to(block[None], (lax.axis_size(axis),) + blo...  17.8 us
    ppermute x9, starting transfers between devices, swap(): arrived.append(lax.ppermute(outgoing[2 * d + 1], axis, odd))  15.5 us
    all_to_all x1, blocking collectives, body(): lax.all_to_all(grams.reshape(plane, loads // plane, 2 * loads), PLANE, 0,...  11.7 us
    all_to_all x1, starting transfers between devices, across(): lax.all_to_all(column, PLANE, 0, 0, tiled=True)  9.29 us
  transfers between devices with their start and end apart: 21, of which 5 were waited for; matrix products, arithmetic and copies ran while one was open for 0% of the time, Pallas kernels for 2%

profile of v4, /device:TPU:1, one launch (start us, length us, event | category | flops | bytes accessed | tf_op | source)
XLA Modules:
  0.0 226.5 jit_solution(17090614285827668404)
XLA Ops:
  2.2 51.0 %all_to_all.35.column = bf16[32,4,128]{2,1,0:T(4,128)(2,1)S(1)} all-to-all(bf16[32,4,128]{2,1,0:T(4,128)(2,1)S(1)} %modes.1), channel_id=1, replica_groups=mesh['gx'=32,'gy'=8,'gz'=4] {'gx'}, dimensions={0} | all-to-all | bytes 65536 | tf_op jit(solution)/shard_map/all_to_all | solution.py:249
  53.2 1.5 widen.2
  54.7 9.3 %all-to-all-start.1 = ((bf16[32,32,384]{2,1,0:T(8,128)(2,1)}), bf16[32,32,384]{2,1,0:T(8,128)(2,1)S(1)}, u32[]{:S(2)}, u32[]{:S(2)}) async-start(bf16[32,32,384]{2,1,0:T(8,128)(2,1)} %widen.2), calls=%async_computation.1 | async-start | bytes 1572864 | tf_op jit(solution)/shard_map/all_to_all | solution.py:255
  64.1 3.2 %prepare_rows.1 = (f32[8,6272]{1,0:T(8,128)S(1)}, f32[8,6272]{1,0:T(8,128)S(1)}, f32[8,6272]{1,0:T(8,128)S(1)}, f32[8,6272]{1,0:T(8,128)S(1)}, f32[8,6272]{1,0:T(8,128)S(1)}, /*index=5*/f32[8,6272]{1,0:T(8,128)S(1)}) custom-call(s32[6]{0:T(128)S(1)} %stack.27.flags, f32[6,6144]{1,0:T(8,128)S(1)} %copy-done.4, f32[6,6,128]{2,1,0:T(8,128)S(1)} %bitcast.25), custom_call_target="tpu_custom_call" | custom-call | tf_op jit(solution)/shard_map/prepare_rows/pallas_call | solution.py:223
  67.3 2.2 collective-permute-start
  70.1 2.4 %collective-permute-start.2 = (f32[8,6272]{1,0:T(8,128)S(1)}, f32[8,6272]{1,0:T(8,128)S(1)}, u32[]{:S(2)}, u32[]{:S(2)}) collective-permute-start(f32[8,6272]{1,0:T(8,128)S(1)} %get-tuple-element.33), channel_id=1, source_target_pairs={{0,4},{4,0},{8,12},{12,8},{16,20},{20,16},{24,28},{28,24},{1,5},{5... | collective-permute-start | bytes 602120 | tf_op jit(solution)/shard_map/ppermute | solution.py:30
  72.6 3.3 %collective-permute-start.3 = (f32[8,6272]{1,0:T(8,128)S(1)}, f32[8,6272]{1,0:T(8,128)S(1)}, u32[]{:S(2)}, u32[]{:S(2)}) collective-permute-start(f32[8,6272]{1,0:T(8,128)S(1)} %get-tuple-element.34), channel_id=1, source_target_pairs={{4,8},{8,4},{12,16},{16,12},{20,24},{24,20},{5,9},{9,5},{13,17},{1... | collective-permute-start | bytes 602120 | tf_op jit(solution)/shard_map/ppermute | solution.py:31
  75.9 3.1 %collective-permute-start.4 = (f32[8,6272]{1,0:T(8,128)S(1)}, f32[8,6272]{1,0:T(8,128)S(1)}, u32[]{:S(2)}, u32[]{:S(2)}) collective-permute-start(f32[8,6272]{1,0:T(8,128)S(1)} %get-tuple-element.35), channel_id=1, source_target_pairs={{0,1},{1,0},{2,3},{3,2},{4,5},{5,4},{6,7},{7,6},{8,9},{9,8},{10,11... | collective-permute-start | bytes 602120 | tf_op jit(solution)/shard_map/ppermute | solution.py:30
  79.9 2.5 %collective-permute-done.4.refs_4_ = f32[8,6272]{1,0:T(8,128)S(1)} collective-permute-done((f32[8,6272]{1,0:T(8,128)S(1)}, f32[8,6272]{1,0:T(8,128)S(1)}, u32[]{:S(2)}, u32[]{:S(2)}) %collective-permute-start.4) | collective-permute-done | bytes 200736 | tf_op jit(solution)/shard_map/ppermute | solution.py:30
  82.4 0.9 build_rows.1
  83.3 1.3 copy-done.1
  84.6 1.6 copy-done.2
  86.2 3.6 %start_fields.1 = (f32[64,768]{1,0:T(8,128)S(1)}, f32[64,768]{1,0:T(8,128)S(1)}, f32[64,128]{1,0:T(8,128)S(1)}, f32[64,128]{1,0:T(8,128)S(1)}, f32[64,128]{1,0:T...) custom-call(s32[6]{0:T(128)S(1)} %stack.27.flags, ...), custom_call_target="tpu_custom_call" | custom-call | tf_op jit(solution)/shard_map/start_fields/pallas_call | solution.py:223
  89.8 6.7 %collective-permute-start.10 = (f32[64,128]{1,0:T(8,128)S(1)}, f32[64,128]{1,0:T(8,128)S(1)}, u32[]{:S(2)}, u32[]{:S(2)}) collective-permute-start(f32[64,128]{1,0:T(8,128)S(1)} %get-tuple-element.44), channel_id=1, source_target_pairs={{0,1},{1,0},{2,3},{3,2},{4,5},{5,4},{6,7},{7,6},{8,9},{9,8},{10,11... | collective-permute-start | bytes 98312 | tf_op jit(solution)/shard_map/ppermute | solution.py:30
  97.1 3.8 %collective-permute-start.6 = (f32[64,128]{1,0:T(8,128)S(1)}, f32[64,128]{1,0:T(8,128)S(1)}, u32[]{:S(2)}, u32[]{:S(2)}) collective-permute-start(f32[64,128]{1,0:T(8,128)S(1)} %get-tuple-element.40), channel_id=1, source_target_pairs={{0,32},{32,0},{64,96},{96,64},{128,160},{160,128},{192,224},{224,1... | collective-permute-start | bytes 98312 | tf_op jit(solution)/shard_map/ppermute | solution.py:30
  101.5 1.9 collective-permute-start.8
  103.5 6.1 %collective-permute-start.9 = (f32[64,128]{1,0:T(8,128)S(1)}, f32[64,128]{1,0:T(8,128)S(1)}, u32[]{:S(2)}, u32[]{:S(2)}) collective-permute-start(f32[64,128]{1,0:T(8,128)S(1)} %get-tuple-element.43), channel_id=1, source_target_pairs={{4,8},{8,4},{12,16},{16,12},{20,24},{24,20},{5,9},{9,5},{13,17},{1... | collective-permute-start | bytes 98312 | tf_op jit(solution)/shard_map/ppermute | solution.py:31
  109.6 1.5 collective-permute-done.9.refs_3_
  111.2 1.0 residual.1
  112.2 30.0 %all_to_all.36.column = bf16[32,4,128]{2,1,0:T(4,128)(2,1)S(1)} all-to-all(bf16[32,4,128]{2,1,0:T(4,128)(2,1)S(1)} %get-tuple-element.46), channel_id=1, replica_groups=mesh['gx'=32,'gy'=8,'gz'=4] {'gx'}, dimensions={0} | all-to-all | bytes 65536 | tf_op jit(solution)/shard_map/all_to_all | solution.py:249
  142.8 23.2 %all_to_all.37 = bf16[32,32,384]{2,1,0:T(8,128)(2,1)S(1)} all-to-all(bf16[32,32,384]{2,1,0:T(8,128)(2,1)S(1)} %widen.3), channel_id=1, replica_groups=mesh['gx'=32,'gy'=8,'gz'=4] {'gy','gz'}, dimensions={0} | all-to-all | bytes 1572864 | tf_op jit(solution)/shard_map/all_to_all | solution.py:255
  166.0 4.6 %project.1 = (f32[64,768]{1,0:T(8,128)S(1)}, f32[64,768]{1,0:T(8,128)S(1)}, f32[64,128]{1,0:T(8,128)S(1)}, f32[64,128]{1,0:T(8,128)}, f32[64,128]{1,0:T(8,128)},...) custom-call(s32[6]{0:T(128)S(1)} %stack.27.flags, ...), custom_call_target="tpu_custom_call" | custom-call | tf_op jit(solution)/shard_map/project/pallas_call | solution.py:223
  170.6 11.7 %all_to_all.38 = f32[32,2,128]{2,1,0:T(2,128)S(1)} all-to-all(f32[32,2,128]{2,1,0:T(2,128)S(1)} %bitcast.30), channel_id=1, replica_groups=mesh['gx'=32,'gy'=8,'gz'=4] {'gy','gz'}, dimensions={0} | all-to-all | bytes 65536 | tf_op jit(solution)/shard_map/all_to_all | solution.py:311
  183.0 3.8 %all-to-all-start.5 = ((f32[32,2,128]{2,1,0:T(2,128)}), f32[32,2,128]{2,1,0:T(2,128)S(1)}, u32[]{:S(2)}, u32[]{:S(2)}) async-start(f32[32,2,128]{2,1,0:T(2,128)} %broadcast_in_dim.4), calls=%async_computation.5 | async-start | bytes 65536 | tf_op jit(solution)/shard_map/all_to_all | solution.py:19
  186.8 3.0 %collective-permute-start.12 = (f32[64,128]{1,0:T(8,128)}, f32[64,128]{1,0:T(8,128)S(1)}, u32[]{:S(2)}, u32[]{:S(2)}) collective-permute-start(f32[64,128]{1,0:T(8,128)} %get-tuple-element.52), channel_id=1, source_target_pairs={{0,32},{32,0},{64,96},{96,64},{128,160},{160,128},{192,224},{224,1... | collective-permute-start | bytes 98312 | tf_op jit(solution)/shard_map/ppermute | solution.py:30
  190.5 2.9 %collective-permute-start.14 = (f32[64,128]{1,0:T(8,128)}, f32[64,128]{1,0:T(8,128)S(1)}, u32[]{:S(2)}, u32[]{:S(2)}) collective-permute-start(f32[64,128]{1,0:T(8,128)} %get-tuple-element.54), channel_id=1, source_target_pairs={{0,4},{4,0},{8,12},{12,8},{16,20},{20,16},{24,28},{28,24},{1,5},{5... | collective-permute-start | bytes 98312 | tf_op jit(solution)/shard_map/ppermute | solution.py:30
  193.4 2.1 collective-permute-start.15
  195.5 2.2 collective-permute-start.16
  198.4 10.6 %all-to-all-done.5 = f32[32,2,128]{2,1,0:T(2,128)S(1)} async-done(((f32[32,2,128]{2,1,0:T(2,128)}), f32[32,2,128]{2,1,0:T(2,128)S(1)}, u32[]{:S(2)}, u32[]{:S(2)}) %all-to-all-start.5) | async-done | bytes 32800 | tf_op jit(solution)/shard_map/all_to_all | solution.py:19
  209.7 5.4 %all-to-all-start.6 = ((f32[32,2,128]{2,1,0:T(2,128)}), f32[32,2,128]{2,1,0:T(2,128)S(1)}, u32[]{:S(2)}, u32[]{:S(2)}) async-start(f32[32,2,128]{2,1,0:T(2,128)} %broadcast_in_dim.5), calls=%async_computation.6 | async-start | bytes 65536 | tf_op jit(solution)/shard_map/all_to_all | solution.py:19
  215.1 7.3 %all-to-all-done.6 = f32[32,2,128]{2,1,0:T(2,128)S(1)} async-done(((f32[32,2,128]{2,1,0:T(2,128)}), f32[32,2,128]{2,1,0:T(2,128)S(1)}, u32[]{:S(2)}, u32[]{:S(2)}) %all-to-all-start.6) | async-done | bytes 32800 | tf_op jit(solution)/shard_map/all_to_all | solution.py:19
  222.4 4.1 %final_update.1 = (f32[6,64,128]{2,1,0:T(8,128)}, f32[6,64,128]{2,1,0:T(8,128)}) custom-call(s32[6]{0:T(128)S(1)} %stack.27.flags, f32[64,128]{1,0:T(8,128)S(1)} %bitcast.29, f32[64,768]{1,0:T(8,128)S(1)} %get-tuple-element.49.multipliers, f32[64,768]{1,0:T(8,128)S(1)} %get-tuple-element.47.residual, f32[64,768]{1,0:T(8,128)S(1)} %get-tuple-element.50.field, ...), custom_call_target="tpu_custom_call" | custom-call | tf_op jit(solution)/shard_map/final_update/pallas_call | solution.py:223
  (48 shorter events, 7.8 us)
Async XLA Ops:
  0.6 63.4 %copy-start.8 = (f32[1,1,1,6,3,2,128]{6,5,4,3,2,1,0:T(2,128)S(1)}, f32[1,1,1,6,3,2,128]{6,5,4,3,2,1,0:T(2,128)}, u32[]{:S(2)}) copy-start(f32[1,1,1,6,3,2,128]{6,5,4,3,2,1,0:T(2,128)} %param.6) | copy-start | bytes 55300
  0.6 63.4 %copy-start.4 = (f32[6,6144]{1,0:T(8,128)S(1)}, f32[6,6144]{1,0:T(8,128)}, u32[]{:S(2)}) copy-start(f32[6,6144]{1,0:T(8,128)} %rows.1) | copy-start | bytes 442372
  0.7 84.0 %copy-start = (f32[1,1,1,768,768]{4,3,2,1,0:T(8,128)S(1)}, f32[1,1,1,768,768]{4,3,2,1,0:T(8,128)}, u32[]{:S(2)}) copy-start(f32[1,1,1,768,768]{4,3,2,1,0:T(8,128)} %param.5) | copy-start | bytes 7077892
  54.7 29.9 %all-to-all-start.1 = ((bf16[32,32,384]{2,1,0:T(8,128)(2,1)}), bf16[32,32,384]{2,1,0:T(8,128)(2,1)S(1)}, u32[]{:S(2)}, u32[]{:S(2)}) async-start(bf16[32,32,384]{2,1,0:T(8,128)(2,1)} %widen.2), calls=%async_computation.1 | async-start | bytes 1572864 | tf_op jit(solution)/shard_map/all_to_all | solution.py:255
  67.3 11.7 %collective-permute-start = (f32[8,6272]{1,0:T(8,128)S(1)}, f32[8,6272]{1,0:T(8,128)S(1)}, u32[]{:S(2)}, u32[]{:S(2)}) collective-permute-start(f32[8,6272]{1,0:T(8,128)S(1)} %get-tuple-element.31.own), channel_id=1, source_target_pairs={{0,32},{32,0},{64,96},{96,64},{128,160},{160,128},{192,224},{224,1... | collective-permute-start | bytes 602120 | tf_op jit(solution)/shard_map/ppermute | solution.py:30
  69.5 10.2 %collective-permute-start.1 = (f32[8,6272]{1,0:T(8,128)S(1)}, f32[8,6272]{1,0:T(8,128)S(1)}, u32[]{:S(2)}, u32[]{:S(2)}) collective-permute-start(f32[8,6272]{1,0:T(8,128)S(1)} %get-tuple-element.32), channel_id=1, source_target_pairs={{32,64},{64,32},{96,128},{128,96},{160,192},{192,160},{224,256},{2... | collective-permute-start | bytes 602120 | tf_op jit(solution)/shard_map/ppermute | solution.py:31
  70.1 9.6 %collective-permute-start.2 = (f32[8,6272]{1,0:T(8,128)S(1)}, f32[8,6272]{1,0:T(8,128)S(1)}, u32[]{:S(2)}, u32[]{:S(2)}) collective-permute-start(f32[8,6272]{1,0:T(8,128)S(1)} %get-tuple-element.33), channel_id=1, source_target_pairs={{0,4},{4,0},{8,12},{12,8},{16,20},{20,16},{24,28},{28,24},{1,5},{5... | collective-permute-start | bytes 602120 | tf_op jit(solution)/shard_map/ppermute | solution.py:30
  72.6 7.3 %collective-permute-start.3 = (f32[8,6272]{1,0:T(8,128)S(1)}, f32[8,6272]{1,0:T(8,128)S(1)}, u32[]{:S(2)}, u32[]{:S(2)}) collective-permute-start(f32[8,6272]{1,0:T(8,128)S(1)} %get-tuple-element.34), channel_id=1, source_target_pairs={{4,8},{8,4},{12,16},{16,12},{20,24},{24,20},{5,9},{9,5},{13,17},{1... | collective-permute-start | bytes 602120 | tf_op jit(solution)/shard_map/ppermute | solution.py:31
  75.9 6.5 %collective-permute-start.4 = (f32[8,6272]{1,0:T(8,128)S(1)}, f32[8,6272]{1,0:T(8,128)S(1)}, u32[]{:S(2)}, u32[]{:S(2)}) collective-permute-start(f32[8,6272]{1,0:T(8,128)S(1)} %get-tuple-element.35), channel_id=1, source_target_pairs={{0,1},{1,0},{2,3},{3,2},{4,5},{5,4},{6,7},{7,6},{8,9},{9,8},{10,11... | collective-permute-start | bytes 602120 | tf_op jit(solution)/shard_map/ppermute | solution.py:30
  79.0 3.4 %collective-permute-start.5 = (f32[8,6272]{1,0:T(8,128)S(1)}, f32[8,6272]{1,0:T(8,128)S(1)}, u32[]{:S(2)}, u32[]{:S(2)}) collective-permute-start(f32[8,6272]{1,0:T(8,128)S(1)} %get-tuple-element.36), channel_id=1, source_target_pairs={{1,2},{2,1},{5,6},{6,5},{9,10},{10,9},{13,14},{14,13},{17,18},{18,... | collective-permute-start | bytes 602120 | tf_op jit(solution)/shard_map/ppermute | solution.py:31
  83.3 1.3 copy-start.1
  84.6 1.6 copy-start.2
  86.2 25.0 %copy-start.5 = (f32[1,1,1,3,2,64,128]{6,5,4,3,2,1,0:T(8,128)S(1)}, f32[1,1,1,3,2,64,128]{6,5,4,3,2,1,0:T(8,128)}, u32[]{:S(2)}) copy-start(f32[1,1,1,3,2,64,128]{6,5,4,3,2,1,0:T(8,128)} %param.9) | copy-start | bytes 589828
  89.8 76.3 %copy-start.3 = (bf16[3,336,1024]{2,1,0:T(8,128)(2,1)S(1)}, bf16[3,336,1024]{2,1,0:T(8,128)(2,1)}, u32[]{:S(2)}) copy-start(bf16[3,336,1024]{2,1,0:T(8,128)(2,1)} %copy-done.1) | copy-start | bytes 6193156
  89.8 13.7 %collective-permute-start.10 = (f32[64,128]{1,0:T(8,128)S(1)}, f32[64,128]{1,0:T(8,128)S(1)}, u32[]{:S(2)}, u32[]{:S(2)}) collective-permute-start(f32[64,128]{1,0:T(8,128)S(1)} %get-tuple-element.44), channel_id=1, source_target_pairs={{0,1},{1,0},{2,3},{3,2},{4,5},{5,4},{6,7},{7,6},{8,9},{9,8},{10,11... | collective-permute-start | bytes 98312 | tf_op jit(solution)/shard_map/ppermute | solution.py:30
  96.4 13.1 %collective-permute-start.11 = (f32[64,128]{1,0:T(8,128)S(1)}, f32[64,128]{1,0:T(8,128)S(1)}, u32[]{:S(2)}, u32[]{:S(2)}) collective-permute-start(f32[64,128]{1,0:T(8,128)S(1)} %get-tuple-element.45), channel_id=1, source_target_pairs={{1,2},{2,1},{5,6},{6,5},{9,10},{10,9},{13,14},{14,13},{17,18},{18,... | collective-permute-start | bytes 98312 | tf_op jit(solution)/shard_map/ppermute | solution.py:31
  97.1 12.5 %collective-permute-start.6 = (f32[64,128]{1,0:T(8,128)S(1)}, f32[64,128]{1,0:T(8,128)S(1)}, u32[]{:S(2)}, u32[]{:S(2)}) collective-permute-start(f32[64,128]{1,0:T(8,128)S(1)} %get-tuple-element.40), channel_id=1, source_target_pairs={{0,32},{32,0},{64,96},{96,64},{128,160},{160,128},{192,224},{224,1... | collective-permute-start | bytes 98312 | tf_op jit(solution)/shard_map/ppermute | solution.py:30
  100.9 8.7 %collective-permute-start.7 = (f32[64,128]{1,0:T(8,128)S(1)}, f32[64,128]{1,0:T(8,128)S(1)}, u32[]{:S(2)}, u32[]{:S(2)}) collective-permute-start(f32[64,128]{1,0:T(8,128)S(1)} %get-tuple-element.41), channel_id=1, source_target_pairs={{32,64},{64,32},{96,128},{128,96},{160,192},{192,160},{224,256},{2... | collective-permute-start | bytes 98312 | tf_op jit(solution)/shard_map/ppermute | solution.py:31
  101.5 8.1 %collective-permute-start.8 = (f32[64,128]{1,0:T(8,128)S(1)}, f32[64,128]{1,0:T(8,128)S(1)}, u32[]{:S(2)}, u32[]{:S(2)}) collective-permute-start(f32[64,128]{1,0:T(8,128)S(1)} %get-tuple-element.42), channel_id=1, source_target_pairs={{0,4},{4,0},{8,12},{12,8},{16,20},{20,16},{24,28},{28,24},{1,5},{5... | collective-permute-start | bytes 98312 | tf_op jit(solution)/shard_map/ppermute | solution.py:30
  103.5 7.7 %collective-permute-start.9 = (f32[64,128]{1,0:T(8,128)S(1)}, f32[64,128]{1,0:T(8,128)S(1)}, u32[]{:S(2)}, u32[]{:S(2)}) collective-permute-start(f32[64,128]{1,0:T(8,128)S(1)} %get-tuple-element.43), channel_id=1, source_target_pairs={{4,8},{8,4},{12,16},{16,12},{20,24},{24,20},{5,9},{9,5},{13,17},{1... | collective-permute-start | bytes 98312 | tf_op jit(solution)/shard_map/ppermute | solution.py:31
  170.6 16.2 %copy-start.6 = (f32[64,128]{1,0:T(8,128)}, f32[64,128]{1,0:T(8,128)S(1)}, u32[]{:S(2)}) copy-start(f32[64,128]{1,0:T(8,128)S(1)} %get-tuple-element.57) | copy-start | bytes 98308
  170.6 19.2 %copy-start.7 = (f32[64,128]{1,0:T(8,128)}, f32[64,128]{1,0:T(8,128)S(1)}, u32[]{:S(2)}) copy-start(f32[64,128]{1,0:T(8,128)S(1)} %get-tuple-element.56) | copy-start | bytes 98308
  183.0 26.0 %all-to-all-start.5 = ((f32[32,2,128]{2,1,0:T(2,128)}), f32[32,2,128]{2,1,0:T(2,128)S(1)}, u32[]{:S(2)}, u32[]{:S(2)}) async-start(f32[32,2,128]{2,1,0:T(2,128)} %broadcast_in_dim.4), calls=%async_computation.5 | async-start | bytes 65536 | tf_op jit(solution)/shard_map/all_to_all | solution.py:19
  186.8 10.9 %collective-permute-start.12 = (f32[64,128]{1,0:T(8,128)}, f32[64,128]{1,0:T(8,128)S(1)}, u32[]{:S(2)}, u32[]{:S(2)}) collective-permute-start(f32[64,128]{1,0:T(8,128)} %get-tuple-element.52), channel_id=1, source_target_pairs={{0,32},{32,0},{64,96},{96,64},{128,160},{160,128},{192,224},{224,1... | collective-permute-start | bytes 98312 | tf_op jit(solution)/shard_map/ppermute | solution.py:30
  189.8 25.2 %collective-permute-start.13 = (f32[64,128]{1,0:T(8,128)}, f32[64,128]{1,0:T(8,128)S(1)}, u32[]{:S(2)}, u32[]{:S(2)}) collective-permute-start(f32[64,128]{1,0:T(8,128)} %get-tuple-element.53), channel_id=1, source_target_pairs={{32,64},{64,32},{96,128},{128,96},{160,192},{192,160},{224,256},{2... | collective-permute-start | bytes 98312 | tf_op jit(solution)/shard_map/ppermute | solution.py:31
  190.5 24.6 %collective-permute-start.14 = (f32[64,128]{1,0:T(8,128)}, f32[64,128]{1,0:T(8,128)S(1)}, u32[]{:S(2)}, u32[]{:S(2)}) collective-permute-start(f32[64,128]{1,0:T(8,128)} %get-tuple-element.54), channel_id=1, source_target_pairs={{0,4},{4,0},{8,12},{12,8},{16,20},{20,16},{24,28},{28,24},{1,5},{5... | collective-permute-start | bytes 98312 | tf_op jit(solution)/shard_map/ppermute | solution.py:30
  193.4 21.7 %collective-permute-start.15 = (f32[64,128]{1,0:T(8,128)}, f32[64,128]{1,0:T(8,128)S(1)}, u32[]{:S(2)}, u32[]{:S(2)}) collective-permute-start(f32[64,128]{1,0:T(8,128)} %get-tuple-element.55), channel_id=1, source_target_pairs={{4,8},{8,4},{12,16},{16,12},{20,24},{24,20},{5,9},{9,5},{13,17},{1... | collective-permute-start | bytes 98312 | tf_op jit(solution)/shard_map/ppermute | solution.py:31
  195.5 19.6 %collective-permute-start.16 = (f32[64,128]{1,0:T(8,128)}, f32[64,128]{1,0:T(8,128)S(1)}, u32[]{:S(2)}, u32[]{:S(2)}) collective-permute-start(f32[64,128]{1,0:T(8,128)} %copy-done.7), channel_id=1, source_target_pairs={{0,1},{1,0},{2,3},{3,2},{4,5},{5,4},{6,7},{7,6},{8,9},{9,8},{10,11... | collective-permute-start | bytes 98312 | tf_op jit(solution)/shard_map/ppermute | solution.py:30
  197.8 17.4 %collective-permute-start.17 = (f32[64,128]{1,0:T(8,128)}, f32[64,128]{1,0:T(8,128)S(1)}, u32[]{:S(2)}, u32[]{:S(2)}) collective-permute-start(f32[64,128]{1,0:T(8,128)} %copy-done.6), channel_id=1, source_target_pairs={{1,2},{2,1},{5,6},{6,5},{9,10},{10,9},{13,14},{14,13},{17,18},{18,... | collective-permute-start | bytes 98312 | tf_op jit(solution)/shard_map/ppermute | solution.py:31
  209.7 12.7 %all-to-all-start.6 = ((f32[32,2,128]{2,1,0:T(2,128)}), f32[32,2,128]{2,1,0:T(2,128)S(1)}, u32[]{:S(2)}, u32[]{:S(2)}) async-start(f32[32,2,128]{2,1,0:T(2,128)} %broadcast_in_dim.5), calls=%async_computation.6 | async-start | bytes 65536 | tf_op jit(solution)/shard_map/all_to_all | solution.py:19

commit v5 on v4

--- a/solution.py
+++ b/solution.py
@@ -59,8 +59,8 @@
                 out[:, begin : begin + 128] = block
     for d in range(3):
         is_even = flags[d] == 0
-        minus = jnp.concatenate([traces[2 * d], blank], axis=0)
-        plus = jnp.concatenate([traces[2 * d + 1], blank], axis=0)
+        minus = jnp.concatenate([traces[:, d, 0, :], blank], axis=0)
+        plus = jnp.concatenate([traces[:, d, 1, :], blank], axis=0)
         packed[2 * d][:, modes * parts :] = jnp.where(is_even, plus, minus)
         packed[2 * d + 1][:, modes * parts :] = jnp.where(is_even, minus, plus)
 
@@ -139,7 +139,7 @@
 
 
 def modes_kernel(flags, right_side, out):
-    as_rows(right_side[...], out)
+    as_rows(jnp.concatenate([right_side[m] for m in range(right_side.shape[0])], axis=0), out)
 
 
 def widen_kernel(flags, column, out):
@@ -149,9 +149,13 @@
         out[p] = wide
 
 
-def start_kernel(flags, stacked, pieces, spread, matrix, field, image, *outgoing):
+def start_kernel(flags, stacked, pieces, spread, stored, field, image, *refs):
+    outgoing, (matrix, arrival) = refs[:6], refs[6:]
+    copy = pltpu.make_async_copy(stored, matrix, arrival)
+    copy.start()
     value = coarse(stacked, pieces, spread)
     field[...] = value
+    copy.wait()
     image[...] = jnp.dot(value, matrix[...], precision=HIGHEST, preferred_element_type=f32)
     send_faces(flags, image, outgoing)
 
@@ -168,9 +172,13 @@
     as_rows(total, sums)
 
 
-def project_kernel(flags, stacked, pieces, spread, matrix, residual, field, image, grams, *outgoing):
+def project_kernel(flags, stacked, pieces, spread, stored, residual, field, image, grams, *refs):
+    outgoing, (matrix, arrival) = refs[:6], refs[6:]
+    copy = pltpu.make_async_copy(stored, matrix, arrival)
+    copy.start()
     value = residual[...] - coarse(stacked, pieces, spread)
     field[...] = value
+    copy.wait()
     applied = jnp.dot(value, matrix[...], precision=HIGHEST, preferred_element_type=f32)
     image[...] = applied
     across = (((1,), (1,)), ((), ()))
@@ -217,13 +225,14 @@
         )
 
 
-def call(kernel, outs, *args, **options):
+def call(kernel, outs, *args, stored=None, **options):
     flags = pl.BlockSpec(memory_space=pltpu.SMEM)
     block = pl.BlockSpec(memory_space=pltpu.VMEM)
     return pl.pallas_call(
         kernel,
         out_shape=[jax.ShapeDtypeStruct(shape, kind) for shape, kind in outs],
-        in_specs=[flags] + [block] * (len(args) - 1),
+        in_specs=[flags]
+        + [pl.BlockSpec(memory_space=pltpu.HBM) if i == stored else block for i in range(1, len(args))],
         out_specs=[block] * len(outs),
         compiler_params=pltpu.CompilerParams(vmem_limit_bytes=24 << 20),
         **options,
@@ -235,12 +244,14 @@
     modes = rigid_modes.shape[3]
     long, plane = lax.axis_size("gx"), lax.axis_size(PLANE)
     parts = long * plane
-    matrix = compliance[0, 0, 0]
+    matrix = pltpu.with_memory_space_constraint(compliance[0, 0, 0], pltpu.HBM)
     traces = rigid_modes[0, 0, 0].transpose(1, 2, 0, 3).reshape(6, modes, face)
     gaps = dual_rhs[0, 0, 0].reshape(6, loads, face)
+    right_side = coarse_rhs[0, 0, 0].reshape(modes, 1, loads)
     where = [lax.axis_index(axis) for axis in AXES]
     flags = jnp.stack([w % 2 for w in where] + [jnp.minimum(w, 1) for w in where]).astype(jnp.int32)
     wide, faces = ((loads, 6 * face), f32), ((6, loads, face), f32)
+    held = [pltpu.VMEM(matrix.shape, f32), pltpu.SemaphoreType.DMA]
     packs = ((8, modes * parts + face), f32)
 
     row = ((long, modes // 2 + 1, 2 * loads), bf16)
@@ -254,18 +265,19 @@
         )[0]
         return lax.all_to_all(column, PLANE, 0, 0, tiled=True).reshape(parts, modes * loads)
 
-    column = along(call(modes_kernel, [row], flags, coarse_rhs[0, 0, 0], name="modes")[0])
+    column = along(call(modes_kernel, [row], flags, right_side, name="modes")[0])
     packed = call(
         functools.partial(prepare, modes, long, plane),
         [packs] * 6,
         flags,
         coarse_inverse,
-        traces,
+        rigid_modes[0, 0, 0],
         scratch_shapes=[pltpu.VMEM((modes * parts, 8), f32)],
         name="prepare_rows",
     )
     in_plane = swap(packed[2:], PLANE)
-    arrived = swap(packed[:2], AXES[:1]) + in_plane
+    arrived = swap(packed[:2], AXES[:1])
+    arrived += [pltpu.with_memory_space_constraint(a, pltpu.HBM) for a in in_plane]
     stacked = across(column)
     pieces, spread = call(
         functools.partial(build, modes, parts),
@@ -285,6 +297,8 @@
         pieces,
         spread,
         matrix,
+        stored=4,
+        scratch_shapes=held,
         name="start_fields",
     )
     residual, sums = call(
@@ -306,6 +320,8 @@
         spread,
         matrix,
         residual,
+        stored=4,
+        scratch_shapes=held,
         name="project",
     )
     grams = lax.all_to_all(

time: 227 us -> 227 us (level)
  local copies, waits for them, and re-layouts: 5.11 us -> 2.78 us
    unnamed x19 -> x16, local copies, waits for them, and re-layouts: 3.78 us -> 1.44 us
where the time goes in v5:
time: 227 us; the launch traced here: 226 us
  blocking collectives  116 us (51%)
  starting transfers between devices  62.3 us (27%)
  Pallas kernels  22 us (10%)
  waiting for transfers between devices  22 us (10%)
  local copies, waits for them, and re-layouts  2.78 us (1%)
    all_to_all x2, blocking collectives, along(): return lax.all_to_all(rows, 'gx', 0, 0, tiled=True)  81 us
    ppermute x9, starting transfers between devices, swap(): arrived.append(lax.ppermute(outgoing[2 * d], axis, even))  27.9 us
    all_to_all x1, blocking collectives, across(): lax.all_to_all(column, PLANE, 0, 0, tiled=True)  23.2 us
    pallas_call x9, Pallas kernels, call(): pl.pallas_call(kernel, out_shape=[jax.ShapeDtypeStruct(shape, kind) for s...  22 us
    all_to_all x2, waiting for transfers between devices, to_all(): lax.all_to_all(jnp.broadcast_to(block[None], (lax.axis_size(axis),) + blo...  17.7 us
    ppermute x9, starting transfers between devices, swap(): arrived.append(lax.ppermute(outgoing[2 * d + 1], axis, odd))  15.5 us
    all_to_all x1, blocking collectives, body(): lax.all_to_all(grams.reshape(plane, loads // plane, 2 * loads), PLANE, 0,...  11.7 us
    all_to_all x2, starting transfers between devices, to_all(): lax.all_to_all(jnp.broadcast_to(block[None], (lax.axis_size(axis),) + blo...  9.58 us
  transfers between devices with their start and end apart: 21, of which 5 were waited for; matrix products, arithmetic and copies ran while one was open for 0% of the time, Pallas kernels for 2%

profile of v5, /device:TPU:1, one launch (start us, length us, event | category | flops | bytes accessed | tf_op | source)
XLA Modules:
  0.0 226.1 jit_solution(567558676283892858)
XLA Ops:
  0.8 0.7 copy-done.3
  2.1 51.0 %all_to_all.35.column = bf16[32,4,128]{2,1,0:T(4,128)(2,1)S(1)} all-to-all(bf16[32,4,128]{2,1,0:T(4,128)(2,1)S(1)} %modes.1), channel_id=1, replica_groups=mesh['gx'=32,'gy'=8,'gz'=4] {'gx'}, dimensions={0} | all-to-all | bytes 65536 | tf_op jit(solution)/shard_map/all_to_all | solution.py:260
  53.1 1.5 widen.2
  54.6 9.3 %all-to-all-start.1 = ((bf16[32,32,384]{2,1,0:T(8,128)(2,1)}), bf16[32,32,384]{2,1,0:T(8,128)(2,1)S(1)}, u32[]{:S(2)}, u32[]{:S(2)}) async-start(bf16[32,32,384]{2,1,0:T(8,128)(2,1)} %widen.2), calls=%async_computation.1 | async-start | bytes 1572864 | tf_op jit(solution)/shard_map/all_to_all | solution.py:266
  63.9 3.2 %prepare_rows.1 = (f32[8,6272]{1,0:T(8,128)S(1)}, f32[8,6272]{1,0:T(8,128)S(1)}, f32[8,6272]{1,0:T(8,128)S(1)}, f32[8,6272]{1,0:T(8,128)S(1)}, f32[8,6272]{1,0:T(8,128)S(1)}, /*index=5*/f32[8,6272]{1,0:T(8,128)S(1)}) custom-call(s32[6]{0:T(128)S(1)} %stack.27.flags, f32[6,6144]{1,0:T(8,128)S(1)} %copy-done, f32[6,3,2,128]{3,2,1,0:T(2,128)S(1)} %bitcast.25), custom_call_target="tpu_custom_call" | custom-call | tf_op jit(solution)/shard_map/prepare_rows/pallas_call | solution.py:231
  67.1 2.2 collective-permute-start
  70.0 2.4 %collective-permute-start.2 = (f32[8,6272]{1,0:T(8,128)S(1)}, f32[8,6272]{1,0:T(8,128)S(1)}, u32[]{:S(2)}, u32[]{:S(2)}) collective-permute-start(f32[8,6272]{1,0:T(8,128)S(1)} %get-tuple-element.33), channel_id=1, source_target_pairs={{0,4},{4,0},{8,12},{12,8},{16,20},{20,16},{24,28},{28,24},{1,5},{5... | collective-permute-start | bytes 602120 | tf_op jit(solution)/shard_map/ppermute | solution.py:30
  72.4 3.3 %collective-permute-start.3 = (f32[8,6272]{1,0:T(8,128)S(1)}, f32[8,6272]{1,0:T(8,128)S(1)}, u32[]{:S(2)}, u32[]{:S(2)}) collective-permute-start(f32[8,6272]{1,0:T(8,128)S(1)} %get-tuple-element.34), channel_id=1, source_target_pairs={{4,8},{8,4},{12,16},{16,12},{20,24},{24,20},{5,9},{9,5},{13,17},{1... | collective-permute-start | bytes 602120 | tf_op jit(solution)/shard_map/ppermute | solution.py:31
  75.7 3.1 %collective-permute-start.4 = (f32[8,6272]{1,0:T(8,128)S(1)}, f32[8,6272]{1,0:T(8,128)S(1)}, u32[]{:S(2)}, u32[]{:S(2)}) collective-permute-start(f32[8,6272]{1,0:T(8,128)S(1)} %get-tuple-element.35), channel_id=1, source_target_pairs={{0,1},{1,0},{2,3},{3,2},{4,5},{5,4},{6,7},{7,6},{8,9},{9,8},{10,11... | collective-permute-start | bytes 602120 | tf_op jit(solution)/shard_map/ppermute | solution.py:30
  78.8 0.7 collective-permute-start.5
  79.7 2.5 %collective-permute-done.4.refs_4_ = f32[8,6272]{1,0:T(8,128)S(1)} collective-permute-done((f32[8,6272]{1,0:T(8,128)S(1)}, f32[8,6272]{1,0:T(8,128)S(1)}, u32[]{:S(2)}, u32[]{:S(2)}) %collective-permute-start.4) | collective-permute-done | bytes 200736 | tf_op jit(solution)/shard_map/ppermute | solution.py:30
  82.9 1.6 build_rows.1
  84.6 5.0 %start_fields.1 = (f32[64,768]{1,0:T(8,128)S(1)}, f32[64,768]{1,0:T(8,128)S(1)}, f32[64,128]{1,0:T(8,128)S(1)}, f32[64,128]{1,0:T(8,128)S(1)}, f32[64,128]{1,0:T...) custom-call(s32[6]{0:T(128)S(1)} %stack.27.flags, ...), custom_call_target="tpu_custom_call" | custom-call | tf_op jit(solution)/shard_map/start_fields/pallas_call | solution.py:231
  89.6 6.5 %collective-permute-start.10 = (f32[64,128]{1,0:T(8,128)S(1)}, f32[64,128]{1,0:T(8,128)S(1)}, u32[]{:S(2)}, u32[]{:S(2)}) collective-permute-start(f32[64,128]{1,0:T(8,128)S(1)} %get-tuple-element.44), channel_id=1, source_target_pairs={{0,1},{1,0},{2,3},{3,2},{4,5},{5,4},{6,7},{7,6},{8,9},{9,8},{10,11... | collective-permute-start | bytes 98312 | tf_op jit(solution)/shard_map/ppermute | solution.py:30
  96.7 3.8 %collective-permute-start.6 = (f32[64,128]{1,0:T(8,128)S(1)}, f32[64,128]{1,0:T(8,128)S(1)}, u32[]{:S(2)}, u32[]{:S(2)}) collective-permute-start(f32[64,128]{1,0:T(8,128)S(1)} %get-tuple-element.40), channel_id=1, source_target_pairs={{0,32},{32,0},{64,96},{96,64},{128,160},{160,128},{192,224},{224,1... | collective-permute-start | bytes 98312 | tf_op jit(solution)/shard_map/ppermute | solution.py:30
  101.2 1.9 collective-permute-start.8
  103.1 6.1 %collective-permute-start.9 = (f32[64,128]{1,0:T(8,128)S(1)}, f32[64,128]{1,0:T(8,128)S(1)}, u32[]{:S(2)}, u32[]{:S(2)}) collective-permute-start(f32[64,128]{1,0:T(8,128)S(1)} %get-tuple-element.43), channel_id=1, source_target_pairs={{4,8},{8,4},{12,16},{16,12},{20,24},{24,20},{5,9},{9,5},{13,17},{1... | collective-permute-start | bytes 98312 | tf_op jit(solution)/shard_map/ppermute | solution.py:31
  109.2 1.5 collective-permute-done.9.refs_3_
  110.8 1.0 residual.1
  111.8 30.0 %all_to_all.36.column = bf16[32,4,128]{2,1,0:T(4,128)(2,1)S(1)} all-to-all(bf16[32,4,128]{2,1,0:T(4,128)(2,1)S(1)} %get-tuple-element.46), channel_id=1, replica_groups=mesh['gx'=32,'gy'=8,'gz'=4] {'gx'}, dimensions={0} | all-to-all | bytes 65536 | tf_op jit(solution)/shard_map/all_to_all | solution.py:260
  142.4 23.2 %all_to_all.37 = bf16[32,32,384]{2,1,0:T(8,128)(2,1)S(1)} all-to-all(bf16[32,32,384]{2,1,0:T(8,128)(2,1)S(1)} %widen.3), channel_id=1, replica_groups=mesh['gx'=32,'gy'=8,'gz'=4] {'gy','gz'}, dimensions={0} | all-to-all | bytes 1572864 | tf_op jit(solution)/shard_map/all_to_all | solution.py:266
  165.6 4.3 %project.1 = (f32[64,768]{1,0:T(8,128)S(1)}, f32[64,768]{1,0:T(8,128)S(1)}, f32[64,128]{1,0:T(8,128)S(1)}, f32[64,128]{1,0:T(8,128)S(1)}, f32[64,128]{1,0:T(8,12...) custom-call(s32[6]{0:T(128)S(1)} %stack.27.flags, ...), custom_call_target="tpu_custom_call" | custom-call | tf_op jit(solution)/shard_map/project/pallas_call | solution.py:231
  169.9 11.7 %all_to_all.38 = f32[32,2,128]{2,1,0:T(2,128)S(1)} all-to-all(f32[32,2,128]{2,1,0:T(2,128)S(1)} %bitcast.27), channel_id=1, replica_groups=mesh['gx'=32,'gy'=8,'gz'=4] {'gy','gz'}, dimensions={0} | all-to-all | bytes 65536 | tf_op jit(solution)/shard_map/all_to_all | solution.py:327
  182.3 4.0 %all-to-all-start.5 = ((f32[32,2,128]{2,1,0:T(2,128)}), f32[32,2,128]{2,1,0:T(2,128)S(1)}, u32[]{:S(2)}, u32[]{:S(2)}) async-start(f32[32,2,128]{2,1,0:T(2,128)} %broadcast_in_dim.4), calls=%async_computation.5 | async-start | bytes 65536 | tf_op jit(solution)/shard_map/all_to_all | solution.py:19
  186.4 3.0 %collective-permute-start.12 = (f32[64,128]{1,0:T(8,128)S(1)}, f32[64,128]{1,0:T(8,128)S(1)}, u32[]{:S(2)}, u32[]{:S(2)}) collective-permute-start(f32[64,128]{1,0:T(8,128)S(1)} %get-tuple-element.52), channel_id=1, source_target_pairs={{0,32},{32,0},{64,96},{96,64},{128,160},{160,128},{192,224},{224,1... | collective-permute-start | bytes 98312 | tf_op jit(solution)/shard_map/ppermute | solution.py:30
  190.1 2.9 %collective-permute-start.14 = (f32[64,128]{1,0:T(8,128)S(1)}, f32[64,128]{1,0:T(8,128)S(1)}, u32[]{:S(2)}, u32[]{:S(2)}) collective-permute-start(f32[64,128]{1,0:T(8,128)S(1)} %get-tuple-element.54), channel_id=1, source_target_pairs={{0,4},{4,0},{8,12},{12,8},{16,20},{20,16},{24,28},{28,24},{1,5},{5... | collective-permute-start | bytes 98312 | tf_op jit(solution)/shard_map/ppermute | solution.py:30
  192.9 2.1 collective-permute-start.15
  195.1 2.2 collective-permute-start.16
  198.0 10.5 %all-to-all-done.5 = f32[32,2,128]{2,1,0:T(2,128)S(1)} async-done(((f32[32,2,128]{2,1,0:T(2,128)}), f32[32,2,128]{2,1,0:T(2,128)S(1)}, u32[]{:S(2)}, u32[]{:S(2)}) %all-to-all-start.5) | async-done | bytes 32800 | tf_op jit(solution)/shard_map/all_to_all | solution.py:19
  209.1 5.6 %all-to-all-start.6 = ((f32[32,2,128]{2,1,0:T(2,128)}), f32[32,2,128]{2,1,0:T(2,128)S(1)}, u32[]{:S(2)}, u32[]{:S(2)}) async-start(f32[32,2,128]{2,1,0:T(2,128)} %broadcast_in_dim.5), calls=%async_computation.6 | async-start | bytes 65536 | tf_op jit(solution)/shard_map/all_to_all | solution.py:19
  214.8 7.3 %all-to-all-done.6 = f32[32,2,128]{2,1,0:T(2,128)S(1)} async-done(((f32[32,2,128]{2,1,0:T(2,128)}), f32[32,2,128]{2,1,0:T(2,128)S(1)}, u32[]{:S(2)}, u32[]{:S(2)}) %all-to-all-start.6) | async-done | bytes 32800 | tf_op jit(solution)/shard_map/all_to_all | solution.py:19
  222.0 4.1 %final_update.1 = (f32[6,64,128]{2,1,0:T(8,128)}, f32[6,64,128]{2,1,0:T(8,128)}) custom-call(s32[6]{0:T(128)S(1)} %stack.27.flags, f32[64,128]{1,0:T(8,128)S(1)} %bitcast.24, f32[64,768]{1,0:T(8,128)S(1)} %get-tuple-element.49.multipliers, f32[64,768]{1,0:T(8,128)S(1)} %get-tuple-element.47.residual, f32[64,768]{1,0:T(8,128)S(1)} %get-tuple-element.50.field, ...), custom_call_target="tpu_custom_call" | custom-call | tf_op jit(solution)/shard_map/final_update/pallas_call | solution.py:231
  (45 shorter events, 7.0 us)
Async XLA Ops:
  0.6 63.3 %copy-start.2 = (f32[1,1,1,6,3,2,128]{6,5,4,3,2,1,0:T(2,128)S(1)}, f32[1,1,1,6,3,2,128]{6,5,4,3,2,1,0:T(2,128)}, u32[]{:S(2)}) copy-start(f32[1,1,1,6,3,2,128]{6,5,4,3,2,1,0:T(2,128)} %param.6) | copy-start | bytes 55300
  0.6 63.3 %copy-start = (f32[6,6144]{1,0:T(8,128)S(1)}, f32[6,6144]{1,0:T(8,128)}, u32[]{:S(2)}) copy-start(f32[6,6144]{1,0:T(8,128)} %rows.1) | copy-start | bytes 442372
  0.8 0.7 copy-start.3
  54.6 30.0 %all-to-all-start.1 = ((bf16[32,32,384]{2,1,0:T(8,128)(2,1)}), bf16[32,32,384]{2,1,0:T(8,128)(2,1)S(1)}, u32[]{:S(2)}, u32[]{:S(2)}) async-start(bf16[32,32,384]{2,1,0:T(8,128)(2,1)} %widen.2), calls=%async_computation.1 | async-start | bytes 1572864 | tf_op jit(solution)/shard_map/all_to_all | solution.py:266
  67.1 11.7 %collective-permute-start = (f32[8,6272]{1,0:T(8,128)S(1)}, f32[8,6272]{1,0:T(8,128)S(1)}, u32[]{:S(2)}, u32[]{:S(2)}) collective-permute-start(f32[8,6272]{1,0:T(8,128)S(1)} %get-tuple-element.31.own), channel_id=1, source_target_pairs={{0,32},{32,0},{64,96},{96,64},{128,160},{160,128},{192,224},{224,1... | collective-permute-start | bytes 602120 | tf_op jit(solution)/shard_map/ppermute | solution.py:30
  69.3 10.2 %collective-permute-start.1 = (f32[8,6272]{1,0:T(8,128)S(1)}, f32[8,6272]{1,0:T(8,128)S(1)}, u32[]{:S(2)}, u32[]{:S(2)}) collective-permute-start(f32[8,6272]{1,0:T(8,128)S(1)} %get-tuple-element.32), channel_id=1, source_target_pairs={{32,64},{64,32},{96,128},{128,96},{160,192},{192,160},{224,256},{2... | collective-permute-start | bytes 602120 | tf_op jit(solution)/shard_map/ppermute | solution.py:31
  70.0 9.6 %collective-permute-start.2 = (f32[8,6272]{1,0:T(8,128)S(1)}, f32[8,6272]{1,0:T(8,128)S(1)}, u32[]{:S(2)}, u32[]{:S(2)}) collective-permute-start(f32[8,6272]{1,0:T(8,128)S(1)} %get-tuple-element.33), channel_id=1, source_target_pairs={{0,4},{4,0},{8,12},{12,8},{16,20},{20,16},{24,28},{28,24},{1,5},{5... | collective-permute-start | bytes 602120 | tf_op jit(solution)/shard_map/ppermute | solution.py:30
  72.4 7.3 %collective-permute-start.3 = (f32[8,6272]{1,0:T(8,128)S(1)}, f32[8,6272]{1,0:T(8,128)S(1)}, u32[]{:S(2)}, u32[]{:S(2)}) collective-permute-start(f32[8,6272]{1,0:T(8,128)S(1)} %get-tuple-element.34), channel_id=1, source_target_pairs={{4,8},{8,4},{12,16},{16,12},{20,24},{24,20},{5,9},{9,5},{13,17},{1... | collective-permute-start | bytes 602120 | tf_op jit(solution)/shard_map/ppermute | solution.py:31
  75.7 6.5 %collective-permute-start.4 = (f32[8,6272]{1,0:T(8,128)S(1)}, f32[8,6272]{1,0:T(8,128)S(1)}, u32[]{:S(2)}, u32[]{:S(2)}) collective-permute-start(f32[8,6272]{1,0:T(8,128)S(1)} %get-tuple-element.35), channel_id=1, source_target_pairs={{0,1},{1,0},{2,3},{3,2},{4,5},{5,4},{6,7},{7,6},{8,9},{9,8},{10,11... | collective-permute-start | bytes 602120 | tf_op jit(solution)/shard_map/ppermute | solution.py:30
  78.8 3.4 %collective-permute-start.5 = (f32[8,6272]{1,0:T(8,128)S(1)}, f32[8,6272]{1,0:T(8,128)S(1)}, u32[]{:S(2)}, u32[]{:S(2)}) collective-permute-start(f32[8,6272]{1,0:T(8,128)S(1)} %get-tuple-element.36), channel_id=1, source_target_pairs={{1,2},{2,1},{5,6},{6,5},{9,10},{10,9},{13,14},{14,13},{17,18},{18,... | collective-permute-start | bytes 602120 | tf_op jit(solution)/shard_map/ppermute | solution.py:31
  79.6 2.6 %copy-start.4 = (f32[8,6272]{1,0:T(8,128)}, f32[8,6272]{1,0:T(8,128)S(1)}, u32[]{:S(2)}) copy-start(f32[8,6272]{1,0:T(8,128)S(1)} %collective-permute-done.2.refs_2_) | copy-start | bytes 602116
  79.7 2.5 %copy-start.5 = (f32[8,6272]{1,0:T(8,128)}, f32[8,6272]{1,0:T(8,128)S(1)}, u32[]{:S(2)}) copy-start(f32[8,6272]{1,0:T(8,128)S(1)} %collective-permute-done.3.refs_3_) | copy-start | bytes 602116
  82.2 0.7 copy-start.6
  82.2 0.7 copy-start.7
  84.5 26.2 %copy-start.1 = (f32[1,1,1,3,2,64,128]{6,5,4,3,2,1,0:T(8,128)S(1)}, f32[1,1,1,3,2,64,128]{6,5,4,3,2,1,0:T(8,128)}, u32[]{:S(2)}) copy-start(f32[1,1,1,3,2,64,128]{6,5,4,3,2,1,0:T(8,128)} %param.9) | copy-start | bytes 589828
  89.6 13.5 %collective-permute-start.10 = (f32[64,128]{1,0:T(8,128)S(1)}, f32[64,128]{1,0:T(8,128)S(1)}, u32[]{:S(2)}, u32[]{:S(2)}) collective-permute-start(f32[64,128]{1,0:T(8,128)S(1)} %get-tuple-element.44), channel_id=1, source_target_pairs={{0,1},{1,0},{2,3},{3,2},{4,5},{5,4},{6,7},{7,6},{8,9},{9,8},{10,11... | collective-permute-start | bytes 98312 | tf_op jit(solution)/shard_map/ppermute | solution.py:30
  96.0 13.1 %collective-permute-start.11 = (f32[64,128]{1,0:T(8,128)S(1)}, f32[64,128]{1,0:T(8,128)S(1)}, u32[]{:S(2)}, u32[]{:S(2)}) collective-permute-start(f32[64,128]{1,0:T(8,128)S(1)} %get-tuple-element.45), channel_id=1, source_target_pairs={{1,2},{2,1},{5,6},{6,5},{9,10},{10,9},{13,14},{14,13},{17,18},{18,... | collective-permute-start | bytes 98312 | tf_op jit(solution)/shard_map/ppermute | solution.py:31
  96.7 12.5 %collective-permute-start.6 = (f32[64,128]{1,0:T(8,128)S(1)}, f32[64,128]{1,0:T(8,128)S(1)}, u32[]{:S(2)}, u32[]{:S(2)}) collective-permute-start(f32[64,128]{1,0:T(8,128)S(1)} %get-tuple-element.40), channel_id=1, source_target_pairs={{0,32},{32,0},{64,96},{96,64},{128,160},{160,128},{192,224},{224,1... | collective-permute-start | bytes 98312 | tf_op jit(solution)/shard_map/ppermute | solution.py:30
  100.5 8.7 %collective-permute-start.7 = (f32[64,128]{1,0:T(8,128)S(1)}, f32[64,128]{1,0:T(8,128)S(1)}, u32[]{:S(2)}, u32[]{:S(2)}) collective-permute-start(f32[64,128]{1,0:T(8,128)S(1)} %get-tuple-element.41), channel_id=1, source_target_pairs={{32,64},{64,32},{96,128},{128,96},{160,192},{192,160},{224,256},{2... | collective-permute-start | bytes 98312 | tf_op jit(solution)/shard_map/ppermute | solution.py:31
  101.2 8.1 %collective-permute-start.8 = (f32[64,128]{1,0:T(8,128)S(1)}, f32[64,128]{1,0:T(8,128)S(1)}, u32[]{:S(2)}, u32[]{:S(2)}) collective-permute-start(f32[64,128]{1,0:T(8,128)S(1)} %get-tuple-element.42), channel_id=1, source_target_pairs={{0,4},{4,0},{8,12},{12,8},{16,20},{20,16},{24,28},{28,24},{1,5},{5... | collective-permute-start | bytes 98312 | tf_op jit(solution)/shard_map/ppermute | solution.py:30
  103.1 7.7 %collective-permute-start.9 = (f32[64,128]{1,0:T(8,128)S(1)}, f32[64,128]{1,0:T(8,128)S(1)}, u32[]{:S(2)}, u32[]{:S(2)}) collective-permute-start(f32[64,128]{1,0:T(8,128)S(1)} %get-tuple-element.43), channel_id=1, source_target_pairs={{4,8},{8,4},{12,16},{16,12},{20,24},{24,20},{5,9},{9,5},{13,17},{1... | collective-permute-start | bytes 98312 | tf_op jit(solution)/shard_map/ppermute | solution.py:31
  182.3 26.1 %all-to-all-start.5 = ((f32[32,2,128]{2,1,0:T(2,128)}), f32[32,2,128]{2,1,0:T(2,128)S(1)}, u32[]{:S(2)}, u32[]{:S(2)}) async-start(f32[32,2,128]{2,1,0:T(2,128)} %broadcast_in_dim.4), calls=%async_computation.5 | async-start | bytes 65536 | tf_op jit(solution)/shard_map/all_to_all | solution.py:19
  186.4 10.9 %collective-permute-start.12 = (f32[64,128]{1,0:T(8,128)S(1)}, f32[64,128]{1,0:T(8,128)S(1)}, u32[]{:S(2)}, u32[]{:S(2)}) collective-permute-start(f32[64,128]{1,0:T(8,128)S(1)} %get-tuple-element.52), channel_id=1, source_target_pairs={{0,32},{32,0},{64,96},{96,64},{128,160},{160,128},{192,224},{224,1... | collective-permute-start | bytes 98312 | tf_op jit(solution)/shard_map/ppermute | solution.py:30
  189.4 25.3 %collective-permute-start.13 = (f32[64,128]{1,0:T(8,128)S(1)}, f32[64,128]{1,0:T(8,128)S(1)}, u32[]{:S(2)}, u32[]{:S(2)}) collective-permute-start(f32[64,128]{1,0:T(8,128)S(1)} %get-tuple-element.53), channel_id=1, source_target_pairs={{32,64},{64,32},{96,128},{128,96},{160,192},{192,160},{224,256},{2... | collective-permute-start | bytes 98312 | tf_op jit(solution)/shard_map/ppermute | solution.py:31
  190.1 24.6 %collective-permute-start.14 = (f32[64,128]{1,0:T(8,128)S(1)}, f32[64,128]{1,0:T(8,128)S(1)}, u32[]{:S(2)}, u32[]{:S(2)}) collective-permute-start(f32[64,128]{1,0:T(8,128)S(1)} %get-tuple-element.54), channel_id=1, source_target_pairs={{0,4},{4,0},{8,12},{12,8},{16,20},{20,16},{24,28},{28,24},{1,5},{5... | collective-permute-start | bytes 98312 | tf_op jit(solution)/shard_map/ppermute | solution.py:30
  192.9 21.8 %collective-permute-start.15 = (f32[64,128]{1,0:T(8,128)S(1)}, f32[64,128]{1,0:T(8,128)S(1)}, u32[]{:S(2)}, u32[]{:S(2)}) collective-permute-start(f32[64,128]{1,0:T(8,128)S(1)} %get-tuple-element.55), channel_id=1, source_target_pairs={{4,8},{8,4},{12,16},{16,12},{20,24},{24,20},{5,9},{9,5},{13,17},{1... | collective-permute-start | bytes 98312 | tf_op jit(solution)/shard_map/ppermute | solution.py:31
  195.1 19.6 %collective-permute-start.16 = (f32[64,128]{1,0:T(8,128)S(1)}, f32[64,128]{1,0:T(8,128)S(1)}, u32[]{:S(2)}, u32[]{:S(2)}) collective-permute-start(f32[64,128]{1,0:T(8,128)S(1)} %get-tuple-element.56), channel_id=1, source_target_pairs={{0,1},{1,0},{2,3},{3,2},{4,5},{5,4},{6,7},{7,6},{8,9},{9,8},{10,11... | collective-permute-start | bytes 98312 | tf_op jit(solution)/shard_map/ppermute | solution.py:30
  197.3 17.4 %collective-permute-start.17 = (f32[64,128]{1,0:T(8,128)S(1)}, f32[64,128]{1,0:T(8,128)S(1)}, u32[]{:S(2)}, u32[]{:S(2)}) collective-permute-start(f32[64,128]{1,0:T(8,128)S(1)} %get-tuple-element.57), channel_id=1, source_target_pairs={{1,2},{2,1},{5,6},{6,5},{9,10},{10,9},{13,14},{14,13},{17,18},{18,... | collective-permute-start | bytes 98312 | tf_op jit(solution)/shard_map/ppermute | solution.py:31
  209.1 12.9 %all-to-all-start.6 = ((f32[32,2,128]{2,1,0:T(2,128)}), f32[32,2,128]{2,1,0:T(2,128)S(1)}, u32[]{:S(2)}, u32[]{:S(2)}) async-start(f32[32,2,128]{2,1,0:T(2,128)} %broadcast_in_dim.5), calls=%async_computation.6 | async-start | bytes 65536 | tf_op jit(solution)/shard_map/all_to_all | solution.py:19

commit v6 on v5

--- a/solution.py
+++ b/solution.py
@@ -142,8 +142,10 @@
     as_rows(jnp.concatenate([right_side[m] for m in range(right_side.shape[0])], axis=0), out)
 
 
-def widen_kernel(flags, column, out):
+def widen_kernel(lead, flags, column, out):
     value = column[...].astype(f32)
+    if lead:
+        value = jnp.concatenate([value[-lead:], value[:-lead]], axis=0)
     wide = jnp.concatenate([value[:, q, :] for q in range(value.shape[1] - 1)], axis=1).astype(bf16)
     for p in range(out.shape[0]):
         out[p] = wide
@@ -256,16 +258,22 @@
 
     row = ((long, modes // 2 + 1, 2 * loads), bf16)
 
-    def along(rows):
-        return lax.all_to_all(rows, "gx", 0, 0, tiled=True)
-
-    def across(column):
+    def along(rows, lead=0):
+        group = [[(i + lead) % long for i in range(long)]] if lead else None
+        return lax.all_to_all(rows, "gx", 0, 0, axis_index_groups=group, tiled=True)
+
+    def across(column, lead=0):
         column = call(
-            widen_kernel, [((plane, long, modes * loads), bf16)], flags, column, name="widen"
+            functools.partial(widen_kernel, lead),
+            [((plane, long, modes * loads), bf16)],
+            flags,
+            column,
+            name="widen",
         )[0]
         return lax.all_to_all(column, PLANE, 0, 0, tiled=True).reshape(parts, modes * loads)
 
-    column = along(call(modes_kernel, [row], flags, right_side, name="modes")[0])
+    middle = long // 2
+    column = along(call(modes_kernel, [row], flags, right_side, name="modes")[0], middle)
     packed = call(
         functools.partial(prepare, modes, long, plane),
         [packs] * 6,
@@ -278,7 +286,7 @@
     in_plane = swap(packed[2:], PLANE)
     arrived = swap(packed[:2], AXES[:1])
     arrived += [pltpu.with_memory_space_constraint(a, pltpu.HBM) for a in in_plane]
-    stacked = across(column)
+    stacked = across(column, middle)
     pieces, spread = call(
         functools.partial(build, modes, parts),
         [((modes // 2, 3 * 14 * 8, parts), bf16), ((7 * 8, 6 * face), f32)],

time: 227 us -> 231 us (1.018)
    ppermute x9, starting transfers between devices: 27.9 us -> 30.3 us  [swap(): arrived.append(lax.ppermute(outgoing[2 * d], axis, even))]
where the time goes in v6:
time: 231 us; the launch traced here: 230 us
  blocking collectives  118 us (51%)
  starting transfers between devices  64.2 us (28%)
  Pallas kernels  22 us (10%)
  waiting for transfers between devices  22 us (10%)
  local copies, waits for them, and re-layouts  2.78 us (1%)
    all_to_all x2, blocking collectives, along(): return lax.all_to_all(rows, 'gx', 0, 0, axis_index_groups=group, tiled=True)  82.6 us
    ppermute x9, starting transfers between devices, swap(): arrived.append(lax.ppermute(outgoing[2 * d], axis, even))  30.3 us
    all_to_all x1, blocking collectives, across(): lax.all_to_all(column, PLANE, 0, 0, tiled=True)  23.2 us
    pallas_call x9, Pallas kernels, call(): pl.pallas_call(kernel, out_shape=[jax.ShapeDtypeStruct(shape, kind) for s...  22 us
    all_to_all x2, waiting for transfers between devices, to_all(): lax.all_to_all(jnp.broadcast_to(block[None], (lax.axis_size(axis),) + blo...  17.7 us
    ppermute x9, starting transfers between devices, swap(): arrived.append(lax.ppermute(outgoing[2 * d + 1], axis, odd))  15.5 us
    all_to_all x1, blocking collectives, body(): lax.all_to_all(grams.reshape(plane, loads // plane, 2 * loads), PLANE, 0,...  11.7 us
    all_to_all x2, starting transfers between devices, to_all(): lax.all_to_all(jnp.broadcast_to(block[None], (lax.axis_size(axis),) + blo...  9.58 us
  transfers between devices with their start and end apart: 21, of which 5 were waited for; matrix products, arithmetic and copies ran while one was open for 0% of the time, Pallas kernels for 2%

profile of v6, /device:TPU:1, one launch (start us, length us, event | category | flops | bytes accessed | tf_op | source)
XLA Modules:
  0.0 229.7 jit_solution(6101081966629840055)
XLA Ops:
  0.8 0.7 copy-done.3
  2.1 39.0 %all_to_all.35.column = bf16[32,4,128]{2,1,0:T(4,128)(2,1)S(1)} all-to-all(bf16[32,4,128]{2,1,0:T(4,128)(2,1)S(1)} %modes.1), channel_id=1, replica_groups={{512,544,576,608,640,672,704,736,768,800,832,864,896,928,960,992,0,32,6..., dimensions={0} | all-to-all | bytes 65536 | tf_op jit(solution)/shard_map/all_to_all | solution.py:263
  41.0 1.5 widen.2
  42.6 8.8 %all-to-all-start.1 = ((bf16[32,32,384]{2,1,0:T(8,128)(2,1)}), bf16[32,32,384]{2,1,0:T(8,128)(2,1)S(1)}, u32[]{:S(2)}, u32[]{:S(2)}) async-start(bf16[32,32,384]{2,1,0:T(8,128)(2,1)} %widen.2), calls=%async_computation.1 | async-start | bytes 1572864 | tf_op jit(solution)/shard_map/all_to_all | solution.py:273
  51.4 3.2 %prepare_rows.1 = (f32[8,6272]{1,0:T(8,128)S(1)}, f32[8,6272]{1,0:T(8,128)S(1)}, f32[8,6272]{1,0:T(8,128)S(1)}, f32[8,6272]{1,0:T(8,128)S(1)}, f32[8,6272]{1,0:T(8,128)S(1)}, /*index=5*/f32[8,6272]{1,0:T(8,128)S(1)}) custom-call(s32[6]{0:T(128)S(1)} %stack.27.flags, f32[6,6144]{1,0:T(8,128)S(1)} %copy-done, f32[6,3,2,128]{3,2,1,0:T(2,128)S(1)} %bitcast.25), custom_call_target="tpu_custom_call" | custom-call | tf_op jit(solution)/shard_map/prepare_rows/pallas_call | solution.py:233
  54.7 3.1 %collective-permute-start = (f32[8,6272]{1,0:T(8,128)S(1)}, f32[8,6272]{1,0:T(8,128)S(1)}, u32[]{:S(2)}, u32[]{:S(2)}) collective-permute-start(f32[8,6272]{1,0:T(8,128)S(1)} %get-tuple-element.31.own), channel_id=1, source_target_pairs={{0,32},{32,0},{64,96},{96,64},{128,160},{160,128},{192,224},{224,1... | collective-permute-start | bytes 602120 | tf_op jit(solution)/shard_map/ppermute | solution.py:30
  57.8 0.7 collective-permute-start.1
  58.4 2.4 %collective-permute-start.2 = (f32[8,6272]{1,0:T(8,128)S(1)}, f32[8,6272]{1,0:T(8,128)S(1)}, u32[]{:S(2)}, u32[]{:S(2)}) collective-permute-start(f32[8,6272]{1,0:T(8,128)S(1)} %get-tuple-element.33), channel_id=1, source_target_pairs={{0,4},{4,0},{8,12},{12,8},{16,20},{20,16},{24,28},{28,24},{1,5},{5... | collective-permute-start | bytes 602120 | tf_op jit(solution)/shard_map/ppermute | solution.py:30
  60.9 3.3 %collective-permute-start.3 = (f32[8,6272]{1,0:T(8,128)S(1)}, f32[8,6272]{1,0:T(8,128)S(1)}, u32[]{:S(2)}, u32[]{:S(2)}) collective-permute-start(f32[8,6272]{1,0:T(8,128)S(1)} %get-tuple-element.34), channel_id=1, source_target_pairs={{4,8},{8,4},{12,16},{16,12},{20,24},{24,20},{5,9},{9,5},{13,17},{1... | collective-permute-start | bytes 602120 | tf_op jit(solution)/shard_map/ppermute | solution.py:31
  64.2 3.1 %collective-permute-start.4 = (f32[8,6272]{1,0:T(8,128)S(1)}, f32[8,6272]{1,0:T(8,128)S(1)}, u32[]{:S(2)}, u32[]{:S(2)}) collective-permute-start(f32[8,6272]{1,0:T(8,128)S(1)} %get-tuple-element.35), channel_id=1, source_target_pairs={{0,1},{1,0},{2,3},{3,2},{4,5},{5,4},{6,7},{7,6},{8,9},{9,8},{10,11... | collective-permute-start | bytes 602120 | tf_op jit(solution)/shard_map/ppermute | solution.py:30
  68.2 2.5 %collective-permute-done.4.refs_4_ = f32[8,6272]{1,0:T(8,128)S(1)} collective-permute-done((f32[8,6272]{1,0:T(8,128)S(1)}, f32[8,6272]{1,0:T(8,128)S(1)}, u32[]{:S(2)}, u32[]{:S(2)}) %collective-permute-start.4) | collective-permute-done | bytes 200736 | tf_op jit(solution)/shard_map/ppermute | solution.py:30
  71.4 1.6 build_rows.1
  73.0 5.0 %start_fields.1 = (f32[64,768]{1,0:T(8,128)S(1)}, f32[64,768]{1,0:T(8,128)S(1)}, f32[64,128]{1,0:T(8,128)S(1)}, f32[64,128]{1,0:T(8,128)S(1)}, f32[64,128]{1,0:T...) custom-call(s32[6]{0:T(128)S(1)} %stack.27.flags, ...), custom_call_target="tpu_custom_call" | custom-call | tf_op jit(solution)/shard_map/start_fields/pallas_call | solution.py:233
  78.0 5.9 %collective-permute-start.10 = (f32[64,128]{1,0:T(8,128)S(1)}, f32[64,128]{1,0:T(8,128)S(1)}, u32[]{:S(2)}, u32[]{:S(2)}) collective-permute-start(f32[64,128]{1,0:T(8,128)S(1)} %get-tuple-element.44), channel_id=1, source_target_pairs={{0,1},{1,0},{2,3},{3,2},{4,5},{5,4},{6,7},{7,6},{8,9},{9,8},{10,11... | collective-permute-start | bytes 98312 | tf_op jit(solution)/shard_map/ppermute | solution.py:30
  84.6 5.8 %collective-permute-start.6 = (f32[64,128]{1,0:T(8,128)S(1)}, f32[64,128]{1,0:T(8,128)S(1)}, u32[]{:S(2)}, u32[]{:S(2)}) collective-permute-start(f32[64,128]{1,0:T(8,128)S(1)} %get-tuple-element.40), channel_id=1, source_target_pairs={{0,32},{32,0},{64,96},{96,64},{128,160},{160,128},{192,224},{224,1... | collective-permute-start | bytes 98312 | tf_op jit(solution)/shard_map/ppermute | solution.py:30
  91.0 1.9 collective-permute-start.8
  93.0 6.1 %collective-permute-start.9 = (f32[64,128]{1,0:T(8,128)S(1)}, f32[64,128]{1,0:T(8,128)S(1)}, u32[]{:S(2)}, u32[]{:S(2)}) collective-permute-start(f32[64,128]{1,0:T(8,128)S(1)} %get-tuple-element.43), channel_id=1, source_target_pairs={{4,8},{8,4},{12,16},{16,12},{20,24},{24,20},{5,9},{9,5},{13,17},{1... | collective-permute-start | bytes 98312 | tf_op jit(solution)/shard_map/ppermute | solution.py:31
  99.1 1.5 collective-permute-done.9.refs_3_
  100.7 1.0 residual.1
  101.7 43.7 %all_to_all.36.column = bf16[32,4,128]{2,1,0:T(4,128)(2,1)S(1)} all-to-all(bf16[32,4,128]{2,1,0:T(4,128)(2,1)S(1)} %get-tuple-element.46), channel_id=1, replica_groups=mesh['gx'=32,'gy'=8,'gz'=4] {'gx'}, dimensions={0} | all-to-all | bytes 65536 | tf_op jit(solution)/shard_map/all_to_all | solution.py:263
  146.0 23.2 %all_to_all.37 = bf16[32,32,384]{2,1,0:T(8,128)(2,1)S(1)} all-to-all(bf16[32,32,384]{2,1,0:T(8,128)(2,1)S(1)} %widen.3), channel_id=1, replica_groups=mesh['gx'=32,'gy'=8,'gz'=4] {'gy','gz'}, dimensions={0} | all-to-all | bytes 1572864 | tf_op jit(solution)/shard_map/all_to_all | solution.py:273
  169.2 4.3 %project.1 = (f32[64,768]{1,0:T(8,128)S(1)}, f32[64,768]{1,0:T(8,128)S(1)}, f32[64,128]{1,0:T(8,128)S(1)}, f32[64,128]{1,0:T(8,128)S(1)}, f32[64,128]{1,0:T(8,12...) custom-call(s32[6]{0:T(128)S(1)} %stack.27.flags, ...), custom_call_target="tpu_custom_call" | custom-call | tf_op jit(solution)/shard_map/project/pallas_call | solution.py:233
  173.5 11.7 %all_to_all.38 = f32[32,2,128]{2,1,0:T(2,128)S(1)} all-to-all(f32[32,2,128]{2,1,0:T(2,128)S(1)} %bitcast.27), channel_id=1, replica_groups=mesh['gx'=32,'gy'=8,'gz'=4] {'gy','gz'}, dimensions={0} | all-to-all | bytes 65536 | tf_op jit(solution)/shard_map/all_to_all | solution.py:335
  185.9 4.0 %all-to-all-start.5 = ((f32[32,2,128]{2,1,0:T(2,128)}), f32[32,2,128]{2,1,0:T(2,128)S(1)}, u32[]{:S(2)}, u32[]{:S(2)}) async-start(f32[32,2,128]{2,1,0:T(2,128)} %broadcast_in_dim.4), calls=%async_computation.5 | async-start | bytes 65536 | tf_op jit(solution)/shard_map/all_to_all | solution.py:19
  189.9 3.0 %collective-permute-start.12 = (f32[64,128]{1,0:T(8,128)S(1)}, f32[64,128]{1,0:T(8,128)S(1)}, u32[]{:S(2)}, u32[]{:S(2)}) collective-permute-start(f32[64,128]{1,0:T(8,128)S(1)} %get-tuple-element.52), channel_id=1, source_target_pairs={{0,32},{32,0},{64,96},{96,64},{128,160},{160,128},{192,224},{224,1... | collective-permute-start | bytes 98312 | tf_op jit(solution)/shard_map/ppermute | solution.py:30
  193.6 2.9 %collective-permute-start.14 = (f32[64,128]{1,0:T(8,128)S(1)}, f32[64,128]{1,0:T(8,128)S(1)}, u32[]{:S(2)}, u32[]{:S(2)}) collective-permute-start(f32[64,128]{1,0:T(8,128)S(1)} %get-tuple-element.54), channel_id=1, source_target_pairs={{0,4},{4,0},{8,12},{12,8},{16,20},{20,16},{24,28},{28,24},{1,5},{5... | collective-permute-start | bytes 98312 | tf_op jit(solution)/shard_map/ppermute | solution.py:30
  196.5 2.1 collective-permute-start.15
  198.7 2.2 collective-permute-start.16
  201.5 10.5 %all-to-all-done.5 = f32[32,2,128]{2,1,0:T(2,128)S(1)} async-done(((f32[32,2,128]{2,1,0:T(2,128)}), f32[32,2,128]{2,1,0:T(2,128)S(1)}, u32[]{:S(2)}, u32[]{:S(2)}) %all-to-all-start.5) | async-done | bytes 32800 | tf_op jit(solution)/shard_map/all_to_all | solution.py:19
  212.7 5.6 %all-to-all-start.6 = ((f32[32,2,128]{2,1,0:T(2,128)}), f32[32,2,128]{2,1,0:T(2,128)S(1)}, u32[]{:S(2)}, u32[]{:S(2)}) async-start(f32[32,2,128]{2,1,0:T(2,128)} %broadcast_in_dim.5), calls=%async_computation.6 | async-start | bytes 65536 | tf_op jit(solution)/shard_map/all_to_all | solution.py:19
  218.3 7.3 %all-to-all-done.6 = f32[32,2,128]{2,1,0:T(2,128)S(1)} async-done(((f32[32,2,128]{2,1,0:T(2,128)}), f32[32,2,128]{2,1,0:T(2,128)S(1)}, u32[]{:S(2)}, u32[]{:S(2)}) %all-to-all-start.6) | async-done | bytes 32800 | tf_op jit(solution)/shard_map/all_to_all | solution.py:19
  225.6 4.1 %final_update.1 = (f32[6,64,128]{2,1,0:T(8,128)}, f32[6,64,128]{2,1,0:T(8,128)}) custom-call(s32[6]{0:T(128)S(1)} %stack.27.flags, f32[64,128]{1,0:T(8,128)S(1)} %bitcast.24, f32[64,768]{1,0:T(8,128)S(1)} %get-tuple-element.49.multipliers, f32[64,768]{1,0:T(8,128)S(1)} %get-tuple-element.47.residual, f32[64,768]{1,0:T(8,128)S(1)} %get-tuple-element.50.field, ...), custom_call_target="tpu_custom_call" | custom-call | tf_op jit(solution)/shard_map/final_update/pallas_call | solution.py:233
  (45 shorter events, 7.0 us)
Async XLA Ops:
  0.6 50.8 %copy-start.2 = (f32[1,1,1,6,3,2,128]{6,5,4,3,2,1,0:T(2,128)S(1)}, f32[1,1,1,6,3,2,128]{6,5,4,3,2,1,0:T(2,128)}, u32[]{:S(2)}) copy-start(f32[1,1,1,6,3,2,128]{6,5,4,3,2,1,0:T(2,128)} %param.6) | copy-start | bytes 55300
  0.6 50.8 %copy-start = (f32[6,6144]{1,0:T(8,128)S(1)}, f32[6,6144]{1,0:T(8,128)}, u32[]{:S(2)}) copy-start(f32[6,6144]{1,0:T(8,128)} %rows.1) | copy-start | bytes 442372
  0.8 0.7 copy-start.3
  42.6 30.4 %all-to-all-start.1 = ((bf16[32,32,384]{2,1,0:T(8,128)(2,1)}), bf16[32,32,384]{2,1,0:T(8,128)(2,1)S(1)}, u32[]{:S(2)}, u32[]{:S(2)}) async-start(bf16[32,32,384]{2,1,0:T(8,128)(2,1)} %widen.2), calls=%async_computation.1 | async-start | bytes 1572864 | tf_op jit(solution)/shard_map/all_to_all | solution.py:273
  54.7 12.7 %collective-permute-start = (f32[8,6272]{1,0:T(8,128)S(1)}, f32[8,6272]{1,0:T(8,128)S(1)}, u32[]{:S(2)}, u32[]{:S(2)}) collective-permute-start(f32[8,6272]{1,0:T(8,128)S(1)} %get-tuple-element.31.own), channel_id=1, source_target_pairs={{0,32},{32,0},{64,96},{96,64},{128,160},{160,128},{192,224},{224,1... | collective-permute-start | bytes 602120 | tf_op jit(solution)/shard_map/ppermute | solution.py:30
  57.8 10.2 %collective-permute-start.1 = (f32[8,6272]{1,0:T(8,128)S(1)}, f32[8,6272]{1,0:T(8,128)S(1)}, u32[]{:S(2)}, u32[]{:S(2)}) collective-permute-start(f32[8,6272]{1,0:T(8,128)S(1)} %get-tuple-element.32), channel_id=1, source_target_pairs={{32,64},{64,32},{96,128},{128,96},{160,192},{192,160},{224,256},{2... | collective-permute-start | bytes 602120 | tf_op jit(solution)/shard_map/ppermute | solution.py:31
  58.4 9.6 %collective-permute-start.2 = (f32[8,6272]{1,0:T(8,128)S(1)}, f32[8,6272]{1,0:T(8,128)S(1)}, u32[]{:S(2)}, u32[]{:S(2)}) collective-permute-start(f32[8,6272]{1,0:T(8,128)S(1)} %get-tuple-element.33), channel_id=1, source_target_pairs={{0,4},{4,0},{8,12},{12,8},{16,20},{20,16},{24,28},{28,24},{1,5},{5... | collective-permute-start | bytes 602120 | tf_op jit(solution)/shard_map/ppermute | solution.py:30
  60.9 7.3 %collective-permute-start.3 = (f32[8,6272]{1,0:T(8,128)S(1)}, f32[8,6272]{1,0:T(8,128)S(1)}, u32[]{:S(2)}, u32[]{:S(2)}) collective-permute-start(f32[8,6272]{1,0:T(8,128)S(1)} %get-tuple-element.34), channel_id=1, source_target_pairs={{4,8},{8,4},{12,16},{16,12},{20,24},{24,20},{5,9},{9,5},{13,17},{1... | collective-permute-start | bytes 602120 | tf_op jit(solution)/shard_map/ppermute | solution.py:31
  64.2 6.5 %collective-permute-start.4 = (f32[8,6272]{1,0:T(8,128)S(1)}, f32[8,6272]{1,0:T(8,128)S(1)}, u32[]{:S(2)}, u32[]{:S(2)}) collective-permute-start(f32[8,6272]{1,0:T(8,128)S(1)} %get-tuple-element.35), channel_id=1, source_target_pairs={{0,1},{1,0},{2,3},{3,2},{4,5},{5,4},{6,7},{7,6},{8,9},{9,8},{10,11... | collective-permute-start | bytes 602120 | tf_op jit(solution)/shard_map/ppermute | solution.py:30
  67.3 3.4 %collective-permute-start.5 = (f32[8,6272]{1,0:T(8,128)S(1)}, f32[8,6272]{1,0:T(8,128)S(1)}, u32[]{:S(2)}, u32[]{:S(2)}) collective-permute-start(f32[8,6272]{1,0:T(8,128)S(1)} %get-tuple-element.36), channel_id=1, source_target_pairs={{1,2},{2,1},{5,6},{6,5},{9,10},{10,9},{13,14},{14,13},{17,18},{18,... | collective-permute-start | bytes 602120 | tf_op jit(solution)/shard_map/ppermute | solution.py:31
  68.0 2.6 %copy-start.4 = (f32[8,6272]{1,0:T(8,128)}, f32[8,6272]{1,0:T(8,128)S(1)}, u32[]{:S(2)}) copy-start(f32[8,6272]{1,0:T(8,128)S(1)} %collective-permute-done.2.refs_2_) | copy-start | bytes 602116
  68.2 2.5 %copy-start.5 = (f32[8,6272]{1,0:T(8,128)}, f32[8,6272]{1,0:T(8,128)S(1)}, u32[]{:S(2)}) copy-start(f32[8,6272]{1,0:T(8,128)S(1)} %collective-permute-done.3.refs_3_) | copy-start | bytes 602116
  70.7 0.7 copy-start.6
  70.7 0.7 copy-start.7
  73.0 27.6 %copy-start.1 = (f32[1,1,1,3,2,64,128]{6,5,4,3,2,1,0:T(8,128)S(1)}, f32[1,1,1,3,2,64,128]{6,5,4,3,2,1,0:T(8,128)}, u32[]{:S(2)}) copy-start(f32[1,1,1,3,2,64,128]{6,5,4,3,2,1,0:T(8,128)} %param.9) | copy-start | bytes 589828
  78.0 14.9 %collective-permute-start.10 = (f32[64,128]{1,0:T(8,128)S(1)}, f32[64,128]{1,0:T(8,128)S(1)}, u32[]{:S(2)}, u32[]{:S(2)}) collective-permute-start(f32[64,128]{1,0:T(8,128)S(1)} %get-tuple-element.44), channel_id=1, source_target_pairs={{0,1},{1,0},{2,3},{3,2},{4,5},{5,4},{6,7},{7,6},{8,9},{9,8},{10,11... | collective-permute-start | bytes 98312 | tf_op jit(solution)/shard_map/ppermute | solution.py:30
  83.9 15.1 %collective-permute-start.11 = (f32[64,128]{1,0:T(8,128)S(1)}, f32[64,128]{1,0:T(8,128)S(1)}, u32[]{:S(2)}, u32[]{:S(2)}) collective-permute-start(f32[64,128]{1,0:T(8,128)S(1)} %get-tuple-element.45), channel_id=1, source_target_pairs={{1,2},{2,1},{5,6},{6,5},{9,10},{10,9},{13,14},{14,13},{17,18},{18,... | collective-permute-start | bytes 98312 | tf_op jit(solution)/shard_map/ppermute | solution.py:31
  84.6 14.5 %collective-permute-start.6 = (f32[64,128]{1,0:T(8,128)S(1)}, f32[64,128]{1,0:T(8,128)S(1)}, u32[]{:S(2)}, u32[]{:S(2)}) collective-permute-start(f32[64,128]{1,0:T(8,128)S(1)} %get-tuple-element.40), channel_id=1, source_target_pairs={{0,32},{32,0},{64,96},{96,64},{128,160},{160,128},{192,224},{224,1... | collective-permute-start | bytes 98312 | tf_op jit(solution)/shard_map/ppermute | solution.py:30
  90.4 8.7 %collective-permute-start.7 = (f32[64,128]{1,0:T(8,128)S(1)}, f32[64,128]{1,0:T(8,128)S(1)}, u32[]{:S(2)}, u32[]{:S(2)}) collective-permute-start(f32[64,128]{1,0:T(8,128)S(1)} %get-tuple-element.41), channel_id=1, source_target_pairs={{32,64},{64,32},{96,128},{128,96},{160,192},{192,160},{224,256},{2... | collective-permute-start | bytes 98312 | tf_op jit(solution)/shard_map/ppermute | solution.py:31
  91.0 8.1 %collective-permute-start.8 = (f32[64,128]{1,0:T(8,128)S(1)}, f32[64,128]{1,0:T(8,128)S(1)}, u32[]{:S(2)}, u32[]{:S(2)}) collective-permute-start(f32[64,128]{1,0:T(8,128)S(1)} %get-tuple-element.42), channel_id=1, source_target_pairs={{0,4},{4,0},{8,12},{12,8},{16,20},{20,16},{24,28},{28,24},{1,5},{5... | collective-permute-start | bytes 98312 | tf_op jit(solution)/shard_map/ppermute | solution.py:30
  93.0 7.7 %collective-permute-start.9 = (f32[64,128]{1,0:T(8,128)S(1)}, f32[64,128]{1,0:T(8,128)S(1)}, u32[]{:S(2)}, u32[]{:S(2)}) collective-permute-start(f32[64,128]{1,0:T(8,128)S(1)} %get-tuple-element.43), channel_id=1, source_target_pairs={{4,8},{8,4},{12,16},{16,12},{20,24},{24,20},{5,9},{9,5},{13,17},{1... | collective-permute-start | bytes 98312 | tf_op jit(solution)/shard_map/ppermute | solution.py:31
  185.9 26.1 %all-to-all-start.5 = ((f32[32,2,128]{2,1,0:T(2,128)}), f32[32,2,128]{2,1,0:T(2,128)S(1)}, u32[]{:S(2)}, u32[]{:S(2)}) async-start(f32[32,2,128]{2,1,0:T(2,128)} %broadcast_in_dim.4), calls=%async_computation.5 | async-start | bytes 65536 | tf_op jit(solution)/shard_map/all_to_all | solution.py:19
  189.9 10.9 %collective-permute-start.12 = (f32[64,128]{1,0:T(8,128)S(1)}, f32[64,128]{1,0:T(8,128)S(1)}, u32[]{:S(2)}, u32[]{:S(2)}) collective-permute-start(f32[64,128]{1,0:T(8,128)S(1)} %get-tuple-element.52), channel_id=1, source_target_pairs={{0,32},{32,0},{64,96},{96,64},{128,160},{160,128},{192,224},{224,1... | collective-permute-start | bytes 98312 | tf_op jit(solution)/shard_map/ppermute | solution.py:30
  193.0 25.3 %collective-permute-start.13 = (f32[64,128]{1,0:T(8,128)S(1)}, f32[64,128]{1,0:T(8,128)S(1)}, u32[]{:S(2)}, u32[]{:S(2)}) collective-permute-start(f32[64,128]{1,0:T(8,128)S(1)} %get-tuple-element.53), channel_id=1, source_target_pairs={{32,64},{64,32},{96,128},{128,96},{160,192},{192,160},{224,256},{2... | collective-permute-start | bytes 98312 | tf_op jit(solution)/shard_map/ppermute | solution.py:31
  193.6 24.6 %collective-permute-start.14 = (f32[64,128]{1,0:T(8,128)S(1)}, f32[64,128]{1,0:T(8,128)S(1)}, u32[]{:S(2)}, u32[]{:S(2)}) collective-permute-start(f32[64,128]{1,0:T(8,128)S(1)} %get-tuple-element.54), channel_id=1, source_target_pairs={{0,4},{4,0},{8,12},{12,8},{16,20},{20,16},{24,28},{28,24},{1,5},{5... | collective-permute-start | bytes 98312 | tf_op jit(solution)/shard_map/ppermute | solution.py:30
  196.5 21.8 %collective-permute-start.15 = (f32[64,128]{1,0:T(8,128)S(1)}, f32[64,128]{1,0:T(8,128)S(1)}, u32[]{:S(2)}, u32[]{:S(2)}) collective-permute-start(f32[64,128]{1,0:T(8,128)S(1)} %get-tuple-element.55), channel_id=1, source_target_pairs={{4,8},{8,4},{12,16},{16,12},{20,24},{24,20},{5,9},{9,5},{13,17},{1... | collective-permute-start | bytes 98312 | tf_op jit(solution)/shard_map/ppermute | solution.py:31
  198.7 19.6 %collective-permute-start.16 = (f32[64,128]{1,0:T(8,128)S(1)}, f32[64,128]{1,0:T(8,128)S(1)}, u32[]{:S(2)}, u32[]{:S(2)}) collective-permute-start(f32[64,128]{1,0:T(8,128)S(1)} %get-tuple-element.56), channel_id=1, source_target_pairs={{0,1},{1,0},{2,3},{3,2},{4,5},{5,4},{6,7},{7,6},{8,9},{9,8},{10,11... | collective-permute-start | bytes 98312 | tf_op jit(solution)/shard_map/ppermute | solution.py:30
  200.9 17.4 %collective-permute-start.17 = (f32[64,128]{1,0:T(8,128)S(1)}, f32[64,128]{1,0:T(8,128)S(1)}, u32[]{:S(2)}, u32[]{:S(2)}) collective-permute-start(f32[64,128]{1,0:T(8,128)S(1)} %get-tuple-element.57), channel_id=1, source_target_pairs={{1,2},{2,1},{5,6},{6,5},{9,10},{10,9},{13,14},{14,13},{17,18},{18,... | collective-permute-start | bytes 98312 | tf_op jit(solution)/shard_map/ppermute | solution.py:31
  212.7 12.9 %all-to-all-start.6 = ((f32[32,2,128]{2,1,0:T(2,128)}), f32[32,2,128]{2,1,0:T(2,128)S(1)}, u32[]{:S(2)}, u32[]{:S(2)}) async-start(f32[32,2,128]{2,1,0:T(2,128)} %broadcast_in_dim.5), calls=%async_computation.6 | async-start | bytes 65536 | tf_op jit(solution)/shard_map/all_to_all | solution.py:19
